TPU v7x, 32 devices: a whole 2x2x4 slice. The times are simulated.
32 devices in a mesh: gx: 2 (over y), gy: 4 (over z), gz: 4 (over x, core).
Axes of the slice: x: 2, y: 2, z: 4, core: 2. Of those that a mesh axis runs over, the one named last changes fastest.
Arguments:
- vel_u: bfloat16 [96, 8, 16, 512], P(None, 'gx', 'gy', 'gz'), may hold values from -300 to 300
- vel_v: bfloat16 [96, 8, 16, 512], P(None, 'gx', 'gy', 'gz'), may hold values from -300 to 300
- vel_w: bfloat16 [96, 8, 16, 512], P(None, 'gx', 'gy', 'gz'), may hold values from -300 to 300
- density: bfloat16 [96, 8, 16, 512], P(None, 'gx', 'gy', 'gz'), may hold values from -300 to 300
Outputs:
- basis: float32 [96, 2, 8, 16, 512], P(None, None, 'gx', 'gy', 'gz')
- factor: float32 [96, 96], replicated
All inputs are finite; a program needn't handle non-finite values.
Results may differ from a plain program's by a relative error of at most 0.0015.
Values may be sent and summed in bfloat16 or wider, within the bound.
No kernel may reach another device: no remote copies, remote signals or barrier semaphores. Data moves between devices by JAX's collectives and lax.ppermute only.
A program may use at most 128 MiB of HBM per device.

v0:
```python
import jax
import jax.numpy as jnp
from jax import lax
from jax.sharding import PartitionSpec as P


def with_halo(cells, sides, width):
    for axis, dim in sides:
        count = lax.axis_size(axis)
        head = lax.slice_in_dim(cells, 0, width, axis=dim)
        tail = lax.slice_in_dim(cells, cells.shape[dim] - width, cells.shape[dim], axis=dim)
        cells = jnp.concatenate(
            [
                lax.ppermute(tail, axis, [(i, (i + 1) % count) for i in range(count)]),
                cells,
                lax.ppermute(head, axis, [((i + 1) % count, i) for i in range(count)]),
            ],
            axis=dim,
        )
    return cells


def merged(shard, axis, combine):
    everything = lax.all_gather(shard.astype(jnp.bfloat16), axis)

    def take(k):
        return everything[k].astype(shard.dtype)

    return lax.fori_loop(
        1, lax.axis_size(axis), lambda k, so_far: combine(so_far, take(k)), take(0)
    )


def edge_copy(padded, dim, position, count):
    length = padded.shape[dim]
    outer_first = lax.slice_in_dim(padded, 0, 1, axis=dim)
    inner_first = lax.slice_in_dim(padded, 1, 2, axis=dim)
    inner_final = lax.slice_in_dim(padded, length - 2, length - 1, axis=dim)
    outer_final = lax.slice_in_dim(padded, length - 1, length, axis=dim)
    middle = lax.slice_in_dim(padded, 1, length - 1, axis=dim)
    first_face = jnp.where(position == 0, inner_first, outer_first)
    final_face = jnp.where(position == count - 1, inner_final, outer_final)
    return jnp.concatenate([first_face, middle, final_face], axis=dim)


def central(paired, dim):
    length = paired.shape[dim]
    return lax.slice_in_dim(paired, 2, length, axis=dim) - lax.slice_in_dim(
        paired, 0, length - 2, axis=dim
    )


def combine(left_part, right_part):
    total = jnp.dot(
        left_part, left_part.T, precision=lax.Precision.HIGHEST, preferred_element_type=jnp.float32
    )
    total = total + jnp.dot(
        right_part,
        right_part.T,
        precision=lax.Precision.HIGHEST,
        preferred_element_type=jnp.float32,
    )
    return jnp.linalg.cholesky(total)


def per_device(vel_u, vel_v, vel_w, density):
    stacked = jnp.stack([vel_u, vel_v, vel_w, density])
    where_x = lax.axis_index("gx")
    where_y = lax.axis_index("gy")
    count_x = lax.axis_size("gx")
    count_y = lax.axis_size("gy")
    count_z = lax.axis_size("gz")
    padded = with_halo(stacked, (("gx", 2), ("gy", 3), ("gz", 4)), 1)
    padded = edge_copy(edge_copy(padded, 2, where_x, count_x), 3, where_y, count_y).astype(
        jnp.float32
    )
    stream_pair = padded[:, :, :, 1:-1, 1:-1][0::3]
    normal_pair = padded[:, :, 1:-1, :, 1:-1][1::2]
    span_pair = padded[:, :, 1:-1, 1:-1, :][2:4]
    diff_x = central(stream_pair, 2)
    diff_y = central(normal_pair, 3)
    diff_z = central(span_pair, 4)
    dilatation = 0.5 * (diff_x[0] + diff_y[0] + diff_z[0])
    gradient = jnp.sqrt(
        0.25 * (diff_x[1] * diff_x[1] + diff_y[1] * diff_y[1] + diff_z[1] * diff_z[1]) + 0.25
    )
    derived = jnp.stack([dilatation, gradient], axis=1)
    snap_count = derived.shape[0]
    panel = derived.reshape(snap_count, -1)
    row_total = panel.shape[1] * count_x * count_y * count_z
    moments = (
        jnp.dot(panel, panel.T, precision=lax.Precision.HIGHEST, preferred_element_type=jnp.float32)
        / row_total
    )
    lower = merged(jnp.linalg.cholesky(moments), ("gx", "gy", "gz"), combine)
    basis = jax.scipy.linalg.solve_triangular(lower, panel, lower=True).reshape(derived.shape)
    return (basis, lower.T)


def solution(mesh):
    in_specs = (
        P(None, "gx", "gy", "gz"),
        P(None, "gx", "gy", "gz"),
        P(None, "gx", "gy", "gz"),
        P(None, "gx", "gy", "gz"),
    )
    out_specs = (P(None, None, "gx", "gy", "gz"), P())
    return jax.shard_map(
        per_device, mesh=mesh, in_specs=in_specs, out_specs=out_specs, check_vma=False
    )
```

profile of v0, /device:TPU:0, one launch (start us, length us, event | category | flops | bytes accessed | tf_op | source)
XLA Modules:
  0.0 505.0 jit_solution(17747129925313699697)
XLA Ops:
  5.5 9.9 %collective-permute-done.1 = bf16[4,96,1,4,128]{4,1,3,2,0:T(8,128)(2,1)S(1)} collective-permute-done((bf16[4,96,1,4,128]{4,1,3,2,0:T(8,128)(2,1)S(1)}, bf16[4,96,1,4,128]{4,1,3,2,0:T(8,128)(2,1)S(1)}, u32[]{:S(2)}, u32[]{:S(2)}) %collective-permute-start.1) | collective-permute-done | bytes 393248 | tf_op jit(solution)/shard_map/ppermute | solution.py:16
  27.1 13.8 %collective-permute-done.3 = bf16[4,96,6,1,128]{4,1,3,2,0:T(8,128)(2,1)S(1)} collective-permute-done((bf16[4,96,6,1,128]{4,1,3,2,0:T(8,128)(2,1)S(1)}, bf16[4,96,6,1,128]{4,1,3,2,0:T(8,128)(2,1)S(1)}, u32[]{:S(2)}, u32[]{:S(2)}) %collective-permute-start.3) | collective-permute-done | bytes 589856 | tf_op jit(solution)/shard_map/ppermute | solution.py:16
  40.9 11.5 %collective-permute-done.2 = bf16[4,96,6,1,128]{4,1,3,2,0:T(8,128)(2,1)S(1)} collective-permute-done((bf16[4,96,6,1,128]{4,1,3,2,0:T(8,128)(2,1)S(1)}, bf16[4,96,6,1,128]{4,1,3,2,0:T(8,128)(2,1)S(1)}, u32[]{:S(2)}, u32[]{:S(2)}) %collective-permute-start.2) | collective-permute-done | bytes 589856 | tf_op jit(solution)/shard_map/ppermute | solution.py:14
  71.1 12.0 %pad_maximum_fusion = bf16[4,96,6,6,130]{4,1,3,2,0:T(8,128)(2,1)S(1)} fusion(bf16[4,96,6,6,1]{4,1,3,2,0:T(8,128)(2,1)S(1)} %copy.42, bf16[4,96,6,1,128]{4,1,3,2,0:T(8,128)(2,1)} %copy-done.6, bf16[4,96,1,4,128]{4,1,3,2,0:T(8,128)(2,1)} %copy-done.4, bf16[1,96,4,4,128]{4,1,3,2,0:T(8,128)(2,1)} %copy-done, bf16[1,96,4,4,128]{4,1,3,2,0:T(8,128)(2,1)} %copy-done.1, ...), kind=kLoop, calls=%fused_computation.11 | loop fusion | flops 35942400 | bytes 7188480 | tf_op jit(solution)/shard_map/concatenate | solution.py:12
  105.3 8.8 %cholesky.55 = f32[96,96]{1,0:T(8,128)S(1)} custom-call(f32[96,96]{1,0:T(8,128)S(1)} %fusion.16), custom_call_target="Cholesky" | custom-call | tf_op jit(solution)/shard_map/jit(cholesky)/cholesky | solution.py:95
  115.4 42.1 %all-gather = bf16[3072,96]{1,0:T(8,128)(2,1)S(1)} all-gather(bf16[96,96]{1,0:T(8,128)(2,1)S(1)} %select_convert_fusion), channel_id=2, replica_groups=mesh['gx'=2,'gy'=4,'gz'=4] {'gx','gy','gz'}, dimensions={0}, use_global_device_ids=true | all-gather | bytes 608256 | tf_op jit(solution)/shard_map/all_gather | solution.py:24
  157.5 329.7 %while.15 = (s32[]{:T(128)}, f32[96,96]{1,0:T(8,128)S(1)}, bf16[32,96,96]{2,1,0:T(8,128)(2,1)S(1)}, s32[]{:T(128)}, s32[]{:T(128)}, /*index=5*/s32[]{:T(128)}) while((s32[]{:T(128)}, f32[96,96]{1,0:T(8,128)S(1)}, bf16[32,96,96]{2,1,0:T(8,128)(2,1)S(1)}, s32[]{:T(128)}, s32[]{:T(128)}, /*index=5*/s32[]{:T(128)}) %tuple.55), condition=%wide.region_3.5_spmd, body=%wide.region_2.4_spmd.sunk | while | flops 12469348 | bytes 480117 | solution.py:29
  158.0 8.8 %cholesky.118 = f32[96,96]{1,0:T(8,128)S(1)} custom-call(f32[96,96]{1,0:T(8,128)S(1)} %fusion.30), custom_call_target="Cholesky" | custom-call | tf_op jit(solution)/shard_map/while/body/eval_jaxpr/jit(cholesky)/cholesky | solution.py:63
  168.7 8.8 %cholesky.118 = f32[96,96]{1,0:T(8,128)S(1)} custom-call(f32[96,96]{1,0:T(8,128)S(1)} %fusion.30), custom_call_target="Cholesky" | custom-call | tf_op jit(solution)/shard_map/while/body/eval_jaxpr/jit(cholesky)/cholesky | solution.py:63
  179.3 8.8 %cholesky.118 = f32[96,96]{1,0:T(8,128)S(1)} custom-call(f32[96,96]{1,0:T(8,128)S(1)} %fusion.30), custom_call_target="Cholesky" | custom-call | tf_op jit(solution)/shard_map/while/body/eval_jaxpr/jit(cholesky)/cholesky | solution.py:63
  189.9 8.8 %cholesky.118 = f32[96,96]{1,0:T(8,128)S(1)} custom-call(f32[96,96]{1,0:T(8,128)S(1)} %fusion.30), custom_call_target="Cholesky" | custom-call | tf_op jit(solution)/shard_map/while/body/eval_jaxpr/jit(cholesky)/cholesky | solution.py:63
  200.6 8.8 %cholesky.118 = f32[96,96]{1,0:T(8,128)S(1)} custom-call(f32[96,96]{1,0:T(8,128)S(1)} %fusion.30), custom_call_target="Cholesky" | custom-call | tf_op jit(solution)/shard_map/while/body/eval_jaxpr/jit(cholesky)/cholesky | solution.py:63
  211.2 8.8 %cholesky.118 = f32[96,96]{1,0:T(8,128)S(1)} custom-call(f32[96,96]{1,0:T(8,128)S(1)} %fusion.30), custom_call_target="Cholesky" | custom-call | tf_op jit(solution)/shard_map/while/body/eval_jaxpr/jit(cholesky)/cholesky | solution.py:63
  221.9 8.8 %cholesky.118 = f32[96,96]{1,0:T(8,128)S(1)} custom-call(f32[96,96]{1,0:T(8,128)S(1)} %fusion.30), custom_call_target="Cholesky" | custom-call | tf_op jit(solution)/shard_map/while/body/eval_jaxpr/jit(cholesky)/cholesky | solution.py:63
  232.5 8.8 %cholesky.118 = f32[96,96]{1,0:T(8,128)S(1)} custom-call(f32[96,96]{1,0:T(8,128)S(1)} %fusion.30), custom_call_target="Cholesky" | custom-call | tf_op jit(solution)/shard_map/while/body/eval_jaxpr/jit(cholesky)/cholesky | solution.py:63
  243.1 8.8 %cholesky.118 = f32[96,96]{1,0:T(8,128)S(1)} custom-call(f32[96,96]{1,0:T(8,128)S(1)} %fusion.30), custom_call_target="Cholesky" | custom-call | tf_op jit(solution)/shard_map/while/body/eval_jaxpr/jit(cholesky)/cholesky | solution.py:63
  253.8 8.8 %cholesky.118 = f32[96,96]{1,0:T(8,128)S(1)} custom-call(f32[96,96]{1,0:T(8,128)S(1)} %fusion.30), custom_call_target="Cholesky" | custom-call | tf_op jit(solution)/shard_map/while/body/eval_jaxpr/jit(cholesky)/cholesky | solution.py:63
  264.4 8.8 %cholesky.118 = f32[96,96]{1,0:T(8,128)S(1)} custom-call(f32[96,96]{1,0:T(8,128)S(1)} %fusion.30), custom_call_target="Cholesky" | custom-call | tf_op jit(solution)/shard_map/while/body/eval_jaxpr/jit(cholesky)/cholesky | solution.py:63
  275.0 8.8 %cholesky.118 = f32[96,96]{1,0:T(8,128)S(1)} custom-call(f32[96,96]{1,0:T(8,128)S(1)} %fusion.30), custom_call_target="Cholesky" | custom-call | tf_op jit(solution)/shard_map/while/body/eval_jaxpr/jit(cholesky)/cholesky | solution.py:63
  285.7 8.8 %cholesky.118 = f32[96,96]{1,0:T(8,128)S(1)} custom-call(f32[96,96]{1,0:T(8,128)S(1)} %fusion.30), custom_call_target="Cholesky" | custom-call | tf_op jit(solution)/shard_map/while/body/eval_jaxpr/jit(cholesky)/cholesky | solution.py:63
  296.3 8.8 %cholesky.118 = f32[96,96]{1,0:T(8,128)S(1)} custom-call(f32[96,96]{1,0:T(8,128)S(1)} %fusion.30), custom_call_target="Cholesky" | custom-call | tf_op jit(solution)/shard_map/while/body/eval_jaxpr/jit(cholesky)/cholesky | solution.py:63
  306.9 8.8 %cholesky.118 = f32[96,96]{1,0:T(8,128)S(1)} custom-call(f32[96,96]{1,0:T(8,128)S(1)} %fusion.30), custom_call_target="Cholesky" | custom-call | tf_op jit(solution)/shard_map/while/body/eval_jaxpr/jit(cholesky)/cholesky | solution.py:63
  360.1 8.8 %cholesky.118 = f32[96,96]{1,0:T(8,128)S(1)} custom-call(f32[96,96]{1,0:T(8,128)S(1)} %fusion.30), custom_call_target="Cholesky" | custom-call | tf_op jit(solution)/shard_map/while/body/eval_jaxpr/jit(cholesky)/cholesky | solution.py:63
  381.4 8.8 %cholesky.118 = f32[96,96]{1,0:T(8,128)S(1)} custom-call(f32[96,96]{1,0:T(8,128)S(1)} %fusion.30), custom_call_target="Cholesky" | custom-call | tf_op jit(solution)/shard_map/while/body/eval_jaxpr/jit(cholesky)/cholesky | solution.py:63
  (300 shorter events, 254.8 us)
Async XLA Ops:
  0.6 1.4 copy-start.8
  0.6 1.4 copy-start.9
  2.1 50.3 %copy-start = (bf16[1,96,4,4,128]{4,1,3,2,0:T(8,128)(2,1)}, bf16[1,96,4,4,128]{4,1,3,2,0:T(8,128)(2,1)S(1)}, u32[]{:S(2)}) copy-start(bf16[1,96,4,4,128]{4,1,3,2,0:T(8,128)(2,1)S(1)} %get-tuple-element.116) | copy-start | bytes 1179652
  2.1 50.3 %copy-start.1 = (bf16[1,96,4,4,128]{4,1,3,2,0:T(8,128)(2,1)}, bf16[1,96,4,4,128]{4,1,3,2,0:T(8,128)(2,1)S(1)}, u32[]{:S(2)}) copy-start(bf16[1,96,4,4,128]{4,1,3,2,0:T(8,128)(2,1)S(1)} %get-tuple-element.117) | copy-start | bytes 1179652
  2.3 50.0 %copy-start.2 = (bf16[1,96,4,4,128]{4,1,3,2,0:T(8,128)(2,1)}, bf16[1,96,4,4,128]{4,1,3,2,0:T(8,128)(2,1)S(1)}, u32[]{:S(2)}) copy-start(bf16[1,96,4,4,128]{4,1,3,2,0:T(8,128)(2,1)S(1)} %get-tuple-element.118) | copy-start | bytes 1179652
  2.3 50.0 %copy-start.3 = (bf16[1,96,4,4,128]{4,1,3,2,0:T(8,128)(2,1)}, bf16[1,96,4,4,128]{4,1,3,2,0:T(8,128)(2,1)S(1)}, u32[]{:S(2)}) copy-start(bf16[1,96,4,4,128]{4,1,3,2,0:T(8,128)(2,1)S(1)} %get-tuple-element.119) | copy-start | bytes 1179652
  2.4 13.0 %collective-permute-start.1 = (bf16[4,96,1,4,128]{4,1,3,2,0:T(8,128)(2,1)S(1)}, bf16[4,96,1,4,128]{4,1,3,2,0:T(8,128)(2,1)S(1)}, u32[]{:S(2)}, u32[]{:S(2)}) collective-permute-start(bf16[4,96,1,4,128]{4,1,3,2,0:T(8,128)(2,1)S(1)} %get-tuple-element.115), channel_id=1, source_target_pairs={{16,0},{0,16},{17,1},{1,17},{18,2},{2,18},{19,3},{3,19},{20,4},{4,... | collective-permute-start | bytes 1179656 | tf_op jit(solution)/shard_map/ppermute | solution.py:16
  5.5 17.5 %collective-permute-start = (bf16[4,96,1,4,128]{4,1,3,2,0:T(8,128)(2,1)S(1)}, bf16[4,96,1,4,128]{4,1,3,2,0:T(8,128)(2,1)S(1)}, u32[]{:S(2)}, u32[]{:S(2)}) collective-permute-start(bf16[4,96,1,4,128]{4,1,3,2,0:T(8,128)(2,1)S(1)} %get-tuple-element.114), channel_id=1, source_target_pairs={{0,16},{16,0},{1,17},{17,1},{2,18},{18,2},{3,19},{19,3},{4,20},{20... | collective-permute-start | bytes 1179656 | tf_op jit(solution)/shard_map/ppermute | solution.py:14
  15.4 37.0 %copy-start.4 = (bf16[4,96,1,4,128]{4,1,3,2,0:T(8,128)(2,1)}, bf16[4,96,1,4,128]{4,1,3,2,0:T(8,128)(2,1)S(1)}, u32[]{:S(2)}) copy-start(bf16[4,96,1,4,128]{4,1,3,2,0:T(8,128)(2,1)S(1)} %collective-permute-done.1) | copy-start | bytes 1179652
  23.0 29.4 %copy-start.5 = (bf16[4,96,1,4,128]{4,1,3,2,0:T(8,128)(2,1)}, bf16[4,96,1,4,128]{4,1,3,2,0:T(8,128)(2,1)S(1)}, u32[]{:S(2)}) copy-start(bf16[4,96,1,4,128]{4,1,3,2,0:T(8,128)(2,1)S(1)} %collective-permute-done) | copy-start | bytes 1179652
  23.2 17.7 %collective-permute-start.3 = (bf16[4,96,6,1,128]{4,1,3,2,0:T(8,128)(2,1)S(1)}, bf16[4,96,6,1,128]{4,1,3,2,0:T(8,128)(2,1)S(1)}, u32[]{:S(2)}, u32[]{:S(2)}) collective-permute-start(bf16[4,96,6,1,128]{4,1,3,2,0:T(8,128)(2,1)S(1)} %get-tuple-element.113), channel_id=1, source_target_pairs={{4,0},{8,4},{12,8},{0,12},{5,1},{9,5},{13,9},{1,13},{6,2},{10,6},{... | collective-permute-start | bytes 1769480 | tf_op jit(solution)/shard_map/ppermute | solution.py:16
  27.1 25.3 %collective-permute-start.2 = (bf16[4,96,6,1,128]{4,1,3,2,0:T(8,128)(2,1)S(1)}, bf16[4,96,6,1,128]{4,1,3,2,0:T(8,128)(2,1)S(1)}, u32[]{:S(2)}, u32[]{:S(2)}) collective-permute-start(bf16[4,96,6,1,128]{4,1,3,2,0:T(8,128)(2,1)S(1)} %get-tuple-element.112), channel_id=1, source_target_pairs={{0,4},{4,8},{8,12},{12,0},{1,5},{5,9},{9,13},{13,1},{2,6},{6,10},{... | collective-permute-start | bytes 1769480 | tf_op jit(solution)/shard_map/ppermute | solution.py:14
  40.9 11.5 %copy-start.6 = (bf16[4,96,6,1,128]{4,1,3,2,0:T(8,128)(2,1)}, bf16[4,96,6,1,128]{4,1,3,2,0:T(8,128)(2,1)S(1)}, u32[]{:S(2)}) copy-start(bf16[4,96,6,1,128]{4,1,3,2,0:T(8,128)(2,1)S(1)} %collective-permute-done.3) | copy-start | bytes 1769476
  52.4 0.8 copy-start.7
  61.4 2.8 collective-permute-start.5
  63.6 3.7 collective-permute-start.4
where the time goes:
time: 506 us; the launch traced here: 505 us
  other arithmetic  354 us (70%)
  waiting for transfers between devices  43.4 us (9%)
  blocking collectives  42.1 us (8%)
  local copies, waits for them, and re-layouts  40.7 us (8%)
  matrix products  14.7 us (3%)
  starting transfers between devices  7.5 us (1%)
    another operation x93, other arithmetic, combine(): return jnp.linalg.cholesky(total)  293 us
    all_gather x1, blocking collectives, merged(): everything = lax.all_gather(shard.astype(jnp.bfloat16), axis)  42.1 us
    ppermute x3, waiting for transfers between devices, with_halo(): lax.ppermute(head, axis, [((i + 1) % count, i) for i in range(count)])  23.6 us
    select_n x31, other arithmetic, combine(): return jnp.linalg.cholesky(total)  20.3 us
    ppermute x3, waiting for transfers between devices, with_halo(): lax.ppermute(tail, axis, [(i, (i + 1) % count) for i in range(count)])  19.7 us
    concatenate x2, other arithmetic, with_halo(): jnp.concatenate([lax.ppermute(tail, axis, [(i, (i + 1) % count) for i in...  12.7 us
  transfers between devices with their start and end apart: 6, of which 5 were waited for; matrix products, arithmetic and copies ran while one was open for 1% of the time, Pallas kernels for 0%

commit v1 on v0

v1 whole, which is shorter than its diff:
```python
import functools

import jax
import jax.numpy as jnp
from jax import lax
from jax.experimental import pallas as pl
from jax.experimental.pallas import tpu as pltpu
from jax.sharding import PartitionSpec as P

F32 = jnp.float32
BF16 = jnp.bfloat16
LANES = 128
VMEM = pl.BlockSpec(memory_space=pltpu.VMEM)


def pairs(count, first, periodic):
    out = []
    for low in range(first, count - 1, 2):
        out += [(low, low + 1), (low + 1, low)]
    if first and periodic:
        out += [(count - 1, 0), (0, count - 1)]
    return out


def lane_index(rows):
    return lax.broadcasted_iota(jnp.int32, (rows, LANES), 1)


def pack_kernel(dims, u, v, w, rho, fields, x0, x1, y0, y1, z0, z1, wide):
    snaps, nx, ny = dims
    cells = nx * ny
    x_even = lax.axis_index("gx") % 2 == 0
    y_even = lax.axis_index("gy") % 2 == 0
    z_even = lax.axis_index("gz") % 2 == 0
    lane = lane_index(snaps)
    column = jnp.zeros((snaps, LANES), F32)
    for f, ref in enumerate((u, v, w, rho)):
        wide[f] = ref[...].astype(F32)

    def row(f, r):
        return wide[f, pl.ds(r, snaps, stride=cells), :]

    for f in range(4):
        for r in range(cells):
            cell = row(f, r)
            fields[f, r] = cell.astype(BF16)
            if f >= 2:
                k = (f - 2) * cells + r
                moved = pltpu.roll(cell, 2 * k + 1, 1)
                column = jnp.where((lane == 2 * k) | (lane == 2 * k + 1), moved, column)
    for i, f in enumerate((0, 3)):
        for y in range(ny):
            first, final = fields[f, y], fields[f, (nx - 1) * ny + y]
            x0[i, y] = jnp.where(x_even, final, first)
            x1[i, y] = jnp.where(x_even, first, final)
    for i, f in enumerate((1, 3)):
        for x in range(nx):
            first, final = fields[f, x * ny], fields[f, x * ny + ny - 1]
            y0[i, x] = jnp.where(y_even, final, first)
            y1[i, x] = jnp.where(y_even, first, final)
    final = jnp.where(lane % 2 == 0, column, 0.0)
    first = jnp.where(lane % 2 == 1, column, 0.0)
    z0[...] = jnp.where(z_even, final, first).astype(BF16)
    z1[...] = jnp.where(z_even, first, final).astype(BF16)


def panel_kernel(dims, scale, sizes, fields, x0, x1, y0, y1, z0, z1, panel, moments):
    snaps, nx, ny = dims
    cells = nx * ny
    at_x, at_y = lax.axis_index("gx"), lax.axis_index("gy")
    x_even, y_even = at_x % 2 == 0, at_y % 2 == 0
    lane = lane_index(snaps)
    edges = z0[...].astype(F32) + z1[...].astype(F32)

    def cell(f, r):
        return fields[f, r].astype(F32)

    def side(even, edge, own, recv_even, recv_odd):
        return jnp.where(edge, own, jnp.where(even, recv_even, recv_odd)).astype(F32)

    def diff_x(f, i, x, y):
        r = x * ny + y
        if x == 0:
            left = side(x_even, at_x == 0, fields[f, y], x1[i, y], x0[i, y])
        else:
            left = cell(f, r - ny)
        if x == nx - 1:
            right = side(x_even, at_x == sizes[0] - 1, fields[f, r], x0[i, y], x1[i, y])
        else:
            right = cell(f, r + ny)
        return right - left

    def diff_y(f, i, x, y):
        r = x * ny + y
        if y == 0:
            left = side(y_even, at_y == 0, fields[f, r], y1[i, x], y0[i, x])
        else:
            left = cell(f, r - 1)
        if y == ny - 1:
            right = side(y_even, at_y == sizes[1] - 1, fields[f, r], y0[i, x], y1[i, x])
        else:
            right = cell(f, r + 1)
        return right - left

    def diff_z(f, i, r):
        k = i * cells + r
        value = cell(f, r)
        ends = jnp.take_along_axis(
            edges, jnp.where(lane == LANES - 1, 2 * k + 1, 2 * k), axis=1
        )
        left = jnp.where(lane == 0, ends, pltpu.roll(value, 1, 1))
        right = jnp.where(lane == LANES - 1, ends, pltpu.roll(value, LANES - 1, 1))
        return right - left

    def put(c, value):
        high = value.astype(BF16)
        panel[0:snaps, c * LANES : (c + 1) * LANES] = high
        panel[snaps : 2 * snaps, c * LANES : (c + 1) * LANES] = (
            value - high.astype(F32)
        ).astype(BF16)

    for x in range(nx):
        for y in range(ny):
            r = x * ny + y
            dilatation = 0.5 * (diff_x(0, 0, x, y) + diff_y(1, 0, x, y) + diff_z(2, 0, r))
            put(r, dilatation)
            rx, ry, rz = diff_x(3, 1, x, y), diff_y(3, 1, x, y), diff_z(3, 1, r)
            put(cells + r, jnp.sqrt(0.25 * (rx * rx + ry * ry + rz * rz) + 0.25))

    def product(a, b):
        return lax.dot_general(a, b, (((1,), (1,)), ((), ())), preferred_element_type=F32)

    high, low = panel[0:snaps, :], panel[snaps : 2 * snaps, :]
    moments[...] = (product(high, high) + product(high, low) + product(low, high)) * scale


def basis_kernel(dims, moments, panel, basis, factor, work, inverse):
    snaps, nx, ny = dims
    cells = 2 * nx * ny
    lane = lane_index(8)
    sub = lax.broadcasted_iota(jnp.int32, (8, LANES), 0)
    groups = snaps // 8
    work[...] = jnp.zeros_like(work)
    work[:, 0:snaps] = moments[...]

    def spread(value, j):
        return jnp.broadcast_to(value[:, j : j + 1], (8, LANES))

    for g in range(groups):
        base = 8 * g
        rows = [jnp.broadcast_to(work[base + i : base + i + 1, :], (8, LANES)) for i in range(8)]
        small = [[spread(rows[i], base + j) for j in range(i + 1)] for i in range(8)]
        ratio = []
        for j in range(8):
            here = base + j
            root = lax.rsqrt(small[j][j])
            inv = root * root
            ratio.append(inv)
            pivot = jnp.where(lane == here, 1.0, rows[j])
            for i in range(j + 1, 8):
                m = small[i][j] * inv
                rows[i] = jnp.where(lane == here, 0.0, rows[i]) - m * pivot
                for k in range(j + 1, i + 1):
                    small[i][k] = small[i][k] - m * small[k][j]
            scaled = rows[j] * root
            factor[here : here + 1, :] = jnp.where(lane >= here, scaled, 0.0)[0:1, 0:snaps]
            inverse[here : here + 1, :] = jnp.where(
                lane < here, scaled, jnp.where(lane == here, root, 0.0)
            )[0:1, :]
        outer = []
        for j in range(8):
            here = base + j
            clean = jnp.where((lane > here) & (lane < base + 8), 0.0, rows[j])
            outer.append(jnp.where(lane == here, 1.0, clean))
        inside = (lane >= base) & (lane < base + 8)
        for h in range(g + 1, groups):
            block = jnp.where(inside, 0.0, work[8 * h : 8 * h + 8, :])
            for j in range(8):
                m = jnp.take_along_axis(rows[j] * ratio[j], sub + 8 * h, axis=1)
                block = block - m * outer[j]
            work[8 * h : 8 * h + 8, :] = block

    low_inv = inverse[:, 0:snaps]
    high = low_inv.astype(BF16)
    rest = (low_inv - high.astype(F32)).astype(BF16)
    left = jnp.concatenate([high, high], axis=1)
    for c in range(cells):
        block = panel[:, c * LANES : (c + 1) * LANES]
        out = jnp.dot(left, block, preferred_element_type=F32) + jnp.dot(
            rest, block[0:snaps, :], preferred_element_type=F32
        )
        basis[pl.ds(c, snaps, stride=cells), :] = out


def swap(value, axis, first, periodic=False):
    return lax.ppermute(value, axis, pairs(lax.axis_size(axis), first, periodic))


def total_over(value, axis):
    count = lax.axis_size(axis)
    if count & (count - 1):
        return lax.psum(value, axis)
    step = 1
    while step < count:
        value = value + lax.ppermute(value, axis, [(i, i ^ step) for i in range(count)])
        step *= 2
    return value


def per_device(vel_u, vel_v, vel_w, density):
    snaps, nx, ny, nz = vel_u.shape
    cells = nx * ny
    dims = (snaps, nx, ny)
    sizes = tuple(lax.axis_size(a) for a in ("gx", "gy", "gz"))
    flat = [a.reshape(snaps * cells, nz) for a in (vel_u, vel_v, vel_w, density)]
    params = pltpu.CompilerParams(vmem_limit_bytes=48 << 20)
    x_face = jax.ShapeDtypeStruct((2, ny, snaps, nz), BF16)
    y_face = jax.ShapeDtypeStruct((2, nx, snaps, nz), BF16)
    z_face = jax.ShapeDtypeStruct((snaps, nz), BF16)
    fields, x0, x1, y0, y1, z0, z1 = pl.pallas_call(
        functools.partial(pack_kernel, dims),
        out_shape=(
            jax.ShapeDtypeStruct((4, cells, snaps, nz), BF16),
            x_face,
            x_face,
            y_face,
            y_face,
            z_face,
            z_face,
        ),
        in_specs=[VMEM] * 4,
        out_specs=[VMEM] * 7,
        scratch_shapes=[pltpu.VMEM((4, snaps * cells, nz), F32)],
        compiler_params=params,
        name="pack",
    )(*flat)
    x0 = swap(x0, "gx", 0)
    y0 = swap(y0, "gy", 0)
    if sizes[1] > 2:
        y1 = swap(y1, "gy", 1)
    z0 = swap(z0, "gz", 0)
    z1 = swap(z1, "gz", 1, True)
    if sizes[0] > 2:
        x1 = swap(x1, "gx", 1)
    scale = 1.0 / (2 * cells * nz * sizes[0] * sizes[1] * sizes[2])
    panel, moments = pl.pallas_call(
        functools.partial(panel_kernel, dims, scale, sizes),
        out_shape=(
            jax.ShapeDtypeStruct((2 * snaps, 2 * cells * nz), BF16),
            jax.ShapeDtypeStruct((snaps, snaps), F32),
        ),
        in_specs=[VMEM] * 7,
        out_specs=[VMEM] * 2,
        compiler_params=params,
        name="panel",
    )(fields, x0, x1, y0, y1, z0, z1)
    for axis in ("gz", "gy", "gx"):
        moments = total_over(moments, axis)
    basis, factor = pl.pallas_call(
        functools.partial(basis_kernel, dims),
        out_shape=(
            jax.ShapeDtypeStruct((snaps * 2 * cells, nz), F32),
            jax.ShapeDtypeStruct((snaps, snaps), F32),
        ),
        in_specs=[VMEM] * 2,
        out_specs=[VMEM] * 2,
        scratch_shapes=[pltpu.VMEM((snaps, LANES), F32), pltpu.VMEM((snaps, LANES), F32)],
        compiler_params=params,
        name="basis",
    )(moments, panel)
    return basis.reshape(snaps, 2, nx, ny, nz), factor


def solution(mesh):
    spec = P(None, "gx", "gy", "gz")
    return jax.shard_map(
        per_device,
        mesh=mesh,
        in_specs=(spec,) * 4,
        out_specs=(P(None, None, "gx", "gy", "gz"), P()),
        check_vma=False,
    )
```

time: 506 us -> 45.5 us (0.09)
  other arithmetic: 354 us -> 0.04 us
  blocking collectives: 42.1 us -> 0 us
  local copies, waits for them, and re-layouts: 40.7 us -> 3.97 us
  waiting for transfers between devices: 43.4 us -> 14 us
  matrix products: 14.7 us -> 0 us
  starting transfers between devices: 7.5 us -> 17.1 us
  Pallas kernels: 0 us -> 9.51 us
    another operation x99 -> x0, other arithmetic: 310 us -> none  [the longest x93 293 us: combine(): return jnp.linalg.cholesky(total)]
    all_gather x1 -> x0, blocking collectives: 42.1 us -> none  [merged(): everything = lax.all_gather(shard.astype(jnp.bfloat16), axis)]
    ppermute x6 -> x10, waiting for transfers between devices: 43.4 us -> 14 us  [the longest x5 11.5 us: total_over(): lax.ppermute(value, axis, [(i, i ^ step) for i in range(count)])]
    select_n x33 -> x0, other arithmetic: 21.6 us -> none  [the longest x31 20.3 us: combine(): return jnp.linalg.cholesky(total)]
    slice x9 -> x0, local copies, waits for them, and re-layouts: 20.7 us -> none  [the longest x2 5.68 us: with_halo(): lax.slice_in_dim(cells, cells.shape[dim] - width, cells.shape[dim], axis=...]
    concatenate x3 -> x0, other arithmetic: 14.1 us -> none  [the longest x2 12.7 us: with_halo(): jnp.concatenate([lax.ppermute(tail, axis, [(i, (i + 1) % count) for i in...]
    dot_general x63 -> x0, matrix products: 12.4 us -> none  [the longest x31 6.94 us: combine(): jnp.dot(left_part, left_part.T, precision=lax.Precision.HIGHEST, preferre...]
    ppermute x6 -> x10, starting transfers between devices: 7.5 us -> 17.1 us  [the longest x5 10.1 us: total_over(): lax.ppermute(value, axis, [(i, i ^ step) for i in range(count)])]
  transfers between devices with their start and end apart: 6 -> 10, of which waited for: 5 -> 7; matrix products, arithmetic and copies ran while one was open for 1% -> 0% of each run, Pallas kernels for 0% -> 0%
where the time goes in v1:
time: 45.5 us; the launch traced here: 45.2 us
  starting transfers between devices  17.1 us (38%)
  waiting for transfers between devices  14 us (31%)
  Pallas kernels  9.51 us (21%)
  local copies, waits for them, and re-layouts  3.97 us (9%)
  between operations  0.68 us (1%)
    ppermute x5, waiting for transfers between devices, total_over(): lax.ppermute(value, axis, [(i, i ^ step) for i in range(count)])  11.5 us
    ppermute x5, starting transfers between devices, total_over(): lax.ppermute(value, axis, [(i, i ^ step) for i in range(count)])  10.1 us
    ppermute x5, starting transfers between devices, swap(): lax.ppermute(value, axis, pairs(lax.axis_size(axis), first, periodic))  6.95 us
    pallas_call x1, Pallas kernels, per_device(): pl.pallas_call(functools.partial(basis_kernel, dims), out_shape=(jax.Shap...  5.99 us
    unnamed x8, local copies, waits for them, and re-layouts  3.97 us
    ppermute x5, waiting for transfers between devices, swap(): lax.ppermute(value, axis, pairs(lax.axis_size(axis), first, periodic))  2.43 us
    pallas_call x1, Pallas kernels, per_device(): pl.pallas_call(functools.partial(panel_kernel, dims, scale, sizes), out_s...  2.2 us
    pallas_call x1, Pallas kernels, per_device(): pl.pallas_call(functools.partial(pack_kernel, dims), out_shape=(jax.Shape...  1.32 us
  transfers between devices with their start and end apart: 10, of which 7 were waited for; matrix products, arithmetic and copies ran while one was open for 0% of the time, Pallas kernels for 0%

profile of v1, /device:TPU:0, one launch (start us, length us, event | category | flops | bytes accessed | tf_op | source)
XLA Modules:
  0.0 45.2 jit_solution(4652402647694367966)
XLA Ops:
  0.6 1.0 %copy-done = bf16[96,4,4,128]{3,2,1,0:T(4,128)(2,1)S(1)} copy-done((bf16[96,4,4,128]{3,2,1,0:T(4,128)(2,1)S(1)}, bf16[96,4,4,128]{3,2,1,0:T(4,128)(2,1)}, u32[]{:S(2)}) %copy-start) | copy-done | bytes 393240
  1.6 1.0 %copy-done.1 = bf16[96,4,4,128]{3,2,1,0:T(4,128)(2,1)S(1)} copy-done((bf16[96,4,4,128]{3,2,1,0:T(4,128)(2,1)S(1)}, bf16[96,4,4,128]{3,2,1,0:T(4,128)(2,1)}, u32[]{:S(2)}) %copy-start.1) | copy-done | bytes 393240
  2.6 1.0 %copy-done.2 = bf16[96,4,4,128]{3,2,1,0:T(4,128)(2,1)S(1)} copy-done((bf16[96,4,4,128]{3,2,1,0:T(4,128)(2,1)S(1)}, bf16[96,4,4,128]{3,2,1,0:T(4,128)(2,1)}, u32[]{:S(2)}) %copy-start.2) | copy-done | bytes 393240
  3.6 1.0 %copy-done.3 = bf16[96,4,4,128]{3,2,1,0:T(4,128)(2,1)S(1)} copy-done((bf16[96,4,4,128]{3,2,1,0:T(4,128)(2,1)S(1)}, bf16[96,4,4,128]{3,2,1,0:T(4,128)(2,1)}, u32[]{:S(2)}) %copy-start.3) | copy-done | bytes 393240
  4.6 1.3 %pack.1 = (bf16[4,16,96,128]{3,2,1,0:T(8,128)(2,1)S(1)}, bf16[2,4,96,128]{3,2,1,0:T(8,128)(2,1)S(1)}, bf16[2,4,96,128]{3,2,1,0:T(8,128)(2,1)S(1)}, bf16[2,4,96,1...) custom-call(bf16[1536,128]{1,0:T(8,128)(2,1)S(1)} %bitcast.5, ...), custom_call_target="tpu_custom_call" | custom-call | tf_op jit(solution)/shard_map/pack/pallas_call | solution.py:220
  5.9 3.0 %collective-permute-start = (bf16[2,4,96,128]{3,2,1,0:T(8,128)(2,1)S(1)}, bf16[2,4,96,128]{3,2,1,0:T(8,128)(2,1)S(1)}, u32[]{:S(2)}, u32[]{:S(2)}) collective-permute-start(bf16[2,4,96,128]{3,2,1,0:T(8,128)(2,1)S(1)} %get-tuple-element.14), channel_id=1, source_target_pairs={{0,16},{16,0},{1,17},{17,1},{2,18},{18,2},{3,19},{19,3},{4,20},{20... | collective-permute-start | bytes 589832 | tf_op jit(solution)/shard_map/ppermute | solution.py:196
  9.0 1.6 %collective-permute-start.1 = (bf16[2,4,96,128]{3,2,1,0:T(8,128)(2,1)S(1)}, bf16[2,4,96,128]{3,2,1,0:T(8,128)(2,1)S(1)}, u32[]{:S(2)}, u32[]{:S(2)}) collective-permute-start(bf16[2,4,96,128]{3,2,1,0:T(8,128)(2,1)S(1)} %get-tuple-element.16), channel_id=1, source_target_pairs={{0,4},{4,0},{8,12},{12,8},{1,5},{5,1},{9,13},{13,9},{2,6},{6,2},{1... | collective-permute-start | bytes 589832 | tf_op jit(solution)/shard_map/ppermute | solution.py:196
  10.6 0.7 %collective-permute-start.2 = (bf16[2,4,96,128]{3,2,1,0:T(8,128)(2,1)S(1)}, bf16[2,4,96,128]{3,2,1,0:T(8,128)(2,1)S(1)}, u32[]{:S(2)}, u32[]{:S(2)}) collective-permute-start(bf16[2,4,96,128]{3,2,1,0:T(8,128)(2,1)S(1)} %get-tuple-element.17), channel_id=1, source_target_pairs={{4,8},{8,4},{5,9},{9,5},{6,10},{10,6},{7,11},{11,7},{20,24},{24,20... | collective-permute-start | bytes 589832 | tf_op jit(solution)/shard_map/ppermute | solution.py:196
  11.2 0.1 collective-permute-start.3
  11.3 1.6 %collective-permute-start.4 = (bf16[96,128]{1,0:T(8,128)(2,1)S(1)}, bf16[96,128]{1,0:T(8,128)(2,1)S(1)}, u32[]{:S(2)}, u32[]{:S(2)}) collective-permute-start(bf16[96,128]{1,0:T(8,128)(2,1)S(1)} %get-tuple-element.19), channel_id=1, source_target_pairs={{1,2},{2,1},{3,0},{0,3},{5,6},{6,5},{7,4},{4,7},{9,10},{10,9},{11,... | collective-permute-start | bytes 73736 | tf_op jit(solution)/shard_map/ppermute | solution.py:196
  12.9 1.7 %collective-permute-done.4.z1 = bf16[96,128]{1,0:T(8,128)(2,1)S(1)} collective-permute-done((bf16[96,128]{1,0:T(8,128)(2,1)S(1)}, bf16[96,128]{1,0:T(8,128)(2,1)S(1)}, u32[]{:S(2)}, u32[]{:S(2)}) %collective-permute-start.4) | collective-permute-done | bytes 24608 | tf_op jit(solution)/shard_map/ppermute | solution.py:196
  14.6 0.7 %collective-permute-done.1.y0 = bf16[2,4,96,128]{3,2,1,0:T(8,128)(2,1)S(1)} collective-permute-done((bf16[2,4,96,128]{3,2,1,0:T(8,128)(2,1)S(1)}, bf16[2,4,96,128]{3,2,1,0:T(8,128)(2,1)S(1)}, u32[]{:S(2)}, u32[]{:S(2)}) %collective-permute-start.1) | collective-permute-done | bytes 196640 | tf_op jit(solution)/shard_map/ppermute | solution.py:196
  15.3 2.2 %panel.1 = (bf16[192,4096]{1,0:T(8,128)(2,1)S(1)}, f32[96,96]{1,0:T(8,128)S(1)}) custom-call(bf16[4,16,96,128]{3,2,1,0:T(8,128)(2,1)S(1)} %get-tuple-element.13.fields, bf16[2,4,96,128]{3,2,1,0:T(8,128)(2,1)S(1)} %collective-permute-done.x0, bf16[2,4,96,128]{3,2,1,0:T(8,128)(2,1)S(1)} %get-tuple-element.15.x1, ...), custom_call_target="tpu_custom_call" | custom-call | tf_op jit(solution)/shard_map/panel/pallas_call | solution.py:246
  17.6 0.1 collective-permute-start.5
  17.6 1.2 %collective-permute-done.5 = f32[96,96]{1,0:T(8,128)S(1)} collective-permute-done((f32[96,96]{1,0:T(8,128)S(1)}, f32[96,96]{1,0:T(8,128)S(1)}, u32[]{:S(2)}, u32[]{:S(2)}) %collective-permute-start.5) | collective-permute-done | bytes 36896 | tf_op jit(solution)/shard_map/ppermute | solution.py:205
  18.9 1.5 %collective-permute-start.6 = (f32[96,96]{1,0:T(8,128)S(1)}, f32[96,96]{1,0:T(8,128)S(1)}, u32[]{:S(2)}, u32[]{:S(2)}) collective-permute-start(f32[96,96]{1,0:T(8,128)S(1)} %add.15), channel_id=1, source_target_pairs={{0,2},{1,3},{2,0},{3,1},{4,6},{5,7},{6,4},{7,5},{8,10},{9,11},{10,... | collective-permute-start | bytes 110600 | tf_op jit(solution)/shard_map/ppermute | solution.py:205
  20.4 2.6 %collective-permute-done.6 = f32[96,96]{1,0:T(8,128)S(1)} collective-permute-done((f32[96,96]{1,0:T(8,128)S(1)}, f32[96,96]{1,0:T(8,128)S(1)}, u32[]{:S(2)}, u32[]{:S(2)}) %collective-permute-start.6) | collective-permute-done | bytes 36896 | tf_op jit(solution)/shard_map/ppermute | solution.py:205
  23.0 4.7 %collective-permute-start.7 = (f32[96,96]{1,0:T(8,128)S(1)}, f32[96,96]{1,0:T(8,128)S(1)}, u32[]{:S(2)}, u32[]{:S(2)}) collective-permute-start(f32[96,96]{1,0:T(8,128)S(1)} %add.16), channel_id=1, source_target_pairs={{0,4},{4,0},{8,12},{12,8},{1,5},{5,1},{9,13},{13,9},{2,6},{6,2},{1... | collective-permute-start | bytes 110600 | tf_op jit(solution)/shard_map/ppermute | solution.py:205
  27.7 2.1 %collective-permute-done.7 = f32[96,96]{1,0:T(8,128)S(1)} collective-permute-done((f32[96,96]{1,0:T(8,128)S(1)}, f32[96,96]{1,0:T(8,128)S(1)}, u32[]{:S(2)}, u32[]{:S(2)}) %collective-permute-start.7) | collective-permute-done | bytes 36896 | tf_op jit(solution)/shard_map/ppermute | solution.py:205
  29.7 3.3 %collective-permute-start.8 = (f32[96,96]{1,0:T(8,128)S(1)}, f32[96,96]{1,0:T(8,128)S(1)}, u32[]{:S(2)}, u32[]{:S(2)}) collective-permute-start(f32[96,96]{1,0:T(8,128)S(1)} %add.17), channel_id=1, source_target_pairs={{0,8},{4,12},{8,0},{12,4},{1,9},{5,13},{9,1},{13,5},{2,10},{6,14},... | collective-permute-start | bytes 110600 | tf_op jit(solution)/shard_map/ppermute | solution.py:205
  33.0 2.1 %collective-permute-done.8 = f32[96,96]{1,0:T(8,128)S(1)} collective-permute-done((f32[96,96]{1,0:T(8,128)S(1)}, f32[96,96]{1,0:T(8,128)S(1)}, u32[]{:S(2)}, u32[]{:S(2)}) %collective-permute-start.8) | collective-permute-done | bytes 36896 | tf_op jit(solution)/shard_map/ppermute | solution.py:205
  35.1 0.6 %collective-permute-start.9 = (f32[96,96]{1,0:T(8,128)S(1)}, f32[96,96]{1,0:T(8,128)S(1)}, u32[]{:S(2)}, u32[]{:S(2)}) collective-permute-start(f32[96,96]{1,0:T(8,128)S(1)} %add.18), channel_id=1, source_target_pairs={{0,16},{16,0},{1,17},{17,1},{2,18},{18,2},{3,19},{19,3},{4,20},{20... | collective-permute-start | bytes 110600 | tf_op jit(solution)/shard_map/ppermute | solution.py:205
  35.6 3.6 %collective-permute-done.9 = f32[96,96]{1,0:T(8,128)S(1)} collective-permute-done((f32[96,96]{1,0:T(8,128)S(1)}, f32[96,96]{1,0:T(8,128)S(1)}, u32[]{:S(2)}, u32[]{:S(2)}) %collective-permute-start.9) | collective-permute-done | bytes 36896 | tf_op jit(solution)/shard_map/ppermute | solution.py:205
  39.2 6.0 %basis.1 = (f32[3072,128]{1,0:T(8,128)}, f32[96,96]{1,0:T(8,128)}) custom-call(f32[96,96]{1,0:T(8,128)S(1)} %add.19.moments, bf16[192,4096]{1,0:T(8,128)(2,1)S(1)} %get-tuple-element.21.panel), custom_call_target="tpu_custom_call" | custom-call | tf_op jit(solution)/shard_map/basis/pallas_call | solution.py:259
  (12 shorter events, 0.1 us)
Async XLA Ops:
  0.6 1.0 %copy-start = (bf16[96,4,4,128]{3,2,1,0:T(4,128)(2,1)S(1)}, bf16[96,4,4,128]{3,2,1,0:T(4,128)(2,1)}, u32[]{:S(2)}) copy-start(bf16[96,4,4,128]{3,2,1,0:T(4,128)(2,1)} %param.4) | copy-start | bytes 1179652
  1.6 1.0 %copy-start.1 = (bf16[96,4,4,128]{3,2,1,0:T(4,128)(2,1)S(1)}, bf16[96,4,4,128]{3,2,1,0:T(4,128)(2,1)}, u32[]{:S(2)}) copy-start(bf16[96,4,4,128]{3,2,1,0:T(4,128)(2,1)} %param.5) | copy-start | bytes 1179652
  2.6 1.0 %copy-start.2 = (bf16[96,4,4,128]{3,2,1,0:T(4,128)(2,1)S(1)}, bf16[96,4,4,128]{3,2,1,0:T(4,128)(2,1)}, u32[]{:S(2)}) copy-start(bf16[96,4,4,128]{3,2,1,0:T(4,128)(2,1)} %param.6) | copy-start | bytes 1179652
  3.6 1.0 %copy-start.3 = (bf16[96,4,4,128]{3,2,1,0:T(4,128)(2,1)S(1)}, bf16[96,4,4,128]{3,2,1,0:T(4,128)(2,1)}, u32[]{:S(2)}) copy-start(bf16[96,4,4,128]{3,2,1,0:T(4,128)(2,1)} %param.7) | copy-start | bytes 1179652
  5.9 8.7 %collective-permute-start = (bf16[2,4,96,128]{3,2,1,0:T(8,128)(2,1)S(1)}, bf16[2,4,96,128]{3,2,1,0:T(8,128)(2,1)S(1)}, u32[]{:S(2)}, u32[]{:S(2)}) collective-permute-start(bf16[2,4,96,128]{3,2,1,0:T(8,128)(2,1)S(1)} %get-tuple-element.14), channel_id=1, source_target_pairs={{0,16},{16,0},{1,17},{17,1},{2,18},{18,2},{3,19},{19,3},{4,20},{20... | collective-permute-start | bytes 589832 | tf_op jit(solution)/shard_map/ppermute | solution.py:196
  9.0 6.4 %collective-permute-start.1 = (bf16[2,4,96,128]{3,2,1,0:T(8,128)(2,1)S(1)}, bf16[2,4,96,128]{3,2,1,0:T(8,128)(2,1)S(1)}, u32[]{:S(2)}, u32[]{:S(2)}) collective-permute-start(bf16[2,4,96,128]{3,2,1,0:T(8,128)(2,1)S(1)} %get-tuple-element.16), channel_id=1, source_target_pairs={{0,4},{4,0},{8,12},{12,8},{1,5},{5,1},{9,13},{13,9},{2,6},{6,2},{1... | collective-permute-start | bytes 589832 | tf_op jit(solution)/shard_map/ppermute | solution.py:196
  10.6 4.8 %collective-permute-start.2 = (bf16[2,4,96,128]{3,2,1,0:T(8,128)(2,1)S(1)}, bf16[2,4,96,128]{3,2,1,0:T(8,128)(2,1)S(1)}, u32[]{:S(2)}, u32[]{:S(2)}) collective-permute-start(bf16[2,4,96,128]{3,2,1,0:T(8,128)(2,1)S(1)} %get-tuple-element.17), channel_id=1, source_target_pairs={{4,8},{8,4},{5,9},{9,5},{6,10},{10,6},{7,11},{11,7},{20,24},{24,20... | collective-permute-start | bytes 589832 | tf_op jit(solution)/shard_map/ppermute | solution.py:196
  11.2 1.7 %collective-permute-start.3 = (bf16[96,128]{1,0:T(8,128)(2,1)S(1)}, bf16[96,128]{1,0:T(8,128)(2,1)S(1)}, u32[]{:S(2)}, u32[]{:S(2)}) collective-permute-start(bf16[96,128]{1,0:T(8,128)(2,1)S(1)} %get-tuple-element.18), channel_id=1, source_target_pairs={{0,1},{1,0},{2,3},{3,2},{4,5},{5,4},{6,7},{7,6},{8,9},{9,8},{10,11... | collective-permute-start | bytes 73736 | tf_op jit(solution)/shard_map/ppermute | solution.py:196
  11.3 3.3 %collective-permute-start.4 = (bf16[96,128]{1,0:T(8,128)(2,1)S(1)}, bf16[96,128]{1,0:T(8,128)(2,1)S(1)}, u32[]{:S(2)}, u32[]{:S(2)}) collective-permute-start(bf16[96,128]{1,0:T(8,128)(2,1)S(1)} %get-tuple-element.19), channel_id=1, source_target_pairs={{1,2},{2,1},{3,0},{0,3},{5,6},{6,5},{7,4},{4,7},{9,10},{10,9},{11,... | collective-permute-start | bytes 73736 | tf_op jit(solution)/shard_map/ppermute | solution.py:196
  17.6 1.3 %collective-permute-start.5 = (f32[96,96]{1,0:T(8,128)S(1)}, f32[96,96]{1,0:T(8,128)S(1)}, u32[]{:S(2)}, u32[]{:S(2)}) collective-permute-start(f32[96,96]{1,0:T(8,128)S(1)} %get-tuple-element.20), channel_id=1, source_target_pairs={{0,1},{1,0},{2,3},{3,2},{4,5},{5,4},{6,7},{7,6},{8,9},{9,8},{10,11... | collective-permute-start | bytes 110600 | tf_op jit(solution)/shard_map/ppermute | solution.py:205
  18.9 4.1 %collective-permute-start.6 = (f32[96,96]{1,0:T(8,128)S(1)}, f32[96,96]{1,0:T(8,128)S(1)}, u32[]{:S(2)}, u32[]{:S(2)}) collective-permute-start(f32[96,96]{1,0:T(8,128)S(1)} %add.15), channel_id=1, source_target_pairs={{0,2},{1,3},{2,0},{3,1},{4,6},{5,7},{6,4},{7,5},{8,10},{9,11},{10,... | collective-permute-start | bytes 110600 | tf_op jit(solution)/shard_map/ppermute | solution.py:205
  23.0 6.7 %collective-permute-start.7 = (f32[96,96]{1,0:T(8,128)S(1)}, f32[96,96]{1,0:T(8,128)S(1)}, u32[]{:S(2)}, u32[]{:S(2)}) collective-permute-start(f32[96,96]{1,0:T(8,128)S(1)} %add.16), channel_id=1, source_target_pairs={{0,4},{4,0},{8,12},{12,8},{1,5},{5,1},{9,13},{13,9},{2,6},{6,2},{1... | collective-permute-start | bytes 110600 | tf_op jit(solution)/shard_map/ppermute | solution.py:205
  29.7 5.3 %collective-permute-start.8 = (f32[96,96]{1,0:T(8,128)S(1)}, f32[96,96]{1,0:T(8,128)S(1)}, u32[]{:S(2)}, u32[]{:S(2)}) collective-permute-start(f32[96,96]{1,0:T(8,128)S(1)} %add.17), channel_id=1, source_target_pairs={{0,8},{4,12},{8,0},{12,4},{1,9},{5,13},{9,1},{13,5},{2,10},{6,14},... | collective-permute-start | bytes 110600 | tf_op jit(solution)/shard_map/ppermute | solution.py:205
  35.1 4.2 %collective-permute-start.9 = (f32[96,96]{1,0:T(8,128)S(1)}, f32[96,96]{1,0:T(8,128)S(1)}, u32[]{:S(2)}, u32[]{:S(2)}) collective-permute-start(f32[96,96]{1,0:T(8,128)S(1)} %add.18), channel_id=1, source_target_pairs={{0,16},{16,0},{1,17},{17,1},{2,18},{18,2},{3,19},{19,3},{4,20},{20... | collective-permute-start | bytes 110600 | tf_op jit(solution)/shard_map/ppermute | solution.py:205

commit v2 on v1

--- a/solution.py
+++ b/solution.py
@@ -11,6 +11,7 @@
 BF16 = jnp.bfloat16
 LANES = 128
 VMEM = pl.BlockSpec(memory_space=pltpu.VMEM)
+HBM = pl.BlockSpec(memory_space=pltpu.HBM)
 
 
 def pairs(count, first, periodic):
@@ -26,21 +27,50 @@
     return lax.broadcasted_iota(jnp.int32, (rows, LANES), 1)
 
 
-def pack_kernel(dims, u, v, w, rho, fields, x0, x1, y0, y1, z0, z1, wide):
+def fold(full):
+    full = jnp.concatenate([full, jnp.zeros((96, LANES - 96), F32)], axis=1)
+    top, rest = full[0:48], full[48:96]
+    lane = lane_index(48)
+    near = pltpu.roll(rest, 48, 1)
+    far = pltpu.roll(rest, 64, 1)
+    top = jnp.where(lane >= 96, near, top)
+    lane = lane_index(16)
+    middle = jnp.where(lane < 16, near[32:48], top[16:32])
+    bottom = jnp.where(lane < 16, near[0:16], jnp.where(lane < 32, far[16:32], top[32:48]))
+    return jnp.concatenate([top[0:16], middle, bottom], axis=0)
+
+
+def unfold(folded, work):
+    lane = lane_index(16)
+    near = pltpu.roll(folded, 80, 1)
+    far = pltpu.roll(folded[32:48], 64, 1)
+    work[0:48, :] = folded
+    work[48:64, :] = jnp.where(lane < 80, near[0:16], near[32:48])
+    work[64:80, :] = jnp.where(lane < 80, near[16:32], far)
+    work[80:96, :] = jnp.where(lane < 80, near[32:48], near[16:32])
+
+
+def pack_kernel(dims, u, v, w, rho, fields, x0, x1, y0, y1, z0, z1, narrow, wide, arrived):
     snaps, nx, ny = dims
     cells = nx * ny
+    copies = [
+        pltpu.make_async_copy(ref, narrow.at[f], arrived.at[f])
+        for f, ref in enumerate((u, v, w, rho))
+    ]
+    for copy in copies:
+        copy.start()
     x_even = lax.axis_index("gx") % 2 == 0
     y_even = lax.axis_index("gy") % 2 == 0
     z_even = lax.axis_index("gz") % 2 == 0
     lane = lane_index(snaps)
     column = jnp.zeros((snaps, LANES), F32)
-    for f, ref in enumerate((u, v, w, rho)):
-        wide[f] = ref[...].astype(F32)
 
     def row(f, r):
         return wide[f, pl.ds(r, snaps, stride=cells), :]
 
     for f in range(4):
+        copies[f].wait()
+        wide[f] = narrow[f].astype(F32)
         for r in range(cells):
             cell = row(f, r)
             fields[f, r] = cell.astype(BF16)
@@ -131,17 +161,17 @@
         return lax.dot_general(a, b, (((1,), (1,)), ((), ())), preferred_element_type=F32)
 
     high, low = panel[0:snaps, :], panel[snaps : 2 * snaps, :]
-    moments[...] = (product(high, high) + product(high, low) + product(low, high)) * scale
-
-
-def basis_kernel(dims, moments, panel, basis, factor, work, inverse):
+    total = (product(high, high) + product(high, low) + product(low, high)) * scale
+    moments[...] = fold(total)
+
+
+def basis_kernel(dims, moments, panel, basis, factor, work, inverse, ready, sent):
     snaps, nx, ny = dims
     cells = 2 * nx * ny
     lane = lane_index(8)
     sub = lax.broadcasted_iota(jnp.int32, (8, LANES), 0)
     groups = snaps // 8
-    work[...] = jnp.zeros_like(work)
-    work[:, 0:snaps] = moments[...]
+    unfold(moments[...], work)
 
     def spread(value, j):
         return jnp.broadcast_to(value[:, j : j + 1], (8, LANES))
@@ -149,7 +179,7 @@
     for g in range(groups):
         base = 8 * g
         rows = [jnp.broadcast_to(work[base + i : base + i + 1, :], (8, LANES)) for i in range(8)]
-        small = [[spread(rows[i], base + j) for j in range(i + 1)] for i in range(8)]
+        small = [[spread(rows[j], base + i) for j in range(i + 1)] for i in range(8)]
         ratio = []
         for j in range(8):
             here = base + j
@@ -183,13 +213,30 @@
     low_inv = inverse[:, 0:snaps]
     high = low_inv.astype(BF16)
     rest = (low_inv - high.astype(F32)).astype(BF16)
-    left = jnp.concatenate([high, high], axis=1)
-    for c in range(cells):
-        block = panel[:, c * LANES : (c + 1) * LANES]
-        out = jnp.dot(left, block, preferred_element_type=F32) + jnp.dot(
-            rest, block[0:snaps, :], preferred_element_type=F32
+    left = jnp.concatenate(
+        [
+            jnp.concatenate([high, high], axis=1),
+            jnp.concatenate([rest, jnp.zeros_like(rest)], axis=1),
+        ],
+        axis=0,
+    )
+    copies = []
+    for k in range(cells // 8):
+        for c in range(8 * k, 8 * k + 8, 2):
+            both = jnp.dot(
+                left, panel[:, c * LANES : (c + 2) * LANES], preferred_element_type=F32
+            )
+            out = both[0:snaps] + both[snaps : 2 * snaps]
+            for i in range(2):
+                ready[k, pl.ds(c % 8 + i, snaps, stride=8), :] = out[:, i * LANES : (i + 1) * LANES]
+        copies.append(
+            pltpu.make_async_copy(
+                ready.at[k].reshape(snaps, 8, LANES), basis.at[:, 8 * k : 8 * k + 8, :], sent.at[k]
+            )
         )
-        basis[pl.ds(c, snaps, stride=cells), :] = out
+        copies[-1].start()
+    for copy in copies:
+        copy.wait()
 
 
 def swap(value, axis, first, periodic=False):
@@ -212,7 +259,10 @@
     cells = nx * ny
     dims = (snaps, nx, ny)
     sizes = tuple(lax.axis_size(a) for a in ("gx", "gy", "gz"))
-    flat = [a.reshape(snaps * cells, nz) for a in (vel_u, vel_v, vel_w, density)]
+    flat = [
+        pltpu.with_memory_space_constraint(a.reshape(snaps * cells, nz), pltpu.HBM)
+        for a in (vel_u, vel_v, vel_w, density)
+    ]
     params = pltpu.CompilerParams(vmem_limit_bytes=48 << 20)
     x_face = jax.ShapeDtypeStruct((2, ny, snaps, nz), BF16)
     y_face = jax.ShapeDtypeStruct((2, nx, snaps, nz), BF16)
@@ -228,9 +278,13 @@
             z_face,
             z_face,
         ),
-        in_specs=[VMEM] * 4,
+        in_specs=[HBM] * 4,
         out_specs=[VMEM] * 7,
-        scratch_shapes=[pltpu.VMEM((4, snaps * cells, nz), F32)],
+        scratch_shapes=[
+            pltpu.VMEM((4, snaps * cells, nz), BF16),
+            pltpu.VMEM((4, snaps * cells, nz), F32),
+            pltpu.SemaphoreType.DMA((4,)),
+        ],
         compiler_params=params,
         name="pack",
     )(*flat)
@@ -247,7 +301,7 @@
         functools.partial(panel_kernel, dims, scale, sizes),
         out_shape=(
             jax.ShapeDtypeStruct((2 * snaps, 2 * cells * nz), BF16),
-            jax.ShapeDtypeStruct((snaps, snaps), F32),
+            jax.ShapeDtypeStruct((snaps // 2, LANES), F32),
         ),
         in_specs=[VMEM] * 7,
         out_specs=[VMEM] * 2,
@@ -259,12 +313,17 @@
     basis, factor = pl.pallas_call(
         functools.partial(basis_kernel, dims),
         out_shape=(
-            jax.ShapeDtypeStruct((snaps * 2 * cells, nz), F32),
+            jax.ShapeDtypeStruct((snaps, 2 * cells, nz), F32),
             jax.ShapeDtypeStruct((snaps, snaps), F32),
         ),
         in_specs=[VMEM] * 2,
-        out_specs=[VMEM] * 2,
-        scratch_shapes=[pltpu.VMEM((snaps, LANES), F32), pltpu.VMEM((snaps, LANES), F32)],
+        out_specs=[HBM, VMEM],
+        scratch_shapes=[
+            pltpu.VMEM((snaps, LANES), F32),
+            pltpu.VMEM((snaps, LANES), F32),
+            pltpu.VMEM((cells // 4, snaps * 8, nz), F32),
+            pltpu.SemaphoreType.DMA((cells // 4,)),
+        ],
         compiler_params=params,
         name="basis",
     )(moments, panel)

time: 45.5 us -> 40.5 us (0.89)
  local copies, waits for them, and re-layouts: 3.97 us -> 0 us
  waiting for transfers between devices: 14 us -> 12.9 us
  Pallas kernels: 9.51 us -> 10 us
    unnamed x8 -> x0, local copies, waits for them, and re-layouts: 3.97 us -> none
    pallas_call x1, Pallas kernels: 1.32 us -> 2.54 us  [per_device(): pl.pallas_call(functools.partial(pack_kernel, dims), out_shape=(jax.Shape...]
    ppermute x5, waiting for transfers between devices: 11.5 us -> 10.4 us  [total_over(): lax.ppermute(value, axis, [(i, i ^ step) for i in range(count)])]
    pallas_call x1, Pallas kernels: 5.99 us -> 5.21 us  [per_device(): pl.pallas_call(functools.partial(basis_kernel, dims), out_shape=(jax.Shap...]
where the time goes in v2:
time: 40.5 us; the launch traced here: 40.4 us
  starting transfers between devices  16.8 us (41%)
  waiting for transfers between devices  12.9 us (32%)
  Pallas kernels  10 us (25%)
  between operations  0.67 us (2%)
    ppermute x5, waiting for transfers between devices, total_over(): lax.ppermute(value, axis, [(i, i ^ step) for i in range(count)])  10.4 us
    ppermute x5, starting transfers between devices, total_over(): lax.ppermute(value, axis, [(i, i ^ step) for i in range(count)])  9.86 us
    ppermute x5, starting transfers between devices, swap(): lax.ppermute(value, axis, pairs(lax.axis_size(axis), first, periodic))  6.95 us
    pallas_call x1, Pallas kernels, per_device(): pl.pallas_call(functools.partial(basis_kernel, dims), out_shape=(jax.Shap...  5.21 us
    pallas_call x1, Pallas kernels, per_device(): pl.pallas_call(functools.partial(pack_kernel, dims), out_shape=(jax.Shape...  2.54 us
    ppermute x5, waiting for transfers between devices, swap(): lax.ppermute(value, axis, pairs(lax.axis_size(axis), first, periodic))  2.43 us
    pallas_call x1, Pallas kernels, per_device(): pl.pallas_call(functools.partial(panel_kernel, dims, scale, sizes), out_s...  2.27 us
  transfers between devices with their start and end apart: 10, of which 7 were waited for; matrix products, arithmetic and copies ran while one was open for 0% of the time, Pallas kernels for 0%

profile of v2, /device:TPU:0, one launch (start us, length us, event | category | flops | bytes accessed | tf_op | source)
XLA Modules:
  0.0 40.4 jit_solution(13022788941350664929)
XLA Ops:
  0.6 2.5 %pack.1 = (bf16[4,16,96,128]{3,2,1,0:T(8,128)(2,1)S(1)}, bf16[2,4,96,128]{3,2,1,0:T(8,128)(2,1)S(1)}, bf16[2,4,96,128]{3,2,1,0:T(8,128)(2,1)S(1)}, bf16[2,4,96,1...) custom-call(bf16[1536,128]{1,0:T(8,128)(2,1)} %bitcast.5, ...), custom_call_target="tpu_custom_call" | custom-call | tf_op jit(solution)/shard_map/pack/pallas_call | solution.py:270
  3.2 3.0 %collective-permute-start = (bf16[2,4,96,128]{3,2,1,0:T(8,128)(2,1)S(1)}, bf16[2,4,96,128]{3,2,1,0:T(8,128)(2,1)S(1)}, u32[]{:S(2)}, u32[]{:S(2)}) collective-permute-start(bf16[2,4,96,128]{3,2,1,0:T(8,128)(2,1)S(1)} %get-tuple-element.14), channel_id=1, source_target_pairs={{0,16},{16,0},{1,17},{17,1},{2,18},{18,2},{3,19},{19,3},{4,20},{20... | collective-permute-start | bytes 589832 | tf_op jit(solution)/shard_map/ppermute | solution.py:243
  6.2 1.6 %collective-permute-start.1 = (bf16[2,4,96,128]{3,2,1,0:T(8,128)(2,1)S(1)}, bf16[2,4,96,128]{3,2,1,0:T(8,128)(2,1)S(1)}, u32[]{:S(2)}, u32[]{:S(2)}) collective-permute-start(bf16[2,4,96,128]{3,2,1,0:T(8,128)(2,1)S(1)} %get-tuple-element.16), channel_id=1, source_target_pairs={{0,4},{4,0},{8,12},{12,8},{1,5},{5,1},{9,13},{13,9},{2,6},{6,2},{1... | collective-permute-start | bytes 589832 | tf_op jit(solution)/shard_map/ppermute | solution.py:243
  7.8 0.7 %collective-permute-start.2 = (bf16[2,4,96,128]{3,2,1,0:T(8,128)(2,1)S(1)}, bf16[2,4,96,128]{3,2,1,0:T(8,128)(2,1)S(1)}, u32[]{:S(2)}, u32[]{:S(2)}) collective-permute-start(bf16[2,4,96,128]{3,2,1,0:T(8,128)(2,1)S(1)} %get-tuple-element.17), channel_id=1, source_target_pairs={{4,8},{8,4},{5,9},{9,5},{6,10},{10,6},{7,11},{11,7},{20,24},{24,20... | collective-permute-start | bytes 589832 | tf_op jit(solution)/shard_map/ppermute | solution.py:243
  8.5 0.1 collective-permute-start.3
  8.5 1.6 %collective-permute-start.4 = (bf16[96,128]{1,0:T(8,128)(2,1)S(1)}, bf16[96,128]{1,0:T(8,128)(2,1)S(1)}, u32[]{:S(2)}, u32[]{:S(2)}) collective-permute-start(bf16[96,128]{1,0:T(8,128)(2,1)S(1)} %get-tuple-element.19), channel_id=1, source_target_pairs={{1,2},{2,1},{3,0},{0,3},{5,6},{6,5},{7,4},{4,7},{9,10},{10,9},{11,... | collective-permute-start | bytes 73736 | tf_op jit(solution)/shard_map/ppermute | solution.py:243
  10.1 0.0 collective-permute-done.3.z0
  10.1 1.7 %collective-permute-done.4.z1 = bf16[96,128]{1,0:T(8,128)(2,1)S(1)} collective-permute-done((bf16[96,128]{1,0:T(8,128)(2,1)S(1)}, bf16[96,128]{1,0:T(8,128)(2,1)S(1)}, u32[]{:S(2)}, u32[]{:S(2)}) %collective-permute-start.4) | collective-permute-done | bytes 24608 | tf_op jit(solution)/shard_map/ppermute | solution.py:243
  11.9 0.0 collective-permute-done.x0
  11.9 0.7 %collective-permute-done.1.y0 = bf16[2,4,96,128]{3,2,1,0:T(8,128)(2,1)S(1)} collective-permute-done((bf16[2,4,96,128]{3,2,1,0:T(8,128)(2,1)S(1)}, bf16[2,4,96,128]{3,2,1,0:T(8,128)(2,1)S(1)}, u32[]{:S(2)}, u32[]{:S(2)}) %collective-permute-start.1) | collective-permute-done | bytes 196640 | tf_op jit(solution)/shard_map/ppermute | solution.py:243
  12.6 0.0 collective-permute-done.2.y1
  12.6 2.3 %panel.1 = (bf16[192,4096]{1,0:T(8,128)(2,1)S(1)}, f32[48,128]{1,0:T(8,128)S(1)}) custom-call(bf16[4,16,96,128]{3,2,1,0:T(8,128)(2,1)S(1)} %get-tuple-element.13.fields, bf16[2,4,96,128]{3,2,1,0:T(8,128)(2,1)S(1)} %collective-permute-done.x0, bf16[2,4,96,128]{3,2,1,0:T(8,128)(2,1)S(1)} %get-tuple-element.15.x1, ...), custom_call_target="tpu_custom_call" | custom-call | tf_op jit(solution)/shard_map/panel/pallas_call | solution.py:300
  14.8 0.1 collective-permute-start.5
  14.9 1.2 %collective-permute-done.5 = f32[48,128]{1,0:T(8,128)S(1)} collective-permute-done((f32[48,128]{1,0:T(8,128)S(1)}, f32[48,128]{1,0:T(8,128)S(1)}, u32[]{:S(2)}, u32[]{:S(2)}) %collective-permute-start.5) | collective-permute-done | bytes 24608 | tf_op jit(solution)/shard_map/ppermute | solution.py:252
  16.1 1.5 %collective-permute-start.6 = (f32[48,128]{1,0:T(8,128)S(1)}, f32[48,128]{1,0:T(8,128)S(1)}, u32[]{:S(2)}, u32[]{:S(2)}) collective-permute-start(f32[48,128]{1,0:T(8,128)S(1)} %add.15), channel_id=1, source_target_pairs={{0,2},{1,3},{2,0},{3,1},{4,6},{5,7},{6,4},{7,5},{8,10},{9,11},{10,... | collective-permute-start | bytes 73736 | tf_op jit(solution)/shard_map/ppermute | solution.py:252
  17.6 2.3 %collective-permute-done.6 = f32[48,128]{1,0:T(8,128)S(1)} collective-permute-done((f32[48,128]{1,0:T(8,128)S(1)}, f32[48,128]{1,0:T(8,128)S(1)}, u32[]{:S(2)}, u32[]{:S(2)}) %collective-permute-start.6) | collective-permute-done | bytes 24608 | tf_op jit(solution)/shard_map/ppermute | solution.py:252
  19.9 4.6 %collective-permute-start.7 = (f32[48,128]{1,0:T(8,128)S(1)}, f32[48,128]{1,0:T(8,128)S(1)}, u32[]{:S(2)}, u32[]{:S(2)}) collective-permute-start(f32[48,128]{1,0:T(8,128)S(1)} %add.16), channel_id=1, source_target_pairs={{0,4},{4,0},{8,12},{12,8},{1,5},{5,1},{9,13},{13,9},{2,6},{6,2},{1... | collective-permute-start | bytes 73736 | tf_op jit(solution)/shard_map/ppermute | solution.py:252
  24.5 1.8 %collective-permute-done.7 = f32[48,128]{1,0:T(8,128)S(1)} collective-permute-done((f32[48,128]{1,0:T(8,128)S(1)}, f32[48,128]{1,0:T(8,128)S(1)}, u32[]{:S(2)}, u32[]{:S(2)}) %collective-permute-start.7) | collective-permute-done | bytes 24608 | tf_op jit(solution)/shard_map/ppermute | solution.py:252
  26.3 3.2 %collective-permute-start.8 = (f32[48,128]{1,0:T(8,128)S(1)}, f32[48,128]{1,0:T(8,128)S(1)}, u32[]{:S(2)}, u32[]{:S(2)}) collective-permute-start(f32[48,128]{1,0:T(8,128)S(1)} %add.17), channel_id=1, source_target_pairs={{0,8},{4,12},{8,0},{12,4},{1,9},{5,13},{9,1},{13,5},{2,10},{6,14},... | collective-permute-start | bytes 73736 | tf_op jit(solution)/shard_map/ppermute | solution.py:252
  29.5 1.8 %collective-permute-done.8 = f32[48,128]{1,0:T(8,128)S(1)} collective-permute-done((f32[48,128]{1,0:T(8,128)S(1)}, f32[48,128]{1,0:T(8,128)S(1)}, u32[]{:S(2)}, u32[]{:S(2)}) %collective-permute-start.8) | collective-permute-done | bytes 24608 | tf_op jit(solution)/shard_map/ppermute | solution.py:252
  31.3 0.5 %collective-permute-start.9 = (f32[48,128]{1,0:T(8,128)S(1)}, f32[48,128]{1,0:T(8,128)S(1)}, u32[]{:S(2)}, u32[]{:S(2)}) collective-permute-start(f32[48,128]{1,0:T(8,128)S(1)} %add.18), channel_id=1, source_target_pairs={{0,16},{16,0},{1,17},{17,1},{2,18},{18,2},{3,19},{19,3},{4,20},{20... | collective-permute-start | bytes 73736 | tf_op jit(solution)/shard_map/ppermute | solution.py:252
  31.8 3.3 %collective-permute-done.9 = f32[48,128]{1,0:T(8,128)S(1)} collective-permute-done((f32[48,128]{1,0:T(8,128)S(1)}, f32[48,128]{1,0:T(8,128)S(1)}, u32[]{:S(2)}, u32[]{:S(2)}) %collective-permute-start.9) | collective-permute-done | bytes 24608 | tf_op jit(solution)/shard_map/ppermute | solution.py:252
  35.2 5.2 %basis.1 = (f32[96,32,128]{2,1,0:T(8,128)}, f32[96,96]{1,0:T(8,128)}) custom-call(f32[48,128]{1,0:T(8,128)S(1)} %add.19.moments, bf16[192,4096]{1,0:T(8,128)(2,1)S(1)} %get-tuple-element.21.panel), custom_call_target="tpu_custom_call" | custom-call | tf_op jit(solution)/shard_map/basis/pallas_call | solution.py:313
  (5 shorter events, 0.0 us)
Async XLA Ops:
  3.2 8.7 %collective-permute-start = (bf16[2,4,96,128]{3,2,1,0:T(8,128)(2,1)S(1)}, bf16[2,4,96,128]{3,2,1,0:T(8,128)(2,1)S(1)}, u32[]{:S(2)}, u32[]{:S(2)}) collective-permute-start(bf16[2,4,96,128]{3,2,1,0:T(8,128)(2,1)S(1)} %get-tuple-element.14), channel_id=1, source_target_pairs={{0,16},{16,0},{1,17},{17,1},{2,18},{18,2},{3,19},{19,3},{4,20},{20... | collective-permute-start | bytes 589832 | tf_op jit(solution)/shard_map/ppermute | solution.py:243
  6.2 6.4 %collective-permute-start.1 = (bf16[2,4,96,128]{3,2,1,0:T(8,128)(2,1)S(1)}, bf16[2,4,96,128]{3,2,1,0:T(8,128)(2,1)S(1)}, u32[]{:S(2)}, u32[]{:S(2)}) collective-permute-start(bf16[2,4,96,128]{3,2,1,0:T(8,128)(2,1)S(1)} %get-tuple-element.16), channel_id=1, source_target_pairs={{0,4},{4,0},{8,12},{12,8},{1,5},{5,1},{9,13},{13,9},{2,6},{6,2},{1... | collective-permute-start | bytes 589832 | tf_op jit(solution)/shard_map/ppermute | solution.py:243
  7.8 4.8 %collective-permute-start.2 = (bf16[2,4,96,128]{3,2,1,0:T(8,128)(2,1)S(1)}, bf16[2,4,96,128]{3,2,1,0:T(8,128)(2,1)S(1)}, u32[]{:S(2)}, u32[]{:S(2)}) collective-permute-start(bf16[2,4,96,128]{3,2,1,0:T(8,128)(2,1)S(1)} %get-tuple-element.17), channel_id=1, source_target_pairs={{4,8},{8,4},{5,9},{9,5},{6,10},{10,6},{7,11},{11,7},{20,24},{24,20... | collective-permute-start | bytes 589832 | tf_op jit(solution)/shard_map/ppermute | solution.py:243
  8.5 1.7 %collective-permute-start.3 = (bf16[96,128]{1,0:T(8,128)(2,1)S(1)}, bf16[96,128]{1,0:T(8,128)(2,1)S(1)}, u32[]{:S(2)}, u32[]{:S(2)}) collective-permute-start(bf16[96,128]{1,0:T(8,128)(2,1)S(1)} %get-tuple-element.18), channel_id=1, source_target_pairs={{0,1},{1,0},{2,3},{3,2},{4,5},{5,4},{6,7},{7,6},{8,9},{9,8},{10,11... | collective-permute-start | bytes 73736 | tf_op jit(solution)/shard_map/ppermute | solution.py:243
  8.5 3.3 %collective-permute-start.4 = (bf16[96,128]{1,0:T(8,128)(2,1)S(1)}, bf16[96,128]{1,0:T(8,128)(2,1)S(1)}, u32[]{:S(2)}, u32[]{:S(2)}) collective-permute-start(bf16[96,128]{1,0:T(8,128)(2,1)S(1)} %get-tuple-element.19), channel_id=1, source_target_pairs={{1,2},{2,1},{3,0},{0,3},{5,6},{6,5},{7,4},{4,7},{9,10},{10,9},{11,... | collective-permute-start | bytes 73736 | tf_op jit(solution)/shard_map/ppermute | solution.py:243
  14.8 1.3 %collective-permute-start.5 = (f32[48,128]{1,0:T(8,128)S(1)}, f32[48,128]{1,0:T(8,128)S(1)}, u32[]{:S(2)}, u32[]{:S(2)}) collective-permute-start(f32[48,128]{1,0:T(8,128)S(1)} %get-tuple-element.20), channel_id=1, source_target_pairs={{0,1},{1,0},{2,3},{3,2},{4,5},{5,4},{6,7},{7,6},{8,9},{9,8},{10,11... | collective-permute-start | bytes 73736 | tf_op jit(solution)/shard_map/ppermute | solution.py:252
  16.1 3.8 %collective-permute-start.6 = (f32[48,128]{1,0:T(8,128)S(1)}, f32[48,128]{1,0:T(8,128)S(1)}, u32[]{:S(2)}, u32[]{:S(2)}) collective-permute-start(f32[48,128]{1,0:T(8,128)S(1)} %add.15), channel_id=1, source_target_pairs={{0,2},{1,3},{2,0},{3,1},{4,6},{5,7},{6,4},{7,5},{8,10},{9,11},{10,... | collective-permute-start | bytes 73736 | tf_op jit(solution)/shard_map/ppermute | solution.py:252
  19.9 6.4 %collective-permute-start.7 = (f32[48,128]{1,0:T(8,128)S(1)}, f32[48,128]{1,0:T(8,128)S(1)}, u32[]{:S(2)}, u32[]{:S(2)}) collective-permute-start(f32[48,128]{1,0:T(8,128)S(1)} %add.16), channel_id=1, source_target_pairs={{0,4},{4,0},{8,12},{12,8},{1,5},{5,1},{9,13},{13,9},{2,6},{6,2},{1... | collective-permute-start | bytes 73736 | tf_op jit(solution)/shard_map/ppermute | solution.py:252
  26.3 5.0 %collective-permute-start.8 = (f32[48,128]{1,0:T(8,128)S(1)}, f32[48,128]{1,0:T(8,128)S(1)}, u32[]{:S(2)}, u32[]{:S(2)}) collective-permute-start(f32[48,128]{1,0:T(8,128)S(1)} %add.17), channel_id=1, source_target_pairs={{0,8},{4,12},{8,0},{12,4},{1,9},{5,13},{9,1},{13,5},{2,10},{6,14},... | collective-permute-start | bytes 73736 | tf_op jit(solution)/shard_map/ppermute | solution.py:252
  31.3 3.8 %collective-permute-start.9 = (f32[48,128]{1,0:T(8,128)S(1)}, f32[48,128]{1,0:T(8,128)S(1)}, u32[]{:S(2)}, u32[]{:S(2)}) collective-permute-start(f32[48,128]{1,0:T(8,128)S(1)} %add.18), channel_id=1, source_target_pairs={{0,16},{16,0},{1,17},{17,1},{2,18},{18,2},{3,19},{19,3},{4,20},{20... | collective-permute-start | bytes 73736 | tf_op jit(solution)/shard_map/ppermute | solution.py:252

commit v3 on v2

--- a/solution.py
+++ b/solution.py
@@ -2,6 +2,7 @@
 
 import jax
 import jax.numpy as jnp
+import numpy as np
 from jax import lax
 from jax.experimental import pallas as pl
 from jax.experimental.pallas import tpu as pltpu
@@ -14,13 +15,35 @@
 HBM = pl.BlockSpec(memory_space=pltpu.HBM)
 
 
-def pairs(count, first, periodic):
+AXES = ("gx", "gy", "gz")
+
+
+def swapped(value, axis, first, periodic=False):
+    sizes = [lax.axis_size(a) for a in AXES]
+    where = AXES.index(axis)
+    count = sizes[where]
     out = []
-    for low in range(first, count - 1, 2):
-        out += [(low, low + 1), (low + 1, low)]
-    if first and periodic:
-        out += [(count - 1, 0), (0, count - 1)]
-    return out
+    for here in np.ndindex(*sizes):
+        to = list(here)
+        to[where] += 1 if here[where] % 2 == first else -1
+        if periodic:
+            to[where] %= count
+        if not 0 <= to[where] < count:
+            to = [here[0], here[1], here[2] ^ 1]
+        out.append((int(np.ravel_multi_index(here, sizes)), int(np.ravel_multi_index(to, sizes))))
+    return lax.ppermute(value, AXES, out)
+
+
+def summed(value, mate):
+    count = int(np.prod([lax.axis_size(a) for a in AXES]))
+    if count & (count - 1):
+        return lax.psum(value, AXES)
+    steps = [mate] + [
+        1 << k | mate for k in range(count.bit_length() - 1) if 1 << k != mate
+    ]
+    for step in steps:
+        value = value + lax.ppermute(value, AXES, [(i, i ^ step) for i in range(count)])
+    return value
 
 
 def lane_index(rows):
@@ -239,26 +262,11 @@
         copy.wait()
 
 
-def swap(value, axis, first, periodic=False):
-    return lax.ppermute(value, axis, pairs(lax.axis_size(axis), first, periodic))
-
-
-def total_over(value, axis):
-    count = lax.axis_size(axis)
-    if count & (count - 1):
-        return lax.psum(value, axis)
-    step = 1
-    while step < count:
-        value = value + lax.ppermute(value, axis, [(i, i ^ step) for i in range(count)])
-        step *= 2
-    return value
-
-
-def per_device(vel_u, vel_v, vel_w, density):
+def per_device(mate, vel_u, vel_v, vel_w, density):
     snaps, nx, ny, nz = vel_u.shape
     cells = nx * ny
     dims = (snaps, nx, ny)
-    sizes = tuple(lax.axis_size(a) for a in ("gx", "gy", "gz"))
+    sizes = tuple(lax.axis_size(a) for a in AXES)
     flat = [
         pltpu.with_memory_space_constraint(a.reshape(snaps * cells, nz), pltpu.HBM)
         for a in (vel_u, vel_v, vel_w, density)
@@ -288,14 +296,14 @@
         compiler_params=params,
         name="pack",
     )(*flat)
-    x0 = swap(x0, "gx", 0)
-    y0 = swap(y0, "gy", 0)
+    x0 = swapped(x0, "gx", 0)
+    y0 = swapped(y0, "gy", 0)
     if sizes[1] > 2:
-        y1 = swap(y1, "gy", 1)
-    z0 = swap(z0, "gz", 0)
-    z1 = swap(z1, "gz", 1, True)
+        y1 = swapped(y1, "gy", 1)
+    z0 = swapped(z0, "gz", 0)
+    z1 = swapped(z1, "gz", 1, True)
     if sizes[0] > 2:
-        x1 = swap(x1, "gx", 1)
+        x1 = swapped(x1, "gx", 1)
     scale = 1.0 / (2 * cells * nz * sizes[0] * sizes[1] * sizes[2])
     panel, moments = pl.pallas_call(
         functools.partial(panel_kernel, dims, scale, sizes),
@@ -308,8 +316,7 @@
         compiler_params=params,
         name="panel",
     )(fields, x0, x1, y0, y1, z0, z1)
-    for axis in ("gz", "gy", "gx"):
-        moments = total_over(moments, axis)
+    moments = summed(moments, mate)
     basis, factor = pl.pallas_call(
         functools.partial(basis_kernel, dims),
         out_shape=(
@@ -330,10 +337,17 @@
     return basis.reshape(snaps, 2, nx, ny, nz), factor
 
 
+def chip_mate(mesh):
+    devices = list(mesh.devices.flat)
+    at = [getattr(d, "coords", None) for d in devices]
+    near = [k for k in range(1, len(at)) if at[0] is not None and at[k] == at[0]]
+    return near[0] if near and near[0] & (near[0] - 1) == 0 else 1
+
+
 def solution(mesh):
     spec = P(None, "gx", "gy", "gz")
     return jax.shard_map(
-        per_device,
+        functools.partial(per_device, chip_mate(mesh)),
         mesh=mesh,
         in_specs=(spec,) * 4,
         out_specs=(P(None, None, "gx", "gy", "gz"), P()),

time: 40.5 us -> 36.4 us (0.90)
  starting transfers between devices: 16.8 us -> 13.4 us
  waiting for transfers between devices: 12.9 us -> 12.2 us
    ppermute x10, starting transfers between devices: 16.8 us -> 13.4 us  [the longest x5 7.15 us: summed(): lax.ppermute(value, AXES, [(i, i ^ step) for i in range(count)])]
    ppermute x10, waiting for transfers between devices: 12.9 us -> 12.2 us  [the longest x5 9.02 us: summed(): lax.ppermute(value, AXES, [(i, i ^ step) for i in range(count)])]
where the time goes in v3:
time: 36.4 us; the launch traced here: 36.3 us
  starting transfers between devices  13.4 us (37%)
  waiting for transfers between devices  12.2 us (34%)
  Pallas kernels  10 us (27%)
  between operations  0.66 us (2%)
    ppermute x5, waiting for transfers between devices, summed(): lax.ppermute(value, AXES, [(i, i ^ step) for i in range(count)])  9.02 us
    ppermute x5, starting transfers between devices, summed(): lax.ppermute(value, AXES, [(i, i ^ step) for i in range(count)])  7.15 us
    ppermute x5, starting transfers between devices, swapped(): return lax.ppermute(value, AXES, out)  6.22 us
    pallas_call x1, Pallas kernels, per_device(): pl.pallas_call(functools.partial(basis_kernel, dims), out_shape=(jax.Shap...  5.21 us
    ppermute x5, waiting for transfers between devices, swapped(): return lax.ppermute(value, AXES, out)  3.18 us
    pallas_call x1, Pallas kernels, per_device(): pl.pallas_call(functools.partial(pack_kernel, dims), out_shape=(jax.Shape...  2.54 us
    pallas_call x1, Pallas kernels, per_device(): pl.pallas_call(functools.partial(panel_kernel, dims, scale, sizes), out_s...  2.27 us
  transfers between devices with their start and end apart: 10, of which 7 were waited for; matrix products, arithmetic and copies ran while one was open for 0% of the time, Pallas kernels for 0%

profile of v3, /device:TPU:0, one launch (start us, length us, event | category | flops | bytes accessed | tf_op | source)
XLA Modules:
  0.0 36.3 jit_solution(1526811863437876360)
XLA Ops:
  0.6 2.5 %pack.1 = (bf16[4,16,96,128]{3,2,1,0:T(8,128)(2,1)S(1)}, bf16[2,4,96,128]{3,2,1,0:T(8,128)(2,1)S(1)}, bf16[2,4,96,128]{3,2,1,0:T(8,128)(2,1)S(1)}, bf16[2,4,96,1...) custom-call(bf16[1536,128]{1,0:T(8,128)(2,1)} %bitcast.5, ...), custom_call_target="tpu_custom_call" | custom-call | tf_op jit(solution)/shard_map/pack/pallas_call | solution.py:278
  3.2 3.0 %collective-permute-start = (bf16[2,4,96,128]{3,2,1,0:T(8,128)(2,1)S(1)}, bf16[2,4,96,128]{3,2,1,0:T(8,128)(2,1)S(1)}, u32[]{:S(2)}, u32[]{:S(2)}) collective-permute-start(bf16[2,4,96,128]{3,2,1,0:T(8,128)(2,1)S(1)} %get-tuple-element.14), channel_id=1, source_target_pairs={{0,16},{1,17},{2,18},{3,19},{4,20},{5,21},{6,22},{7,23},{8,24},{9,... | collective-permute-start | bytes 589832 | tf_op jit(solution)/shard_map/ppermute | solution.py:34
  6.2 1.6 %collective-permute-start.1 = (bf16[2,4,96,128]{3,2,1,0:T(8,128)(2,1)S(1)}, bf16[2,4,96,128]{3,2,1,0:T(8,128)(2,1)S(1)}, u32[]{:S(2)}, u32[]{:S(2)}) collective-permute-start(bf16[2,4,96,128]{3,2,1,0:T(8,128)(2,1)S(1)} %get-tuple-element.16), channel_id=1, source_target_pairs={{0,4},{1,5},{2,6},{3,7},{4,0},{5,1},{6,2},{7,3},{8,12},{9,13},{10,... | collective-permute-start | bytes 589832 | tf_op jit(solution)/shard_map/ppermute | solution.py:34
  7.8 0.0 collective-permute-start.2
  7.8 0.5 %collective-permute-start.3 = (bf16[96,128]{1,0:T(8,128)(2,1)S(1)}, bf16[96,128]{1,0:T(8,128)(2,1)S(1)}, u32[]{:S(2)}, u32[]{:S(2)}) collective-permute-start(bf16[96,128]{1,0:T(8,128)(2,1)S(1)} %get-tuple-element.18), channel_id=1, source_target_pairs={{0,1},{1,0},{2,3},{3,2},{4,5},{5,4},{6,7},{7,6},{8,9},{9,8},{10,11... | collective-permute-start | bytes 73736 | tf_op jit(solution)/shard_map/ppermute | solution.py:34
  8.3 1.1 %collective-permute-start.4 = (bf16[96,128]{1,0:T(8,128)(2,1)S(1)}, bf16[96,128]{1,0:T(8,128)(2,1)S(1)}, u32[]{:S(2)}, u32[]{:S(2)}) collective-permute-start(bf16[96,128]{1,0:T(8,128)(2,1)S(1)} %get-tuple-element.19), channel_id=1, source_target_pairs={{0,3},{1,2},{2,1},{3,0},{4,7},{5,6},{6,5},{7,4},{8,11},{9,10},{10,... | collective-permute-start | bytes 73736 | tf_op jit(solution)/shard_map/ppermute | solution.py:34
  9.4 0.0 collective-permute-done.3.z0
  9.4 2.2 %collective-permute-done.4.z1 = bf16[96,128]{1,0:T(8,128)(2,1)S(1)} collective-permute-done((bf16[96,128]{1,0:T(8,128)(2,1)S(1)}, bf16[96,128]{1,0:T(8,128)(2,1)S(1)}, u32[]{:S(2)}, u32[]{:S(2)}) %collective-permute-start.4) | collective-permute-done | bytes 24608 | tf_op jit(solution)/shard_map/ppermute | solution.py:34
  11.6 0.0 collective-permute-done.x0
  11.6 0.9 %collective-permute-done.1.y0 = bf16[2,4,96,128]{3,2,1,0:T(8,128)(2,1)S(1)} collective-permute-done((bf16[2,4,96,128]{3,2,1,0:T(8,128)(2,1)S(1)}, bf16[2,4,96,128]{3,2,1,0:T(8,128)(2,1)S(1)}, u32[]{:S(2)}, u32[]{:S(2)}) %collective-permute-start.1) | collective-permute-done | bytes 196640 | tf_op jit(solution)/shard_map/ppermute | solution.py:34
  12.6 0.0 collective-permute-done.2.y1
  12.6 2.3 %panel.1 = (bf16[192,4096]{1,0:T(8,128)(2,1)S(1)}, f32[48,128]{1,0:T(8,128)S(1)}) custom-call(bf16[4,16,96,128]{3,2,1,0:T(8,128)(2,1)S(1)} %get-tuple-element.13.fields, bf16[2,4,96,128]{3,2,1,0:T(8,128)(2,1)S(1)} %collective-permute-done.x0, bf16[2,4,96,128]{3,2,1,0:T(8,128)(2,1)S(1)} %get-tuple-element.15.x1, ...), custom_call_target="tpu_custom_call" | custom-call | tf_op jit(solution)/shard_map/panel/pallas_call | solution.py:308
  14.8 0.1 collective-permute-start.5
  14.9 1.2 %collective-permute-done.5 = f32[48,128]{1,0:T(8,128)S(1)} collective-permute-done((f32[48,128]{1,0:T(8,128)S(1)}, f32[48,128]{1,0:T(8,128)S(1)}, u32[]{:S(2)}, u32[]{:S(2)}) %collective-permute-start.5) | collective-permute-done | bytes 24608 | tf_op jit(solution)/shard_map/ppermute | solution.py:45
  16.1 1.3 %collective-permute-start.6 = (f32[48,128]{1,0:T(8,128)S(1)}, f32[48,128]{1,0:T(8,128)S(1)}, u32[]{:S(2)}, u32[]{:S(2)}) collective-permute-start(f32[48,128]{1,0:T(8,128)S(1)} %add.15), channel_id=1, source_target_pairs={{0,3},{1,2},{2,1},{3,0},{4,7},{5,6},{6,5},{7,4},{8,11},{9,10},{10,... | collective-permute-start | bytes 73736 | tf_op jit(solution)/shard_map/ppermute | solution.py:45
  17.4 2.0 %collective-permute-done.6 = f32[48,128]{1,0:T(8,128)S(1)} collective-permute-done((f32[48,128]{1,0:T(8,128)S(1)}, f32[48,128]{1,0:T(8,128)S(1)}, u32[]{:S(2)}, u32[]{:S(2)}) %collective-permute-start.6) | collective-permute-done | bytes 24608 | tf_op jit(solution)/shard_map/ppermute | solution.py:45
  19.4 2.5 %collective-permute-start.7 = (f32[48,128]{1,0:T(8,128)S(1)}, f32[48,128]{1,0:T(8,128)S(1)}, u32[]{:S(2)}, u32[]{:S(2)}) collective-permute-start(f32[48,128]{1,0:T(8,128)S(1)} %add.16), channel_id=1, source_target_pairs={{0,5},{1,4},{2,7},{3,6},{4,1},{5,0},{6,3},{7,2},{8,13},{9,12},{10,... | collective-permute-start | bytes 73736 | tf_op jit(solution)/shard_map/ppermute | solution.py:45
  21.8 1.5 %collective-permute-done.7 = f32[48,128]{1,0:T(8,128)S(1)} collective-permute-done((f32[48,128]{1,0:T(8,128)S(1)}, f32[48,128]{1,0:T(8,128)S(1)}, u32[]{:S(2)}, u32[]{:S(2)}) %collective-permute-start.7) | collective-permute-done | bytes 24608 | tf_op jit(solution)/shard_map/ppermute | solution.py:45
  23.4 2.9 %collective-permute-start.8 = (f32[48,128]{1,0:T(8,128)S(1)}, f32[48,128]{1,0:T(8,128)S(1)}, u32[]{:S(2)}, u32[]{:S(2)}) collective-permute-start(f32[48,128]{1,0:T(8,128)S(1)} %add.17), channel_id=1, source_target_pairs={{0,9},{1,8},{2,11},{3,10},{4,13},{5,12},{6,15},{7,14},{8,1},{9,0},... | collective-permute-start | bytes 73736 | tf_op jit(solution)/shard_map/ppermute | solution.py:45
  26.3 1.5 %collective-permute-done.8 = f32[48,128]{1,0:T(8,128)S(1)} collective-permute-done((f32[48,128]{1,0:T(8,128)S(1)}, f32[48,128]{1,0:T(8,128)S(1)}, u32[]{:S(2)}, u32[]{:S(2)}) %collective-permute-start.8) | collective-permute-done | bytes 24608 | tf_op jit(solution)/shard_map/ppermute | solution.py:45
  27.8 0.4 %collective-permute-start.9 = (f32[48,128]{1,0:T(8,128)S(1)}, f32[48,128]{1,0:T(8,128)S(1)}, u32[]{:S(2)}, u32[]{:S(2)}) collective-permute-start(f32[48,128]{1,0:T(8,128)S(1)} %add.18), channel_id=1, source_target_pairs={{0,17},{1,16},{2,19},{3,18},{4,21},{5,20},{6,23},{7,22},{8,25},{9,... | collective-permute-start | bytes 73736 | tf_op jit(solution)/shard_map/ppermute | solution.py:45
  28.2 2.8 %collective-permute-done.9 = f32[48,128]{1,0:T(8,128)S(1)} collective-permute-done((f32[48,128]{1,0:T(8,128)S(1)}, f32[48,128]{1,0:T(8,128)S(1)}, u32[]{:S(2)}, u32[]{:S(2)}) %collective-permute-start.9) | collective-permute-done | bytes 24608 | tf_op jit(solution)/shard_map/ppermute | solution.py:45
  31.0 5.2 %basis.1 = (f32[96,32,128]{2,1,0:T(8,128)}, f32[96,96]{1,0:T(8,128)}) custom-call(f32[48,128]{1,0:T(8,128)S(1)} %add.19.moments, bf16[192,4096]{1,0:T(8,128)(2,1)S(1)} %get-tuple-element.21.panel), custom_call_target="tpu_custom_call" | custom-call | tf_op jit(solution)/shard_map/basis/pallas_call | solution.py:320
  (5 shorter events, 0.0 us)
Async XLA Ops:
  3.2 8.5 %collective-permute-start = (bf16[2,4,96,128]{3,2,1,0:T(8,128)(2,1)S(1)}, bf16[2,4,96,128]{3,2,1,0:T(8,128)(2,1)S(1)}, u32[]{:S(2)}, u32[]{:S(2)}) collective-permute-start(bf16[2,4,96,128]{3,2,1,0:T(8,128)(2,1)S(1)} %get-tuple-element.14), channel_id=1, source_target_pairs={{0,16},{1,17},{2,18},{3,19},{4,20},{5,21},{6,22},{7,23},{8,24},{9,... | collective-permute-start | bytes 589832 | tf_op jit(solution)/shard_map/ppermute | solution.py:34
  6.2 6.4 %collective-permute-start.1 = (bf16[2,4,96,128]{3,2,1,0:T(8,128)(2,1)S(1)}, bf16[2,4,96,128]{3,2,1,0:T(8,128)(2,1)S(1)}, u32[]{:S(2)}, u32[]{:S(2)}) collective-permute-start(bf16[2,4,96,128]{3,2,1,0:T(8,128)(2,1)S(1)} %get-tuple-element.16), channel_id=1, source_target_pairs={{0,4},{1,5},{2,6},{3,7},{4,0},{5,1},{6,2},{7,3},{8,12},{9,13},{10,... | collective-permute-start | bytes 589832 | tf_op jit(solution)/shard_map/ppermute | solution.py:34
  7.8 4.8 %collective-permute-start.2 = (bf16[2,4,96,128]{3,2,1,0:T(8,128)(2,1)S(1)}, bf16[2,4,96,128]{3,2,1,0:T(8,128)(2,1)S(1)}, u32[]{:S(2)}, u32[]{:S(2)}) collective-permute-start(bf16[2,4,96,128]{3,2,1,0:T(8,128)(2,1)S(1)} %get-tuple-element.17), channel_id=1, source_target_pairs={{0,1},{1,0},{2,3},{3,2},{4,8},{5,9},{6,10},{7,11},{8,4},{9,5},{10,... | collective-permute-start | bytes 589832 | tf_op jit(solution)/shard_map/ppermute | solution.py:34
  7.8 1.6 %collective-permute-start.3 = (bf16[96,128]{1,0:T(8,128)(2,1)S(1)}, bf16[96,128]{1,0:T(8,128)(2,1)S(1)}, u32[]{:S(2)}, u32[]{:S(2)}) collective-permute-start(bf16[96,128]{1,0:T(8,128)(2,1)S(1)} %get-tuple-element.18), channel_id=1, source_target_pairs={{0,1},{1,0},{2,3},{3,2},{4,5},{5,4},{6,7},{7,6},{8,9},{9,8},{10,11... | collective-permute-start | bytes 73736 | tf_op jit(solution)/shard_map/ppermute | solution.py:34
  8.3 3.3 %collective-permute-start.4 = (bf16[96,128]{1,0:T(8,128)(2,1)S(1)}, bf16[96,128]{1,0:T(8,128)(2,1)S(1)}, u32[]{:S(2)}, u32[]{:S(2)}) collective-permute-start(bf16[96,128]{1,0:T(8,128)(2,1)S(1)} %get-tuple-element.19), channel_id=1, source_target_pairs={{0,3},{1,2},{2,1},{3,0},{4,7},{5,6},{6,5},{7,4},{8,11},{9,10},{10,... | collective-permute-start | bytes 73736 | tf_op jit(solution)/shard_map/ppermute | solution.py:34
  14.8 1.3 %collective-permute-start.5 = (f32[48,128]{1,0:T(8,128)S(1)}, f32[48,128]{1,0:T(8,128)S(1)}, u32[]{:S(2)}, u32[]{:S(2)}) collective-permute-start(f32[48,128]{1,0:T(8,128)S(1)} %get-tuple-element.20), channel_id=1, source_target_pairs={{0,1},{1,0},{2,3},{3,2},{4,5},{5,4},{6,7},{7,6},{8,9},{9,8},{10,11... | collective-permute-start | bytes 73736 | tf_op jit(solution)/shard_map/ppermute | solution.py:45
  16.1 3.3 %collective-permute-start.6 = (f32[48,128]{1,0:T(8,128)S(1)}, f32[48,128]{1,0:T(8,128)S(1)}, u32[]{:S(2)}, u32[]{:S(2)}) collective-permute-start(f32[48,128]{1,0:T(8,128)S(1)} %add.15), channel_id=1, source_target_pairs={{0,3},{1,2},{2,1},{3,0},{4,7},{5,6},{6,5},{7,4},{8,11},{9,10},{10,... | collective-permute-start | bytes 73736 | tf_op jit(solution)/shard_map/ppermute | solution.py:45
  19.4 4.0 %collective-permute-start.7 = (f32[48,128]{1,0:T(8,128)S(1)}, f32[48,128]{1,0:T(8,128)S(1)}, u32[]{:S(2)}, u32[]{:S(2)}) collective-permute-start(f32[48,128]{1,0:T(8,128)S(1)} %add.16), channel_id=1, source_target_pairs={{0,5},{1,4},{2,7},{3,6},{4,1},{5,0},{6,3},{7,2},{8,13},{9,12},{10,... | collective-permute-start | bytes 73736 | tf_op jit(solution)/shard_map/ppermute | solution.py:45
  23.4 4.4 %collective-permute-start.8 = (f32[48,128]{1,0:T(8,128)S(1)}, f32[48,128]{1,0:T(8,128)S(1)}, u32[]{:S(2)}, u32[]{:S(2)}) collective-permute-start(f32[48,128]{1,0:T(8,128)S(1)} %add.17), channel_id=1, source_target_pairs={{0,9},{1,8},{2,11},{3,10},{4,13},{5,12},{6,15},{7,14},{8,1},{9,0},... | collective-permute-start | bytes 73736 | tf_op jit(solution)/shard_map/ppermute | solution.py:45
  27.8 3.3 %collective-permute-start.9 = (f32[48,128]{1,0:T(8,128)S(1)}, f32[48,128]{1,0:T(8,128)S(1)}, u32[]{:S(2)}, u32[]{:S(2)}) collective-permute-start(f32[48,128]{1,0:T(8,128)S(1)} %add.18), channel_id=1, source_target_pairs={{0,17},{1,16},{2,19},{3,18},{4,21},{5,20},{6,23},{7,22},{8,25},{9,... | collective-permute-start | bytes 73736 | tf_op jit(solution)/shard_map/ppermute | solution.py:45

commit v4 on v3

--- a/solution.py
+++ b/solution.py
@@ -11,6 +11,7 @@
 F32 = jnp.float32
 BF16 = jnp.bfloat16
 LANES = 128
+CUTS = (0, 64)
 VMEM = pl.BlockSpec(memory_space=pltpu.VMEM)
 HBM = pl.BlockSpec(memory_space=pltpu.HBM)
 
@@ -188,76 +189,112 @@
     moments[...] = fold(total)
 
 
-def basis_kernel(dims, moments, panel, basis, factor, work, inverse, ready, sent):
+def basis_kernel(
+    dims, moments, panel, basis, factor, work, inverse, upper, columns, held, ready, sent
+):
     snaps, nx, ny = dims
     cells = 2 * nx * ny
+    copies = []
+
+    def emit(first, final):
+        count = final - first
+        exact = inverse[first:final, 0:snaps]
+        high = exact.astype(BF16)
+        rest = (exact - high.astype(F32)).astype(BF16)
+        left = jnp.concatenate(
+            [
+                jnp.concatenate([high, high], axis=1),
+                jnp.concatenate([rest, jnp.zeros_like(rest)], axis=1),
+            ],
+            axis=0,
+        )
+        for c in range(0, cells, 2):
+            both = jnp.dot(left, panel[:, c * LANES : (c + 2) * LANES], preferred_element_type=F32)
+            out = both[0:count] + both[count : 2 * count]
+            for i in range(2):
+                ready[pl.ds(first * cells + c + i, count, stride=cells), :] = out[
+                    :, i * LANES : (i + 1) * LANES
+                ]
+        part = pl.ds(first * cells, count * cells)
+        copies.append(
+            pltpu.make_async_copy(ready.at[part], basis.at[part], sent.at[len(copies)])
+        )
+        copies[-1].start()
+
     lane = lane_index(8)
     sub = lax.broadcasted_iota(jnp.int32, (8, LANES), 0)
     groups = snaps // 8
     unfold(moments[...], work)
 
     def spread(value, j):
-        return jnp.broadcast_to(value[:, j : j + 1], (8, LANES))
-
+        return jnp.take_along_axis(value, jnp.full((8, LANES), j, jnp.int32), axis=1)
+
+    def column_set(base):
+        block = work[base : base + 8, :]
+        return block, [spread(block, base + i) for i in range(8)]
+
+    def repeat(base, block, cols):
+        work[base : base + 8, :] = block
+        for i in range(8):
+            columns[8 * (base + i) : 8 * (base + i) + 8, :] = cols[i]
+        corner = [
+            [columns[pl.ds(8 * (base + i) + j, 8, stride=0), :] for j in range(i + 1)]
+            for i in range(8)
+        ]
+        return [work[pl.ds(base + i, 8, stride=0), :] for i in range(8)], corner
+
+    rows, small = repeat(0, *column_set(0))
     for g in range(groups):
         base = 8 * g
-        rows = [jnp.broadcast_to(work[base + i : base + i + 1, :], (8, LANES)) for i in range(8)]
-        small = [[spread(rows[j], base + i) for j in range(i + 1)] for i in range(8)]
-        ratio = []
+        inside = (lane >= base) & (lane < base + 8)
+        last = g + 1 == groups
+        if not last:
+            block, cols = column_set(base + 8)
+            block = jnp.where(inside, 0.0, block)
+        outer = []
+        done = jnp.zeros((8, LANES), F32)
+        roots = jnp.zeros((8, LANES), F32)
         for j in range(8):
             here = base + j
             root = lax.rsqrt(small[j][j])
             inv = root * root
-            ratio.append(inv)
             pivot = jnp.where(lane == here, 1.0, rows[j])
             for i in range(j + 1, 8):
                 m = small[i][j] * inv
                 rows[i] = jnp.where(lane == here, 0.0, rows[i]) - m * pivot
                 for k in range(j + 1, i + 1):
                     small[i][k] = small[i][k] - m * small[k][j]
-            scaled = rows[j] * root
-            factor[here : here + 1, :] = jnp.where(lane >= here, scaled, 0.0)[0:1, 0:snaps]
-            inverse[here : here + 1, :] = jnp.where(
-                lane < here, scaled, jnp.where(lane == here, root, 0.0)
-            )[0:1, :]
-        outer = []
-        for j in range(8):
-            here = base + j
-            clean = jnp.where((lane > here) & (lane < base + 8), 0.0, rows[j])
-            outer.append(jnp.where(lane == here, 1.0, clean))
-        inside = (lane >= base) & (lane < base + 8)
-        for h in range(g + 1, groups):
+            done = jnp.where(sub == j, rows[j] * root, done)
+            roots = jnp.where(sub == j, root, roots)
+            if last:
+                continue
+            clean = jnp.where((lane > here) & (lane < base + 8), 0.0, pivot) * inv
+            outer.append(clean)
+            m = jnp.take_along_axis(rows[j], sub + base + 8, axis=1)
+            held[8 * here : 8 * here + 8, :] = m
+            block = block - m * clean
+            m = m * inv
+            for i in range(8):
+                cols[i] = cols[i] - m * held[pl.ds(8 * here + i, 8, stride=0), :]
+        upper[base : base + 8, :] = jnp.where(lane >= sub + base, done, 0.0)[:, 0:snaps]
+        inverse[base : base + 8, :] = jnp.where(
+            lane < sub + base, done, jnp.where(lane == sub + base, roots, 0.0)
+        )
+        if last:
+            break
+        if base + 8 in CUTS:
+            emit(CUTS[CUTS.index(base + 8) - 1], base + 8)
+        rows_next, small = repeat(base + 8, block, cols)
+        for h in range(g + 2, groups):
             block = jnp.where(inside, 0.0, work[8 * h : 8 * h + 8, :])
             for j in range(8):
-                m = jnp.take_along_axis(rows[j] * ratio[j], sub + 8 * h, axis=1)
+                m = jnp.take_along_axis(rows[j], sub + 8 * h, axis=1)
                 block = block - m * outer[j]
             work[8 * h : 8 * h + 8, :] = block
-
-    low_inv = inverse[:, 0:snaps]
-    high = low_inv.astype(BF16)
-    rest = (low_inv - high.astype(F32)).astype(BF16)
-    left = jnp.concatenate(
-        [
-            jnp.concatenate([high, high], axis=1),
-            jnp.concatenate([rest, jnp.zeros_like(rest)], axis=1),
-        ],
-        axis=0,
-    )
-    copies = []
-    for k in range(cells // 8):
-        for c in range(8 * k, 8 * k + 8, 2):
-            both = jnp.dot(
-                left, panel[:, c * LANES : (c + 2) * LANES], preferred_element_type=F32
-            )
-            out = both[0:snaps] + both[snaps : 2 * snaps]
-            for i in range(2):
-                ready[k, pl.ds(c % 8 + i, snaps, stride=8), :] = out[:, i * LANES : (i + 1) * LANES]
-        copies.append(
-            pltpu.make_async_copy(
-                ready.at[k].reshape(snaps, 8, LANES), basis.at[:, 8 * k : 8 * k + 8, :], sent.at[k]
-            )
-        )
-        copies[-1].start()
+        rows = rows_next
+    copies.append(pltpu.make_async_copy(upper, factor, sent.at[len(copies)]))
+    copies[-1].start()
+    emit(CUTS[-1], snaps)
     for copy in copies:
         copy.wait()
 
@@ -320,16 +357,19 @@
     basis, factor = pl.pallas_call(
         functools.partial(basis_kernel, dims),
         out_shape=(
-            jax.ShapeDtypeStruct((snaps, 2 * cells, nz), F32),
+            jax.ShapeDtypeStruct((snaps * 2 * cells, nz), F32),
             jax.ShapeDtypeStruct((snaps, snaps), F32),
         ),
         in_specs=[VMEM] * 2,
-        out_specs=[HBM, VMEM],
+        out_specs=[HBM, HBM],
         scratch_shapes=[
             pltpu.VMEM((snaps, LANES), F32),
             pltpu.VMEM((snaps, LANES), F32),
-            pltpu.VMEM((cells // 4, snaps * 8, nz), F32),
-            pltpu.SemaphoreType.DMA((cells // 4,)),
+            pltpu.VMEM((snaps, snaps), F32),
+            pltpu.VMEM((8 * snaps, LANES), F32),
+            pltpu.VMEM((8 * snaps, LANES), F32),
+            pltpu.VMEM((snaps * 2 * cells, nz), F32),
+            pltpu.SemaphoreType.DMA((len(CUTS) + 1,)),
         ],
         compiler_params=params,
         name="basis",

time: 36.4 us -> 35 us (0.962)
  Pallas kernels: 10 us -> 8.61 us
    pallas_call x1, Pallas kernels: 5.21 us -> 3.81 us  [per_device(): pl.pallas_call(functools.partial(basis_kernel, dims), out_shape=(jax.Shap...]
where the time goes in v4:
time: 35 us; the launch traced here: 34.9 us
  starting transfers between devices  13.4 us (38%)
  waiting for transfers between devices  12.2 us (35%)
  Pallas kernels  8.61 us (25%)
  between operations  0.66 us (2%)
    ppermute x5, waiting for transfers between devices, summed(): lax.ppermute(value, AXES, [(i, i ^ step) for i in range(count)])  9.02 us
    ppermute x5, starting transfers between devices, summed(): lax.ppermute(value, AXES, [(i, i ^ step) for i in range(count)])  7.15 us
    ppermute x5, starting transfers between devices, swapped(): return lax.ppermute(value, AXES, out)  6.22 us
    pallas_call x1, Pallas kernels, per_device(): pl.pallas_call(functools.partial(basis_kernel, dims), out_shape=(jax.Shap...  3.81 us
    ppermute x5, waiting for transfers between devices, swapped(): return lax.ppermute(value, AXES, out)  3.18 us
    pallas_call x1, Pallas kernels, per_device(): pl.pallas_call(functools.partial(pack_kernel, dims), out_shape=(jax.Shape...  2.54 us
    pallas_call x1, Pallas kernels, per_device(): pl.pallas_call(functools.partial(panel_kernel, dims, scale, sizes), out_s...  2.27 us
  transfers between devices with their start and end apart: 10, of which 7 were waited for; matrix products, arithmetic and copies ran while one was open for 0% of the time, Pallas kernels for 0%

profile of v4, /device:TPU:0, one launch (start us, length us, event | category | flops | bytes accessed | tf_op | source)
XLA Modules:
  0.0 34.9 jit_solution(4227956435018608346)
XLA Ops:
  0.6 2.5 %pack.1 = (bf16[4,16,96,128]{3,2,1,0:T(8,128)(2,1)S(1)}, bf16[2,4,96,128]{3,2,1,0:T(8,128)(2,1)S(1)}, bf16[2,4,96,128]{3,2,1,0:T(8,128)(2,1)S(1)}, bf16[2,4,96,1...) custom-call(bf16[1536,128]{1,0:T(8,128)(2,1)} %bitcast.5, ...), custom_call_target="tpu_custom_call" | custom-call | tf_op jit(solution)/shard_map/pack/pallas_call | solution.py:315
  3.2 3.0 %collective-permute-start = (bf16[2,4,96,128]{3,2,1,0:T(8,128)(2,1)S(1)}, bf16[2,4,96,128]{3,2,1,0:T(8,128)(2,1)S(1)}, u32[]{:S(2)}, u32[]{:S(2)}) collective-permute-start(bf16[2,4,96,128]{3,2,1,0:T(8,128)(2,1)S(1)} %get-tuple-element.14), channel_id=1, source_target_pairs={{0,16},{1,17},{2,18},{3,19},{4,20},{5,21},{6,22},{7,23},{8,24},{9,... | collective-permute-start | bytes 589832 | tf_op jit(solution)/shard_map/ppermute | solution.py:35
  6.2 1.6 %collective-permute-start.1 = (bf16[2,4,96,128]{3,2,1,0:T(8,128)(2,1)S(1)}, bf16[2,4,96,128]{3,2,1,0:T(8,128)(2,1)S(1)}, u32[]{:S(2)}, u32[]{:S(2)}) collective-permute-start(bf16[2,4,96,128]{3,2,1,0:T(8,128)(2,1)S(1)} %get-tuple-element.16), channel_id=1, source_target_pairs={{0,4},{1,5},{2,6},{3,7},{4,0},{5,1},{6,2},{7,3},{8,12},{9,13},{10,... | collective-permute-start | bytes 589832 | tf_op jit(solution)/shard_map/ppermute | solution.py:35
  7.8 0.0 collective-permute-start.2
  7.8 0.5 %collective-permute-start.3 = (bf16[96,128]{1,0:T(8,128)(2,1)S(1)}, bf16[96,128]{1,0:T(8,128)(2,1)S(1)}, u32[]{:S(2)}, u32[]{:S(2)}) collective-permute-start(bf16[96,128]{1,0:T(8,128)(2,1)S(1)} %get-tuple-element.18), channel_id=1, source_target_pairs={{0,1},{1,0},{2,3},{3,2},{4,5},{5,4},{6,7},{7,6},{8,9},{9,8},{10,11... | collective-permute-start | bytes 73736 | tf_op jit(solution)/shard_map/ppermute | solution.py:35
  8.3 1.1 %collective-permute-start.4 = (bf16[96,128]{1,0:T(8,128)(2,1)S(1)}, bf16[96,128]{1,0:T(8,128)(2,1)S(1)}, u32[]{:S(2)}, u32[]{:S(2)}) collective-permute-start(bf16[96,128]{1,0:T(8,128)(2,1)S(1)} %get-tuple-element.19), channel_id=1, source_target_pairs={{0,3},{1,2},{2,1},{3,0},{4,7},{5,6},{6,5},{7,4},{8,11},{9,10},{10,... | collective-permute-start | bytes 73736 | tf_op jit(solution)/shard_map/ppermute | solution.py:35
  9.4 0.0 collective-permute-done.3.z0
  9.4 2.2 %collective-permute-done.4.z1 = bf16[96,128]{1,0:T(8,128)(2,1)S(1)} collective-permute-done((bf16[96,128]{1,0:T(8,128)(2,1)S(1)}, bf16[96,128]{1,0:T(8,128)(2,1)S(1)}, u32[]{:S(2)}, u32[]{:S(2)}) %collective-permute-start.4) | collective-permute-done | bytes 24608 | tf_op jit(solution)/shard_map/ppermute | solution.py:35
  11.6 0.0 collective-permute-done.x0
  11.6 0.9 %collective-permute-done.1.y0 = bf16[2,4,96,128]{3,2,1,0:T(8,128)(2,1)S(1)} collective-permute-done((bf16[2,4,96,128]{3,2,1,0:T(8,128)(2,1)S(1)}, bf16[2,4,96,128]{3,2,1,0:T(8,128)(2,1)S(1)}, u32[]{:S(2)}, u32[]{:S(2)}) %collective-permute-start.1) | collective-permute-done | bytes 196640 | tf_op jit(solution)/shard_map/ppermute | solution.py:35
  12.6 0.0 collective-permute-done.2.y1
  12.6 2.3 %panel.1 = (bf16[192,4096]{1,0:T(8,128)(2,1)S(1)}, f32[48,128]{1,0:T(8,128)S(1)}) custom-call(bf16[4,16,96,128]{3,2,1,0:T(8,128)(2,1)S(1)} %get-tuple-element.13.fields, bf16[2,4,96,128]{3,2,1,0:T(8,128)(2,1)S(1)} %collective-permute-done.x0, bf16[2,4,96,128]{3,2,1,0:T(8,128)(2,1)S(1)} %get-tuple-element.15.x1, ...), custom_call_target="tpu_custom_call" | custom-call | tf_op jit(solution)/shard_map/panel/pallas_call | solution.py:345
  14.8 0.1 collective-permute-start.5
  14.9 1.2 %collective-permute-done.5 = f32[48,128]{1,0:T(8,128)S(1)} collective-permute-done((f32[48,128]{1,0:T(8,128)S(1)}, f32[48,128]{1,0:T(8,128)S(1)}, u32[]{:S(2)}, u32[]{:S(2)}) %collective-permute-start.5) | collective-permute-done | bytes 24608 | tf_op jit(solution)/shard_map/ppermute | solution.py:46
  16.1 1.3 %collective-permute-start.6 = (f32[48,128]{1,0:T(8,128)S(1)}, f32[48,128]{1,0:T(8,128)S(1)}, u32[]{:S(2)}, u32[]{:S(2)}) collective-permute-start(f32[48,128]{1,0:T(8,128)S(1)} %add.15), channel_id=1, source_target_pairs={{0,3},{1,2},{2,1},{3,0},{4,7},{5,6},{6,5},{7,4},{8,11},{9,10},{10,... | collective-permute-start | bytes 73736 | tf_op jit(solution)/shard_map/ppermute | solution.py:46
  17.4 2.0 %collective-permute-done.6 = f32[48,128]{1,0:T(8,128)S(1)} collective-permute-done((f32[48,128]{1,0:T(8,128)S(1)}, f32[48,128]{1,0:T(8,128)S(1)}, u32[]{:S(2)}, u32[]{:S(2)}) %collective-permute-start.6) | collective-permute-done | bytes 24608 | tf_op jit(solution)/shard_map/ppermute | solution.py:46
  19.4 2.5 %collective-permute-start.7 = (f32[48,128]{1,0:T(8,128)S(1)}, f32[48,128]{1,0:T(8,128)S(1)}, u32[]{:S(2)}, u32[]{:S(2)}) collective-permute-start(f32[48,128]{1,0:T(8,128)S(1)} %add.16), channel_id=1, source_target_pairs={{0,5},{1,4},{2,7},{3,6},{4,1},{5,0},{6,3},{7,2},{8,13},{9,12},{10,... | collective-permute-start | bytes 73736 | tf_op jit(solution)/shard_map/ppermute | solution.py:46
  21.8 1.5 %collective-permute-done.7 = f32[48,128]{1,0:T(8,128)S(1)} collective-permute-done((f32[48,128]{1,0:T(8,128)S(1)}, f32[48,128]{1,0:T(8,128)S(1)}, u32[]{:S(2)}, u32[]{:S(2)}) %collective-permute-start.7) | collective-permute-done | bytes 24608 | tf_op jit(solution)/shard_map/ppermute | solution.py:46
  23.4 2.9 %collective-permute-start.8 = (f32[48,128]{1,0:T(8,128)S(1)}, f32[48,128]{1,0:T(8,128)S(1)}, u32[]{:S(2)}, u32[]{:S(2)}) collective-permute-start(f32[48,128]{1,0:T(8,128)S(1)} %add.17), channel_id=1, source_target_pairs={{0,9},{1,8},{2,11},{3,10},{4,13},{5,12},{6,15},{7,14},{8,1},{9,0},... | collective-permute-start | bytes 73736 | tf_op jit(solution)/shard_map/ppermute | solution.py:46
  26.3 1.5 %collective-permute-done.8 = f32[48,128]{1,0:T(8,128)S(1)} collective-permute-done((f32[48,128]{1,0:T(8,128)S(1)}, f32[48,128]{1,0:T(8,128)S(1)}, u32[]{:S(2)}, u32[]{:S(2)}) %collective-permute-start.8) | collective-permute-done | bytes 24608 | tf_op jit(solution)/shard_map/ppermute | solution.py:46
  27.8 0.4 %collective-permute-start.9 = (f32[48,128]{1,0:T(8,128)S(1)}, f32[48,128]{1,0:T(8,128)S(1)}, u32[]{:S(2)}, u32[]{:S(2)}) collective-permute-start(f32[48,128]{1,0:T(8,128)S(1)} %add.18), channel_id=1, source_target_pairs={{0,17},{1,16},{2,19},{3,18},{4,21},{5,20},{6,23},{7,22},{8,25},{9,... | collective-permute-start | bytes 73736 | tf_op jit(solution)/shard_map/ppermute | solution.py:46
  28.2 2.8 %collective-permute-done.9 = f32[48,128]{1,0:T(8,128)S(1)} collective-permute-done((f32[48,128]{1,0:T(8,128)S(1)}, f32[48,128]{1,0:T(8,128)S(1)}, u32[]{:S(2)}, u32[]{:S(2)}) %collective-permute-start.9) | collective-permute-done | bytes 24608 | tf_op jit(solution)/shard_map/ppermute | solution.py:46
  31.0 3.8 %basis.1 = (f32[3072,128]{1,0:T(8,128)}, f32[96,96]{1,0:T(8,128)}) custom-call(f32[48,128]{1,0:T(8,128)S(1)} %add.19.moments, bf16[192,4096]{1,0:T(8,128)(2,1)S(1)} %get-tuple-element.21.panel), custom_call_target="tpu_custom_call" | custom-call | tf_op jit(solution)/shard_map/basis/pallas_call | solution.py:357
  (5 shorter events, 0.0 us)
Async XLA Ops:
  3.2 8.5 %collective-permute-start = (bf16[2,4,96,128]{3,2,1,0:T(8,128)(2,1)S(1)}, bf16[2,4,96,128]{3,2,1,0:T(8,128)(2,1)S(1)}, u32[]{:S(2)}, u32[]{:S(2)}) collective-permute-start(bf16[2,4,96,128]{3,2,1,0:T(8,128)(2,1)S(1)} %get-tuple-element.14), channel_id=1, source_target_pairs={{0,16},{1,17},{2,18},{3,19},{4,20},{5,21},{6,22},{7,23},{8,24},{9,... | collective-permute-start | bytes 589832 | tf_op jit(solution)/shard_map/ppermute | solution.py:35
  6.2 6.4 %collective-permute-start.1 = (bf16[2,4,96,128]{3,2,1,0:T(8,128)(2,1)S(1)}, bf16[2,4,96,128]{3,2,1,0:T(8,128)(2,1)S(1)}, u32[]{:S(2)}, u32[]{:S(2)}) collective-permute-start(bf16[2,4,96,128]{3,2,1,0:T(8,128)(2,1)S(1)} %get-tuple-element.16), channel_id=1, source_target_pairs={{0,4},{1,5},{2,6},{3,7},{4,0},{5,1},{6,2},{7,3},{8,12},{9,13},{10,... | collective-permute-start | bytes 589832 | tf_op jit(solution)/shard_map/ppermute | solution.py:35
  7.8 4.8 %collective-permute-start.2 = (bf16[2,4,96,128]{3,2,1,0:T(8,128)(2,1)S(1)}, bf16[2,4,96,128]{3,2,1,0:T(8,128)(2,1)S(1)}, u32[]{:S(2)}, u32[]{:S(2)}) collective-permute-start(bf16[2,4,96,128]{3,2,1,0:T(8,128)(2,1)S(1)} %get-tuple-element.17), channel_id=1, source_target_pairs={{0,1},{1,0},{2,3},{3,2},{4,8},{5,9},{6,10},{7,11},{8,4},{9,5},{10,... | collective-permute-start | bytes 589832 | tf_op jit(solution)/shard_map/ppermute | solution.py:35
  7.8 1.6 %collective-permute-start.3 = (bf16[96,128]{1,0:T(8,128)(2,1)S(1)}, bf16[96,128]{1,0:T(8,128)(2,1)S(1)}, u32[]{:S(2)}, u32[]{:S(2)}) collective-permute-start(bf16[96,128]{1,0:T(8,128)(2,1)S(1)} %get-tuple-element.18), channel_id=1, source_target_pairs={{0,1},{1,0},{2,3},{3,2},{4,5},{5,4},{6,7},{7,6},{8,9},{9,8},{10,11... | collective-permute-start | bytes 73736 | tf_op jit(solution)/shard_map/ppermute | solution.py:35
  8.3 3.3 %collective-permute-start.4 = (bf16[96,128]{1,0:T(8,128)(2,1)S(1)}, bf16[96,128]{1,0:T(8,128)(2,1)S(1)}, u32[]{:S(2)}, u32[]{:S(2)}) collective-permute-start(bf16[96,128]{1,0:T(8,128)(2,1)S(1)} %get-tuple-element.19), channel_id=1, source_target_pairs={{0,3},{1,2},{2,1},{3,0},{4,7},{5,6},{6,5},{7,4},{8,11},{9,10},{10,... | collective-permute-start | bytes 73736 | tf_op jit(solution)/shard_map/ppermute | solution.py:35
  14.8 1.3 %collective-permute-start.5 = (f32[48,128]{1,0:T(8,128)S(1)}, f32[48,128]{1,0:T(8,128)S(1)}, u32[]{:S(2)}, u32[]{:S(2)}) collective-permute-start(f32[48,128]{1,0:T(8,128)S(1)} %get-tuple-element.20), channel_id=1, source_target_pairs={{0,1},{1,0},{2,3},{3,2},{4,5},{5,4},{6,7},{7,6},{8,9},{9,8},{10,11... | collective-permute-start | bytes 73736 | tf_op jit(solution)/shard_map/ppermute | solution.py:46
  16.1 3.3 %collective-permute-start.6 = (f32[48,128]{1,0:T(8,128)S(1)}, f32[48,128]{1,0:T(8,128)S(1)}, u32[]{:S(2)}, u32[]{:S(2)}) collective-permute-start(f32[48,128]{1,0:T(8,128)S(1)} %add.15), channel_id=1, source_target_pairs={{0,3},{1,2},{2,1},{3,0},{4,7},{5,6},{6,5},{7,4},{8,11},{9,10},{10,... | collective-permute-start | bytes 73736 | tf_op jit(solution)/shard_map/ppermute | solution.py:46
  19.4 4.0 %collective-permute-start.7 = (f32[48,128]{1,0:T(8,128)S(1)}, f32[48,128]{1,0:T(8,128)S(1)}, u32[]{:S(2)}, u32[]{:S(2)}) collective-permute-start(f32[48,128]{1,0:T(8,128)S(1)} %add.16), channel_id=1, source_target_pairs={{0,5},{1,4},{2,7},{3,6},{4,1},{5,0},{6,3},{7,2},{8,13},{9,12},{10,... | collective-permute-start | bytes 73736 | tf_op jit(solution)/shard_map/ppermute | solution.py:46
  23.4 4.4 %collective-permute-start.8 = (f32[48,128]{1,0:T(8,128)S(1)}, f32[48,128]{1,0:T(8,128)S(1)}, u32[]{:S(2)}, u32[]{:S(2)}) collective-permute-start(f32[48,128]{1,0:T(8,128)S(1)} %add.17), channel_id=1, source_target_pairs={{0,9},{1,8},{2,11},{3,10},{4,13},{5,12},{6,15},{7,14},{8,1},{9,0},... | collective-permute-start | bytes 73736 | tf_op jit(solution)/shard_map/ppermute | solution.py:46
  27.8 3.3 %collective-permute-start.9 = (f32[48,128]{1,0:T(8,128)S(1)}, f32[48,128]{1,0:T(8,128)S(1)}, u32[]{:S(2)}, u32[]{:S(2)}) collective-permute-start(f32[48,128]{1,0:T(8,128)S(1)} %add.18), channel_id=1, source_target_pairs={{0,17},{1,16},{2,19},{3,18},{4,21},{5,20},{6,23},{7,22},{8,25},{9,... | collective-permute-start | bytes 73736 | tf_op jit(solution)/shard_map/ppermute | solution.py:46

commit v5 on v4

--- a/solution.py
+++ b/solution.py
@@ -74,7 +74,18 @@
     work[80:96, :] = jnp.where(lane < 80, near[32:48], near[16:32])
 
 
-def pack_kernel(dims, u, v, w, rho, fields, x0, x1, y0, y1, z0, z1, narrow, wide, arrived):
+def row_of(wide, dims, f, r):
+    return wide[f, pl.ds(r, dims[0], stride=dims[1] * dims[2]), :]
+
+
+def sent_row(dims, f, r):
+    x, y = divmod(r, dims[2])
+    return f >= 2 or (x if f == 0 else y) in (0, dims[1 + f] - 1)
+
+
+def pack_kernel(
+    dims, u, v, w, rho, fields, wide, x0, x1, y0, y1, z0, z1, narrow, extra, arrived
+):
     snaps, nx, ny = dims
     cells = nx * ny
     copies = [
@@ -88,83 +99,113 @@
     z_even = lax.axis_index("gz") % 2 == 0
     lane = lane_index(snaps)
     column = jnp.zeros((snaps, LANES), F32)
-
-    def row(f, r):
-        return wide[f, pl.ds(r, snaps, stride=cells), :]
-
     for f in range(4):
         copies[f].wait()
-        wide[f] = narrow[f].astype(F32)
+        from_rows = functools.partial(row_of, wide if f < 2 else extra, dims, f % 2)
+        if f < 2:
+            wide[f] = narrow[f].astype(F32)
+        else:
+            extra[f - 2] = narrow[f].astype(F32)
         for r in range(cells):
-            cell = row(f, r)
-            fields[f, r] = cell.astype(BF16)
+            if not sent_row(dims, f, r):
+                continue
+            value = from_rows(r)
+            fields[f, r] = value
             if f >= 2:
                 k = (f - 2) * cells + r
-                moved = pltpu.roll(cell, 2 * k + 1, 1)
+                moved = pltpu.roll(value, 2 * k + 1, 1)
                 column = jnp.where((lane == 2 * k) | (lane == 2 * k + 1), moved, column)
-    for i, f in enumerate((0, 3)):
-        for y in range(ny):
-            first, final = fields[f, y], fields[f, (nx - 1) * ny + y]
-            x0[i, y] = jnp.where(x_even, final, first)
-            x1[i, y] = jnp.where(x_even, first, final)
-    for i, f in enumerate((1, 3)):
-        for x in range(nx):
-            first, final = fields[f, x * ny], fields[f, x * ny + ny - 1]
-            y0[i, x] = jnp.where(y_even, final, first)
-            y1[i, x] = jnp.where(y_even, first, final)
+        if f in (0, 3):
+            for y in range(ny):
+                first, final = fields[f, y], fields[f, (nx - 1) * ny + y]
+                x0[f // 3, y] = jnp.where(x_even, final, first).astype(BF16)
+                x1[f // 3, y] = jnp.where(x_even, first, final).astype(BF16)
+        if f in (1, 3):
+            for x in range(nx):
+                first, final = fields[f, x * ny], fields[f, x * ny + ny - 1]
+                y0[f // 3, x] = jnp.where(y_even, final, first).astype(BF16)
+                y1[f // 3, x] = jnp.where(y_even, first, final).astype(BF16)
     final = jnp.where(lane % 2 == 0, column, 0.0)
     first = jnp.where(lane % 2 == 1, column, 0.0)
     z0[...] = jnp.where(z_even, final, first).astype(BF16)
     z1[...] = jnp.where(z_even, first, final).astype(BF16)
 
 
-def panel_kernel(dims, scale, sizes, fields, x0, x1, y0, y1, z0, z1, panel, moments):
+def inner_kernel(dims, fields, wide, inner, select):
+    snaps, nx, ny = dims
+    cells = nx * ny
+    lane = lane_index(snaps)
+
+    def row(f, r):
+        return fields[f, r] if sent_row(dims, f, r) else row_of(wide, dims, f, r)
+
+    sub = lax.broadcasted_iota(jnp.int32, (LANES, LANES), 0)
+    at = lane_index(LANES)
+    first, final = at == 0, at == LANES - 1
+    for k in range(2 * cells):
+        low = jnp.where(first & (sub == 2 * k), -1.0, 0.0)
+        both = jnp.where(final & (sub == 2 * k + 1), 1.0, low)
+        select[:, k * LANES : (k + 1) * LANES] = both.astype(BF16)
+
+    def along(f, position, count, low, high):
+        if position == 0:
+            return row(f, high)
+        if position == count - 1:
+            return -row(f, low)
+        return row(f, high) - row(f, low)
+
+    def across(f, r):
+        value = row(f, r)
+        right = jnp.where(lane == LANES - 1, 0.0, pltpu.roll(value, LANES - 1, 1))
+        return right - jnp.where(lane == 0, 0.0, pltpu.roll(value, 1, 1))
+
+    for x in range(nx):
+        for y in range(ny):
+            r = x * ny + y
+            inner[0, r] = (
+                along(0, x, nx, r - ny, r + ny) + along(1, y, ny, r - 1, r + 1) + across(2, r)
+            )
+            inner[1, r] = along(3, x, nx, r - ny, r + ny)
+            inner[2, r] = along(3, y, ny, r - 1, r + 1)
+            inner[3, r] = across(3, r)
+
+
+def panel_kernel(
+    dims, scale, sizes, fields, inner, select, x0, x1, y0, y1, z0, z1, panel, moments
+):
     snaps, nx, ny = dims
     cells = nx * ny
     at_x, at_y = lax.axis_index("gx"), lax.axis_index("gy")
     x_even, y_even = at_x % 2 == 0, at_y % 2 == 0
-    lane = lane_index(snaps)
-    edges = z0[...].astype(F32) + z1[...].astype(F32)
-
-    def cell(f, r):
-        return fields[f, r].astype(F32)
-
-    def side(even, edge, own, recv_even, recv_odd):
-        return jnp.where(edge, own, jnp.where(even, recv_even, recv_odd)).astype(F32)
-
-    def diff_x(f, i, x, y):
-        r = x * ny + y
+    edges = (z0[...].astype(F32) + z1[...].astype(F32)).astype(BF16)
+
+    def outside(f, r, edge, received):
+        return jnp.where(edge, fields[f, r], received.astype(F32))
+
+    def add_x(value, f, i, x, y):
         if x == 0:
-            left = side(x_even, at_x == 0, fields[f, y], x1[i, y], x0[i, y])
-        else:
-            left = cell(f, r - ny)
+            received = jnp.where(x_even, x1[i, y], x0[i, y])
+            value = value - outside(f, x * ny + y, at_x == 0, received)
         if x == nx - 1:
-            right = side(x_even, at_x == sizes[0] - 1, fields[f, r], x0[i, y], x1[i, y])
-        else:
-            right = cell(f, r + ny)
-        return right - left
-
-    def diff_y(f, i, x, y):
-        r = x * ny + y
+            received = jnp.where(x_even, x0[i, y], x1[i, y])
+            value = value + outside(f, x * ny + y, at_x == sizes[0] - 1, received)
+        return value
+
+    def add_y(value, f, i, x, y):
         if y == 0:
-            left = side(y_even, at_y == 0, fields[f, r], y1[i, x], y0[i, x])
-        else:
-            left = cell(f, r - 1)
+            received = jnp.where(y_even, y1[i, x], y0[i, x])
+            value = value - outside(f, x * ny + y, at_y == 0, received)
         if y == ny - 1:
-            right = side(y_even, at_y == sizes[1] - 1, fields[f, r], y0[i, x], y1[i, x])
-        else:
-            right = cell(f, r + 1)
-        return right - left
-
-    def diff_z(f, i, r):
+            received = jnp.where(y_even, y0[i, x], y1[i, x])
+            value = value + outside(f, x * ny + y, at_y == sizes[1] - 1, received)
+        return value
+
+    def add_z(value, i, r):
         k = i * cells + r
-        value = cell(f, r)
-        ends = jnp.take_along_axis(
-            edges, jnp.where(lane == LANES - 1, 2 * k + 1, 2 * k), axis=1
+        near = jnp.dot(
+            edges, select[:, k * LANES : (k + 1) * LANES], preferred_element_type=F32
         )
-        left = jnp.where(lane == 0, ends, pltpu.roll(value, 1, 1))
-        right = jnp.where(lane == LANES - 1, ends, pltpu.roll(value, LANES - 1, 1))
-        return right - left
+        return value + near
 
     def put(c, value):
         high = value.astype(BF16)
@@ -176,16 +217,19 @@
     for x in range(nx):
         for y in range(ny):
             r = x * ny + y
-            dilatation = 0.5 * (diff_x(0, 0, x, y) + diff_y(1, 0, x, y) + diff_z(2, 0, r))
-            put(r, dilatation)
-            rx, ry, rz = diff_x(3, 1, x, y), diff_y(3, 1, x, y), diff_z(3, 1, r)
+            total = add_y(add_x(inner[0, r], 0, 0, x, y), 1, 0, x, y)
+            put(r, 0.5 * add_z(total, 0, r))
+            rx = add_x(inner[1, r], 3, 1, x, y)
+            ry = add_y(inner[2, r], 3, 1, x, y)
+            rz = add_z(inner[3, r], 1, r)
             put(cells + r, jnp.sqrt(0.25 * (rx * rx + ry * ry + rz * rz) + 0.25))
 
     def product(a, b):
         return lax.dot_general(a, b, (((1,), (1,)), ((), ())), preferred_element_type=F32)
 
-    high, low = panel[0:snaps, :], panel[snaps : 2 * snaps, :]
-    total = (product(high, high) + product(high, low) + product(low, high)) * scale
+    both = product(panel[...], panel[0:snaps, :])
+    cross = both[snaps : 2 * snaps]
+    total = (both[0:snaps] + cross + cross.T) * scale
     moments[...] = fold(total)
 
 
@@ -308,14 +352,15 @@
         pltpu.with_memory_space_constraint(a.reshape(snaps * cells, nz), pltpu.HBM)
         for a in (vel_u, vel_v, vel_w, density)
     ]
-    params = pltpu.CompilerParams(vmem_limit_bytes=48 << 20)
+    params = pltpu.CompilerParams(vmem_limit_bytes=12 << 20)
     x_face = jax.ShapeDtypeStruct((2, ny, snaps, nz), BF16)
     y_face = jax.ShapeDtypeStruct((2, nx, snaps, nz), BF16)
     z_face = jax.ShapeDtypeStruct((snaps, nz), BF16)
-    fields, x0, x1, y0, y1, z0, z1 = pl.pallas_call(
+    fields, wide, x0, x1, y0, y1, z0, z1 = pl.pallas_call(
         functools.partial(pack_kernel, dims),
         out_shape=(
-            jax.ShapeDtypeStruct((4, cells, snaps, nz), BF16),
+            jax.ShapeDtypeStruct((4, cells, snaps, nz), F32),
+            jax.ShapeDtypeStruct((2, snaps * cells, nz), F32),
             x_face,
             x_face,
             y_face,
@@ -324,10 +369,10 @@
             z_face,
         ),
         in_specs=[HBM] * 4,
-        out_specs=[VMEM] * 7,
+        out_specs=[VMEM] * 8,
         scratch_shapes=[
             pltpu.VMEM((4, snaps * cells, nz), BF16),
-            pltpu.VMEM((4, snaps * cells, nz), F32),
+            pltpu.VMEM((2, snaps * cells, nz), F32),
             pltpu.SemaphoreType.DMA((4,)),
         ],
         compiler_params=params,
@@ -341,6 +386,17 @@
     z1 = swapped(z1, "gz", 1, True)
     if sizes[0] > 2:
         x1 = swapped(x1, "gx", 1)
+    inner, select = pl.pallas_call(
+        functools.partial(inner_kernel, dims),
+        out_shape=(
+            jax.ShapeDtypeStruct((4, cells, snaps, nz), F32),
+            jax.ShapeDtypeStruct((nz, 2 * cells * nz), BF16),
+        ),
+        in_specs=[VMEM] * 2,
+        out_specs=[VMEM] * 2,
+        compiler_params=params,
+        name="inner",
+    )(fields, wide)
     scale = 1.0 / (2 * cells * nz * sizes[0] * sizes[1] * sizes[2])
     panel, moments = pl.pallas_call(
         functools.partial(panel_kernel, dims, scale, sizes),
@@ -348,11 +404,11 @@
             jax.ShapeDtypeStruct((2 * snaps, 2 * cells * nz), BF16),
             jax.ShapeDtypeStruct((snaps // 2, LANES), F32),
         ),
-        in_specs=[VMEM] * 7,
+        in_specs=[VMEM] * 9,
         out_specs=[VMEM] * 2,
         compiler_params=params,
         name="panel",
-    )(fields, x0, x1, y0, y1, z0, z1)
+    )(fields, inner, select, x0, x1, y0, y1, z0, z1)
     moments = summed(moments, mate)
     basis, factor = pl.pallas_call(
         functools.partial(basis_kernel, dims),

time: 35 us -> 34.3 us (0.980)
  waiting for transfers between devices: 12.2 us -> 11 us
  Pallas kernels: 8.61 us -> 9.07 us
    ppermute x5, waiting for transfers between devices: 3.18 us -> 1.98 us  [swapped(): return lax.ppermute(value, AXES, out)]
    pallas_call x0 -> x1, Pallas kernels: none -> 1.18 us  [per_device(): pl.pallas_call(functools.partial(inner_kernel, dims), out_shape=(jax.Shap...]
    pallas_call x1, Pallas kernels: 2.27 us -> 1.78 us  [per_device(): pl.pallas_call(functools.partial(panel_kernel, dims, scale, sizes), out_s...]
  transfers between devices with their start and end apart: 10 -> 10, of which waited for: 7 -> 7; matrix products, arithmetic and copies ran while one was open for 0% -> 0% of each run, Pallas kernels for 0% -> 3%
where the time goes in v5:
time: 34.3 us; the launch traced here: 34.2 us
  starting transfers between devices  13.4 us (39%)
  waiting for transfers between devices  11 us (32%)
  Pallas kernels  9.07 us (26%)
  between operations  0.68 us (2%)
    ppermute x5, waiting for transfers between devices, summed(): lax.ppermute(value, AXES, [(i, i ^ step) for i in range(count)])  9.02 us
    ppermute x5, starting transfers between devices, summed(): lax.ppermute(value, AXES, [(i, i ^ step) for i in range(count)])  7.16 us
    ppermute x5, starting transfers between devices, swapped(): return lax.ppermute(value, AXES, out)  6.22 us
    pallas_call x1, Pallas kernels, per_device(): pl.pallas_call(functools.partial(basis_kernel, dims), out_shape=(jax.Shap...  3.81 us
    pallas_call x1, Pallas kernels, per_device(): pl.pallas_call(functools.partial(pack_kernel, dims), out_shape=(jax.Shape...  2.3 us
    ppermute x5, waiting for transfers between devices, swapped(): return lax.ppermute(value, AXES, out)  1.98 us
    pallas_call x1, Pallas kernels, per_device(): pl.pallas_call(functools.partial(panel_kernel, dims, scale, sizes), out_s...  1.78 us
    pallas_call x1, Pallas kernels, per_device(): pl.pallas_call(functools.partial(inner_kernel, dims), out_shape=(jax.Shap...  1.18 us
  transfers between devices with their start and end apart: 10, of which 7 were waited for; matrix products, arithmetic and copies ran while one was open for 0% of the time, Pallas kernels for 3%

profile of v5, /device:TPU:0, one launch (start us, length us, event | category | flops | bytes accessed | tf_op | source)
XLA Modules:
  0.0 34.2 jit_solution(9177275994918533271)
XLA Ops:
  0.6 2.3 %pack.1 = (f32[4,16,96,128]{3,2,1,0:T(8,128)S(1)}, f32[2,1536,128]{2,1,0:T(8,128)S(1)}, bf16[2,4,96,128]{3,2,1,0:T(8,128)(2,1)S(1)}, bf16[2,4,96,128]{3,2,1,0:T(...) custom-call(bf16[1536,128]{1,0:T(8,128)(2,1)} %bitcast.5, ...), custom_call_target="tpu_custom_call" | custom-call | tf_op jit(solution)/shard_map/pack/pallas_call | solution.py:359
  2.9 3.0 %collective-permute-start = (bf16[2,4,96,128]{3,2,1,0:T(8,128)(2,1)S(1)}, bf16[2,4,96,128]{3,2,1,0:T(8,128)(2,1)S(1)}, u32[]{:S(2)}, u32[]{:S(2)}) collective-permute-start(bf16[2,4,96,128]{3,2,1,0:T(8,128)(2,1)S(1)} %get-tuple-element.20), channel_id=1, source_target_pairs={{0,16},{1,17},{2,18},{3,19},{4,20},{5,21},{6,22},{7,23},{8,24},{9,... | collective-permute-start | bytes 589832 | tf_op jit(solution)/shard_map/ppermute | solution.py:35
  6.0 1.6 %collective-permute-start.1 = (bf16[2,4,96,128]{3,2,1,0:T(8,128)(2,1)S(1)}, bf16[2,4,96,128]{3,2,1,0:T(8,128)(2,1)S(1)}, u32[]{:S(2)}, u32[]{:S(2)}) collective-permute-start(bf16[2,4,96,128]{3,2,1,0:T(8,128)(2,1)S(1)} %get-tuple-element.22), channel_id=1, source_target_pairs={{0,4},{1,5},{2,6},{3,7},{4,0},{5,1},{6,2},{7,3},{8,12},{9,13},{10,... | collective-permute-start | bytes 589832 | tf_op jit(solution)/shard_map/ppermute | solution.py:35
  7.5 0.0 collective-permute-start.2
  7.6 0.5 %collective-permute-start.3 = (bf16[96,128]{1,0:T(8,128)(2,1)S(1)}, bf16[96,128]{1,0:T(8,128)(2,1)S(1)}, u32[]{:S(2)}, u32[]{:S(2)}) collective-permute-start(bf16[96,128]{1,0:T(8,128)(2,1)S(1)} %get-tuple-element.24), channel_id=1, source_target_pairs={{0,1},{1,0},{2,3},{3,2},{4,5},{5,4},{6,7},{7,6},{8,9},{9,8},{10,11... | collective-permute-start | bytes 73736 | tf_op jit(solution)/shard_map/ppermute | solution.py:35
  8.1 1.1 %collective-permute-start.4 = (bf16[96,128]{1,0:T(8,128)(2,1)S(1)}, bf16[96,128]{1,0:T(8,128)(2,1)S(1)}, u32[]{:S(2)}, u32[]{:S(2)}) collective-permute-start(bf16[96,128]{1,0:T(8,128)(2,1)S(1)} %get-tuple-element.25), channel_id=1, source_target_pairs={{0,3},{1,2},{2,1},{3,0},{4,7},{5,6},{6,5},{7,4},{8,11},{9,10},{10,... | collective-permute-start | bytes 73736 | tf_op jit(solution)/shard_map/ppermute | solution.py:35
  9.2 1.2 %inner.1 = (f32[4,16,96,128]{3,2,1,0:T(8,128)S(1)}, bf16[128,4096]{1,0:T(8,128)(2,1)S(1)}) custom-call(f32[4,16,96,128]{3,2,1,0:T(8,128)S(1)} %get-tuple-element.16.fields, f32[2,1536,128]{2,1,0:T(8,128)S(1)} %get-tuple-element.17.wide), custom_call_target="tpu_custom_call" | custom-call | tf_op jit(solution)/shard_map/inner/pallas_call | solution.py:389
  10.3 0.0 collective-permute-done.3.z0
  10.4 1.0 %collective-permute-done.4.z1 = bf16[96,128]{1,0:T(8,128)(2,1)S(1)} collective-permute-done((bf16[96,128]{1,0:T(8,128)(2,1)S(1)}, bf16[96,128]{1,0:T(8,128)(2,1)S(1)}, u32[]{:S(2)}, u32[]{:S(2)}) %collective-permute-start.4) | collective-permute-done | bytes 24608 | tf_op jit(solution)/shard_map/ppermute | solution.py:35
  11.4 0.0 collective-permute-done.x0
  11.4 0.9 %collective-permute-done.1.y0 = bf16[2,4,96,128]{3,2,1,0:T(8,128)(2,1)S(1)} collective-permute-done((bf16[2,4,96,128]{3,2,1,0:T(8,128)(2,1)S(1)}, bf16[2,4,96,128]{3,2,1,0:T(8,128)(2,1)S(1)}, u32[]{:S(2)}, u32[]{:S(2)}) %collective-permute-start.1) | collective-permute-done | bytes 196640 | tf_op jit(solution)/shard_map/ppermute | solution.py:35
  12.3 0.0 collective-permute-done.2.y1
  12.3 1.8 %panel.1 = (bf16[192,4096]{1,0:T(8,128)(2,1)S(1)}, f32[48,128]{1,0:T(8,128)S(1)}) custom-call(f32[4,16,96,128]{3,2,1,0:T(8,128)S(1)} %get-tuple-element.16.fields, f32[4,16,96,128]{3,2,1,0:T(8,128)S(1)} %get-tuple-element.18.inner, bf16[128,4096]{1,0:T(8,128)(2,1)S(1)} %get-tuple-element.19.select, bf16[2,4,96,128]{3,2,1,0:T(8,128)(2,1)S(1)} %collective-permute-done.x0, ...), custom_call_target="tpu_custom_call" | custom-call | tf_op jit(solution)/shard_map/panel/pallas_call | solution.py:401
  14.1 0.1 collective-permute-start.5
  14.2 1.2 %collective-permute-done.5 = f32[48,128]{1,0:T(8,128)S(1)} collective-permute-done((f32[48,128]{1,0:T(8,128)S(1)}, f32[48,128]{1,0:T(8,128)S(1)}, u32[]{:S(2)}, u32[]{:S(2)}) %collective-permute-start.5) | collective-permute-done | bytes 24608 | tf_op jit(solution)/shard_map/ppermute | solution.py:46
  15.4 1.3 %collective-permute-start.6 = (f32[48,128]{1,0:T(8,128)S(1)}, f32[48,128]{1,0:T(8,128)S(1)}, u32[]{:S(2)}, u32[]{:S(2)}) collective-permute-start(f32[48,128]{1,0:T(8,128)S(1)} %add.15), channel_id=1, source_target_pairs={{0,3},{1,2},{2,1},{3,0},{4,7},{5,6},{6,5},{7,4},{8,11},{9,10},{10,... | collective-permute-start | bytes 73736 | tf_op jit(solution)/shard_map/ppermute | solution.py:46
  16.7 2.0 %collective-permute-done.6 = f32[48,128]{1,0:T(8,128)S(1)} collective-permute-done((f32[48,128]{1,0:T(8,128)S(1)}, f32[48,128]{1,0:T(8,128)S(1)}, u32[]{:S(2)}, u32[]{:S(2)}) %collective-permute-start.6) | collective-permute-done | bytes 24608 | tf_op jit(solution)/shard_map/ppermute | solution.py:46
  18.6 2.5 %collective-permute-start.7 = (f32[48,128]{1,0:T(8,128)S(1)}, f32[48,128]{1,0:T(8,128)S(1)}, u32[]{:S(2)}, u32[]{:S(2)}) collective-permute-start(f32[48,128]{1,0:T(8,128)S(1)} %add.16), channel_id=1, source_target_pairs={{0,5},{1,4},{2,7},{3,6},{4,1},{5,0},{6,3},{7,2},{8,13},{9,12},{10,... | collective-permute-start | bytes 73736 | tf_op jit(solution)/shard_map/ppermute | solution.py:46
  21.1 1.5 %collective-permute-done.7 = f32[48,128]{1,0:T(8,128)S(1)} collective-permute-done((f32[48,128]{1,0:T(8,128)S(1)}, f32[48,128]{1,0:T(8,128)S(1)}, u32[]{:S(2)}, u32[]{:S(2)}) %collective-permute-start.7) | collective-permute-done | bytes 24608 | tf_op jit(solution)/shard_map/ppermute | solution.py:46
  22.6 2.9 %collective-permute-start.8 = (f32[48,128]{1,0:T(8,128)S(1)}, f32[48,128]{1,0:T(8,128)S(1)}, u32[]{:S(2)}, u32[]{:S(2)}) collective-permute-start(f32[48,128]{1,0:T(8,128)S(1)} %add.17), channel_id=1, source_target_pairs={{0,9},{1,8},{2,11},{3,10},{4,13},{5,12},{6,15},{7,14},{8,1},{9,0},... | collective-permute-start | bytes 73736 | tf_op jit(solution)/shard_map/ppermute | solution.py:46
  25.6 1.5 %collective-permute-done.8 = f32[48,128]{1,0:T(8,128)S(1)} collective-permute-done((f32[48,128]{1,0:T(8,128)S(1)}, f32[48,128]{1,0:T(8,128)S(1)}, u32[]{:S(2)}, u32[]{:S(2)}) %collective-permute-start.8) | collective-permute-done | bytes 24608 | tf_op jit(solution)/shard_map/ppermute | solution.py:46
  27.1 0.4 %collective-permute-start.9 = (f32[48,128]{1,0:T(8,128)S(1)}, f32[48,128]{1,0:T(8,128)S(1)}, u32[]{:S(2)}, u32[]{:S(2)}) collective-permute-start(f32[48,128]{1,0:T(8,128)S(1)} %add.18), channel_id=1, source_target_pairs={{0,17},{1,16},{2,19},{3,18},{4,21},{5,20},{6,23},{7,22},{8,25},{9,... | collective-permute-start | bytes 73736 | tf_op jit(solution)/shard_map/ppermute | solution.py:46
  27.5 2.8 %collective-permute-done.9 = f32[48,128]{1,0:T(8,128)S(1)} collective-permute-done((f32[48,128]{1,0:T(8,128)S(1)}, f32[48,128]{1,0:T(8,128)S(1)}, u32[]{:S(2)}, u32[]{:S(2)}) %collective-permute-start.9) | collective-permute-done | bytes 24608 | tf_op jit(solution)/shard_map/ppermute | solution.py:46
  30.3 3.8 %basis.1 = (f32[3072,128]{1,0:T(8,128)}, f32[96,96]{1,0:T(8,128)}) custom-call(f32[48,128]{1,0:T(8,128)S(1)} %add.19.moments, bf16[192,4096]{1,0:T(8,128)(2,1)S(1)} %get-tuple-element.27.panel), custom_call_target="tpu_custom_call" | custom-call | tf_op jit(solution)/shard_map/basis/pallas_call | solution.py:413
  (5 shorter events, 0.0 us)
Async XLA Ops:
  2.9 8.5 %collective-permute-start = (bf16[2,4,96,128]{3,2,1,0:T(8,128)(2,1)S(1)}, bf16[2,4,96,128]{3,2,1,0:T(8,128)(2,1)S(1)}, u32[]{:S(2)}, u32[]{:S(2)}) collective-permute-start(bf16[2,4,96,128]{3,2,1,0:T(8,128)(2,1)S(1)} %get-tuple-element.20), channel_id=1, source_target_pairs={{0,16},{1,17},{2,18},{3,19},{4,20},{5,21},{6,22},{7,23},{8,24},{9,... | collective-permute-start | bytes 589832 | tf_op jit(solution)/shard_map/ppermute | solution.py:35
  6.0 6.4 %collective-permute-start.1 = (bf16[2,4,96,128]{3,2,1,0:T(8,128)(2,1)S(1)}, bf16[2,4,96,128]{3,2,1,0:T(8,128)(2,1)S(1)}, u32[]{:S(2)}, u32[]{:S(2)}) collective-permute-start(bf16[2,4,96,128]{3,2,1,0:T(8,128)(2,1)S(1)} %get-tuple-element.22), channel_id=1, source_target_pairs={{0,4},{1,5},{2,6},{3,7},{4,0},{5,1},{6,2},{7,3},{8,12},{9,13},{10,... | collective-permute-start | bytes 589832 | tf_op jit(solution)/shard_map/ppermute | solution.py:35
  7.5 4.8 %collective-permute-start.2 = (bf16[2,4,96,128]{3,2,1,0:T(8,128)(2,1)S(1)}, bf16[2,4,96,128]{3,2,1,0:T(8,128)(2,1)S(1)}, u32[]{:S(2)}, u32[]{:S(2)}) collective-permute-start(bf16[2,4,96,128]{3,2,1,0:T(8,128)(2,1)S(1)} %get-tuple-element.23), channel_id=1, source_target_pairs={{0,1},{1,0},{2,3},{3,2},{4,8},{5,9},{6,10},{7,11},{8,4},{9,5},{10,... | collective-permute-start | bytes 589832 | tf_op jit(solution)/shard_map/ppermute | solution.py:35
  7.6 2.8 %collective-permute-start.3 = (bf16[96,128]{1,0:T(8,128)(2,1)S(1)}, bf16[96,128]{1,0:T(8,128)(2,1)S(1)}, u32[]{:S(2)}, u32[]{:S(2)}) collective-permute-start(bf16[96,128]{1,0:T(8,128)(2,1)S(1)} %get-tuple-element.24), channel_id=1, source_target_pairs={{0,1},{1,0},{2,3},{3,2},{4,5},{5,4},{6,7},{7,6},{8,9},{9,8},{10,11... | collective-permute-start | bytes 73736 | tf_op jit(solution)/shard_map/ppermute | solution.py:35
  8.1 3.3 %collective-permute-start.4 = (bf16[96,128]{1,0:T(8,128)(2,1)S(1)}, bf16[96,128]{1,0:T(8,128)(2,1)S(1)}, u32[]{:S(2)}, u32[]{:S(2)}) collective-permute-start(bf16[96,128]{1,0:T(8,128)(2,1)S(1)} %get-tuple-element.25), channel_id=1, source_target_pairs={{0,3},{1,2},{2,1},{3,0},{4,7},{5,6},{6,5},{7,4},{8,11},{9,10},{10,... | collective-permute-start | bytes 73736 | tf_op jit(solution)/shard_map/ppermute | solution.py:35
  14.1 1.3 %collective-permute-start.5 = (f32[48,128]{1,0:T(8,128)S(1)}, f32[48,128]{1,0:T(8,128)S(1)}, u32[]{:S(2)}, u32[]{:S(2)}) collective-permute-start(f32[48,128]{1,0:T(8,128)S(1)} %get-tuple-element.26), channel_id=1, source_target_pairs={{0,1},{1,0},{2,3},{3,2},{4,5},{5,4},{6,7},{7,6},{8,9},{9,8},{10,11... | collective-permute-start | bytes 73736 | tf_op jit(solution)/shard_map/ppermute | solution.py:46
  15.4 3.3 %collective-permute-start.6 = (f32[48,128]{1,0:T(8,128)S(1)}, f32[48,128]{1,0:T(8,128)S(1)}, u32[]{:S(2)}, u32[]{:S(2)}) collective-permute-start(f32[48,128]{1,0:T(8,128)S(1)} %add.15), channel_id=1, source_target_pairs={{0,3},{1,2},{2,1},{3,0},{4,7},{5,6},{6,5},{7,4},{8,11},{9,10},{10,... | collective-permute-start | bytes 73736 | tf_op jit(solution)/shard_map/ppermute | solution.py:46
  18.6 4.0 %collective-permute-start.7 = (f32[48,128]{1,0:T(8,128)S(1)}, f32[48,128]{1,0:T(8,128)S(1)}, u32[]{:S(2)}, u32[]{:S(2)}) collective-permute-start(f32[48,128]{1,0:T(8,128)S(1)} %add.16), channel_id=1, source_target_pairs={{0,5},{1,4},{2,7},{3,6},{4,1},{5,0},{6,3},{7,2},{8,13},{9,12},{10,... | collective-permute-start | bytes 73736 | tf_op jit(solution)/shard_map/ppermute | solution.py:46
  22.6 4.4 %collective-permute-start.8 = (f32[48,128]{1,0:T(8,128)S(1)}, f32[48,128]{1,0:T(8,128)S(1)}, u32[]{:S(2)}, u32[]{:S(2)}) collective-permute-start(f32[48,128]{1,0:T(8,128)S(1)} %add.17), channel_id=1, source_target_pairs={{0,9},{1,8},{2,11},{3,10},{4,13},{5,12},{6,15},{7,14},{8,1},{9,0},... | collective-permute-start | bytes 73736 | tf_op jit(solution)/shard_map/ppermute | solution.py:46
  27.1 3.3 %collective-permute-start.9 = (f32[48,128]{1,0:T(8,128)S(1)}, f32[48,128]{1,0:T(8,128)S(1)}, u32[]{:S(2)}, u32[]{:S(2)}) collective-permute-start(f32[48,128]{1,0:T(8,128)S(1)} %add.18), channel_id=1, source_target_pairs={{0,17},{1,16},{2,19},{3,18},{4,21},{5,20},{6,23},{7,22},{8,25},{9,... | collective-permute-start | bytes 73736 | tf_op jit(solution)/shard_map/ppermute | solution.py:46

commit v6 on v5

--- a/solution.py
+++ b/solution.py
@@ -36,15 +36,26 @@
 
 
 def summed(value, mate):
-    count = int(np.prod([lax.axis_size(a) for a in AXES]))
+    sizes = [lax.axis_size(a) for a in AXES]
+    count = int(np.prod(sizes))
     if count & (count - 1):
         return lax.psum(value, AXES)
-    steps = [mate] + [
-        1 << k | mate for k in range(count.bit_length() - 1) if 1 << k != mate
-    ]
+
+    def other(step):
+        return lax.ppermute(value, AXES, [(i, i ^ step) for i in range(count)])
+
+    steps = [1 << k for k in reversed(range(count.bit_length() - 1)) if 1 << k != mate]
+    last = [k for k in (count // 2, sizes[2]) if k in steps]
+    if len(set(last)) < 2:
+        last = steps[:2]
+    value = value + other(mate)
     for step in steps:
-        value = value + lax.ppermute(value, AXES, [(i, i ^ step) for i in range(count)])
-    return value
+        if step not in last:
+            value = value + other(step | mate)
+    if len(last) < 2:
+        return value + other(last[0] | mate) if last else value
+    one, two, both = other(last[0] | mate), other(last[1] | mate), other(sum(last) | mate)
+    return (value + one) + (two + both)
 
 
 def lane_index(rows):

time: 34.3 us -> 32.7 us (0.953)
  waiting for transfers between devices: 11 us -> 8.29 us
  starting transfers between devices: 13.4 us -> 14.5 us
    ppermute x5 -> x6, waiting for transfers between devices: 9.02 us -> 6.31 us  [other(): return lax.ppermute(value, AXES, [(i, i ^ step) for i in range(count)])]
    ppermute x5 -> x6, starting transfers between devices: 7.16 us -> 8.3 us  [other(): return lax.ppermute(value, AXES, [(i, i ^ step) for i in range(count)])]
  transfers between devices with their start and end apart: 10 -> 11, of which waited for: 7 -> 8; matrix products, arithmetic and copies ran while one was open for 0% -> 0% of each run, Pallas kernels for 3% -> 4%
where the time goes in v6:
time: 32.7 us; the launch traced here: 32.6 us
  starting transfers between devices  14.5 us (44%)
  Pallas kernels  9.07 us (28%)
  waiting for transfers between devices  8.29 us (25%)
  between operations  0.68 us (2%)
    ppermute x6, starting transfers between devices, other(): return lax.ppermute(value, AXES, [(i, i ^ step) for i in range(count)])  8.3 us
    ppermute x6, waiting for transfers between devices, other(): return lax.ppermute(value, AXES, [(i, i ^ step) for i in range(count)])  6.31 us
    ppermute x5, starting transfers between devices, swapped(): return lax.ppermute(value, AXES, out)  6.22 us
    pallas_call x1, Pallas kernels, per_device(): pl.pallas_call(functools.partial(basis_kernel, dims), out_shape=(jax.Shap...  3.81 us
    pallas_call x1, Pallas kernels, per_device(): pl.pallas_call(functools.partial(pack_kernel, dims), out_shape=(jax.Shape...  2.3 us
    ppermute x5, waiting for transfers between devices, swapped(): return lax.ppermute(value, AXES, out)  1.98 us
    pallas_call x1, Pallas kernels, per_device(): pl.pallas_call(functools.partial(panel_kernel, dims, scale, sizes), out_s...  1.78 us
    pallas_call x1, Pallas kernels, per_device(): pl.pallas_call(functools.partial(inner_kernel, dims), out_shape=(jax.Shap...  1.18 us
  transfers between devices with their start and end apart: 11, of which 8 were waited for; matrix products, arithmetic and copies ran while one was open for 0% of the time, Pallas kernels for 4%

profile of v6, /device:TPU:0, one launch (start us, length us, event | category | flops | bytes accessed | tf_op | source)
XLA Modules:
  0.0 32.6 jit_solution(3428140254762271261)
XLA Ops:
  0.6 2.3 %pack.1 = (f32[4,16,96,128]{3,2,1,0:T(8,128)S(1)}, f32[2,1536,128]{2,1,0:T(8,128)S(1)}, bf16[2,4,96,128]{3,2,1,0:T(8,128)(2,1)S(1)}, bf16[2,4,96,128]{3,2,1,0:T(...) custom-call(bf16[1536,128]{1,0:T(8,128)(2,1)} %bitcast.5, ...), custom_call_target="tpu_custom_call" | custom-call | tf_op jit(solution)/shard_map/pack/pallas_call | solution.py:370
  2.9 3.0 %collective-permute-start = (bf16[2,4,96,128]{3,2,1,0:T(8,128)(2,1)S(1)}, bf16[2,4,96,128]{3,2,1,0:T(8,128)(2,1)S(1)}, u32[]{:S(2)}, u32[]{:S(2)}) collective-permute-start(bf16[2,4,96,128]{3,2,1,0:T(8,128)(2,1)S(1)} %get-tuple-element.20), channel_id=1, source_target_pairs={{0,16},{1,17},{2,18},{3,19},{4,20},{5,21},{6,22},{7,23},{8,24},{9,... | collective-permute-start | bytes 589832 | tf_op jit(solution)/shard_map/ppermute | solution.py:35
  6.0 1.6 %collective-permute-start.1 = (bf16[2,4,96,128]{3,2,1,0:T(8,128)(2,1)S(1)}, bf16[2,4,96,128]{3,2,1,0:T(8,128)(2,1)S(1)}, u32[]{:S(2)}, u32[]{:S(2)}) collective-permute-start(bf16[2,4,96,128]{3,2,1,0:T(8,128)(2,1)S(1)} %get-tuple-element.22), channel_id=1, source_target_pairs={{0,4},{1,5},{2,6},{3,7},{4,0},{5,1},{6,2},{7,3},{8,12},{9,13},{10,... | collective-permute-start | bytes 589832 | tf_op jit(solution)/shard_map/ppermute | solution.py:35
  7.6 0.5 %collective-permute-start.3 = (bf16[96,128]{1,0:T(8,128)(2,1)S(1)}, bf16[96,128]{1,0:T(8,128)(2,1)S(1)}, u32[]{:S(2)}, u32[]{:S(2)}) collective-permute-start(bf16[96,128]{1,0:T(8,128)(2,1)S(1)} %get-tuple-element.24), channel_id=1, source_target_pairs={{0,1},{1,0},{2,3},{3,2},{4,5},{5,4},{6,7},{7,6},{8,9},{9,8},{10,11... | collective-permute-start | bytes 73736 | tf_op jit(solution)/shard_map/ppermute | solution.py:35
  8.1 1.1 %collective-permute-start.4 = (bf16[96,128]{1,0:T(8,128)(2,1)S(1)}, bf16[96,128]{1,0:T(8,128)(2,1)S(1)}, u32[]{:S(2)}, u32[]{:S(2)}) collective-permute-start(bf16[96,128]{1,0:T(8,128)(2,1)S(1)} %get-tuple-element.25), channel_id=1, source_target_pairs={{0,3},{1,2},{2,1},{3,0},{4,7},{5,6},{6,5},{7,4},{8,11},{9,10},{10,... | collective-permute-start | bytes 73736 | tf_op jit(solution)/shard_map/ppermute | solution.py:35
  9.2 1.2 %inner.1 = (f32[4,16,96,128]{3,2,1,0:T(8,128)S(1)}, bf16[128,4096]{1,0:T(8,128)(2,1)S(1)}) custom-call(f32[4,16,96,128]{3,2,1,0:T(8,128)S(1)} %get-tuple-element.16.fields, f32[2,1536,128]{2,1,0:T(8,128)S(1)} %get-tuple-element.17.wide), custom_call_target="tpu_custom_call" | custom-call | tf_op jit(solution)/shard_map/inner/pallas_call | solution.py:400
  10.4 1.0 %collective-permute-done.4.z1 = bf16[96,128]{1,0:T(8,128)(2,1)S(1)} collective-permute-done((bf16[96,128]{1,0:T(8,128)(2,1)S(1)}, bf16[96,128]{1,0:T(8,128)(2,1)S(1)}, u32[]{:S(2)}, u32[]{:S(2)}) %collective-permute-start.4) | collective-permute-done | bytes 24608 | tf_op jit(solution)/shard_map/ppermute | solution.py:35
  11.4 0.0 collective-permute-done.x0
  11.4 0.9 %collective-permute-done.1.y0 = bf16[2,4,96,128]{3,2,1,0:T(8,128)(2,1)S(1)} collective-permute-done((bf16[2,4,96,128]{3,2,1,0:T(8,128)(2,1)S(1)}, bf16[2,4,96,128]{3,2,1,0:T(8,128)(2,1)S(1)}, u32[]{:S(2)}, u32[]{:S(2)}) %collective-permute-start.1) | collective-permute-done | bytes 196640 | tf_op jit(solution)/shard_map/ppermute | solution.py:35
  12.3 0.0 collective-permute-done.2.y1
  12.3 1.8 %panel.1 = (bf16[192,4096]{1,0:T(8,128)(2,1)S(1)}, f32[48,128]{1,0:T(8,128)S(1)}) custom-call(f32[4,16,96,128]{3,2,1,0:T(8,128)S(1)} %get-tuple-element.16.fields, f32[4,16,96,128]{3,2,1,0:T(8,128)S(1)} %get-tuple-element.18.inner, bf16[128,4096]{1,0:T(8,128)(2,1)S(1)} %get-tuple-element.19.select, bf16[2,4,96,128]{3,2,1,0:T(8,128)(2,1)S(1)} %collective-permute-done.x0, ...), custom_call_target="tpu_custom_call" | custom-call | tf_op jit(solution)/shard_map/panel/pallas_call | solution.py:412
  14.1 0.1 collective-permute-start.5
  14.2 1.2 %collective-permute-done.5 = f32[48,128]{1,0:T(8,128)S(1)} collective-permute-done((f32[48,128]{1,0:T(8,128)S(1)}, f32[48,128]{1,0:T(8,128)S(1)}, u32[]{:S(2)}, u32[]{:S(2)}) %collective-permute-start.5) | collective-permute-done | bytes 24608 | tf_op jit(solution)/shard_map/ppermute | solution.py:45
  15.4 3.7 %collective-permute-start.6 = (f32[48,128]{1,0:T(8,128)S(1)}, f32[48,128]{1,0:T(8,128)S(1)}, u32[]{:S(2)}, u32[]{:S(2)}) collective-permute-start(f32[48,128]{1,0:T(8,128)S(1)} %add.18), channel_id=1, source_target_pairs={{0,9},{1,8},{2,11},{3,10},{4,13},{5,12},{6,15},{7,14},{8,1},{9,0},... | collective-permute-start | bytes 73736 | tf_op jit(solution)/shard_map/ppermute | solution.py:45
  19.0 1.5 %collective-permute-done.6 = f32[48,128]{1,0:T(8,128)S(1)} collective-permute-done((f32[48,128]{1,0:T(8,128)S(1)}, f32[48,128]{1,0:T(8,128)S(1)}, u32[]{:S(2)}, u32[]{:S(2)}) %collective-permute-start.6) | collective-permute-done | bytes 24608 | tf_op jit(solution)/shard_map/ppermute | solution.py:45
  20.6 1.4 %collective-permute-start.7 = (f32[48,128]{1,0:T(8,128)S(1)}, f32[48,128]{1,0:T(8,128)S(1)}, u32[]{:S(2)}, u32[]{:S(2)}) collective-permute-start(f32[48,128]{1,0:T(8,128)S(1)} %add.19), channel_id=1, source_target_pairs={{0,3},{1,2},{2,1},{3,0},{4,7},{5,6},{6,5},{7,4},{8,11},{9,10},{10,... | collective-permute-start | bytes 73736 | tf_op jit(solution)/shard_map/ppermute | solution.py:45
  22.0 1.8 %collective-permute-done.7 = f32[48,128]{1,0:T(8,128)S(1)} collective-permute-done((f32[48,128]{1,0:T(8,128)S(1)}, f32[48,128]{1,0:T(8,128)S(1)}, u32[]{:S(2)}, u32[]{:S(2)}) %collective-permute-start.7) | collective-permute-done | bytes 24608 | tf_op jit(solution)/shard_map/ppermute | solution.py:45
  23.8 1.4 %collective-permute-start.10 = (f32[48,128]{1,0:T(8,128)S(1)}, f32[48,128]{1,0:T(8,128)S(1)}, u32[]{:S(2)}, u32[]{:S(2)}) collective-permute-start(f32[48,128]{1,0:T(8,128)S(1)} %add.20), channel_id=1, source_target_pairs={{0,21},{1,20},{2,23},{3,22},{4,17},{5,16},{6,19},{7,18},{8,29},{9,... | collective-permute-start | bytes 73736 | tf_op jit(solution)/shard_map/ppermute | solution.py:45
  25.2 0.3 collective-permute-start.9
  25.5 1.5 %collective-permute-start.8 = (f32[48,128]{1,0:T(8,128)S(1)}, f32[48,128]{1,0:T(8,128)S(1)}, u32[]{:S(2)}, u32[]{:S(2)}) collective-permute-start(f32[48,128]{1,0:T(8,128)S(1)} %add.20), channel_id=1, source_target_pairs={{0,17},{1,16},{2,19},{3,18},{4,21},{5,20},{6,23},{7,22},{8,25},{9,... | collective-permute-start | bytes 73736 | tf_op jit(solution)/shard_map/ppermute | solution.py:45
  27.0 1.0 %collective-permute-done.10 = f32[48,128]{1,0:T(8,128)S(1)} collective-permute-done((f32[48,128]{1,0:T(8,128)S(1)}, f32[48,128]{1,0:T(8,128)S(1)}, u32[]{:S(2)}, u32[]{:S(2)}) %collective-permute-start.10) | collective-permute-done | bytes 24608 | tf_op jit(solution)/shard_map/ppermute | solution.py:45
  28.0 0.5 %collective-permute-done.9 = f32[48,128]{1,0:T(8,128)S(1)} collective-permute-done((f32[48,128]{1,0:T(8,128)S(1)}, f32[48,128]{1,0:T(8,128)S(1)}, u32[]{:S(2)}, u32[]{:S(2)}) %collective-permute-start.9) | collective-permute-done | bytes 24608 | tf_op jit(solution)/shard_map/ppermute | solution.py:45
  28.5 0.3 collective-permute-done.8
  28.8 3.8 %basis.1 = (f32[3072,128]{1,0:T(8,128)}, f32[96,96]{1,0:T(8,128)}) custom-call(f32[48,128]{1,0:T(8,128)S(1)} %add_add_fusion.moments, bf16[192,4096]{1,0:T(8,128)(2,1)S(1)} %get-tuple-element.27.panel), custom_call_target="tpu_custom_call" | custom-call | tf_op jit(solution)/shard_map/basis/pallas_call | solution.py:424
  (6 shorter events, 0.0 us)
Async XLA Ops:
  2.9 8.5 %collective-permute-start = (bf16[2,4,96,128]{3,2,1,0:T(8,128)(2,1)S(1)}, bf16[2,4,96,128]{3,2,1,0:T(8,128)(2,1)S(1)}, u32[]{:S(2)}, u32[]{:S(2)}) collective-permute-start(bf16[2,4,96,128]{3,2,1,0:T(8,128)(2,1)S(1)} %get-tuple-element.20), channel_id=1, source_target_pairs={{0,16},{1,17},{2,18},{3,19},{4,20},{5,21},{6,22},{7,23},{8,24},{9,... | collective-permute-start | bytes 589832 | tf_op jit(solution)/shard_map/ppermute | solution.py:35
  6.0 6.4 %collective-permute-start.1 = (bf16[2,4,96,128]{3,2,1,0:T(8,128)(2,1)S(1)}, bf16[2,4,96,128]{3,2,1,0:T(8,128)(2,1)S(1)}, u32[]{:S(2)}, u32[]{:S(2)}) collective-permute-start(bf16[2,4,96,128]{3,2,1,0:T(8,128)(2,1)S(1)} %get-tuple-element.22), channel_id=1, source_target_pairs={{0,4},{1,5},{2,6},{3,7},{4,0},{5,1},{6,2},{7,3},{8,12},{9,13},{10,... | collective-permute-start | bytes 589832 | tf_op jit(solution)/shard_map/ppermute | solution.py:35
  7.5 4.8 %collective-permute-start.2 = (bf16[2,4,96,128]{3,2,1,0:T(8,128)(2,1)S(1)}, bf16[2,4,96,128]{3,2,1,0:T(8,128)(2,1)S(1)}, u32[]{:S(2)}, u32[]{:S(2)}) collective-permute-start(bf16[2,4,96,128]{3,2,1,0:T(8,128)(2,1)S(1)} %get-tuple-element.23), channel_id=1, source_target_pairs={{0,1},{1,0},{2,3},{3,2},{4,8},{5,9},{6,10},{7,11},{8,4},{9,5},{10,... | collective-permute-start | bytes 589832 | tf_op jit(solution)/shard_map/ppermute | solution.py:35
  7.6 2.8 %collective-permute-start.3 = (bf16[96,128]{1,0:T(8,128)(2,1)S(1)}, bf16[96,128]{1,0:T(8,128)(2,1)S(1)}, u32[]{:S(2)}, u32[]{:S(2)}) collective-permute-start(bf16[96,128]{1,0:T(8,128)(2,1)S(1)} %get-tuple-element.24), channel_id=1, source_target_pairs={{0,1},{1,0},{2,3},{3,2},{4,5},{5,4},{6,7},{7,6},{8,9},{9,8},{10,11... | collective-permute-start | bytes 73736 | tf_op jit(solution)/shard_map/ppermute | solution.py:35
  8.1 3.3 %collective-permute-start.4 = (bf16[96,128]{1,0:T(8,128)(2,1)S(1)}, bf16[96,128]{1,0:T(8,128)(2,1)S(1)}, u32[]{:S(2)}, u32[]{:S(2)}) collective-permute-start(bf16[96,128]{1,0:T(8,128)(2,1)S(1)} %get-tuple-element.25), channel_id=1, source_target_pairs={{0,3},{1,2},{2,1},{3,0},{4,7},{5,6},{6,5},{7,4},{8,11},{9,10},{10,... | collective-permute-start | bytes 73736 | tf_op jit(solution)/shard_map/ppermute | solution.py:35
  14.1 1.3 %collective-permute-start.5 = (f32[48,128]{1,0:T(8,128)S(1)}, f32[48,128]{1,0:T(8,128)S(1)}, u32[]{:S(2)}, u32[]{:S(2)}) collective-permute-start(f32[48,128]{1,0:T(8,128)S(1)} %get-tuple-element.26), channel_id=1, source_target_pairs={{0,1},{1,0},{2,3},{3,2},{4,5},{5,4},{6,7},{7,6},{8,9},{9,8},{10,11... | collective-permute-start | bytes 73736 | tf_op jit(solution)/shard_map/ppermute | solution.py:45
  15.4 5.2 %collective-permute-start.6 = (f32[48,128]{1,0:T(8,128)S(1)}, f32[48,128]{1,0:T(8,128)S(1)}, u32[]{:S(2)}, u32[]{:S(2)}) collective-permute-start(f32[48,128]{1,0:T(8,128)S(1)} %add.18), channel_id=1, source_target_pairs={{0,9},{1,8},{2,11},{3,10},{4,13},{5,12},{6,15},{7,14},{8,1},{9,0},... | collective-permute-start | bytes 73736 | tf_op jit(solution)/shard_map/ppermute | solution.py:45
  20.6 3.3 %collective-permute-start.7 = (f32[48,128]{1,0:T(8,128)S(1)}, f32[48,128]{1,0:T(8,128)S(1)}, u32[]{:S(2)}, u32[]{:S(2)}) collective-permute-start(f32[48,128]{1,0:T(8,128)S(1)} %add.19), channel_id=1, source_target_pairs={{0,3},{1,2},{2,1},{3,0},{4,7},{5,6},{6,5},{7,4},{8,11},{9,10},{10,... | collective-permute-start | bytes 73736 | tf_op jit(solution)/shard_map/ppermute | solution.py:45
  23.8 4.2 %collective-permute-start.10 = (f32[48,128]{1,0:T(8,128)S(1)}, f32[48,128]{1,0:T(8,128)S(1)}, u32[]{:S(2)}, u32[]{:S(2)}) collective-permute-start(f32[48,128]{1,0:T(8,128)S(1)} %add.20), channel_id=1, source_target_pairs={{0,21},{1,20},{2,23},{3,22},{4,17},{5,16},{6,19},{7,18},{8,29},{9,... | collective-permute-start | bytes 73736 | tf_op jit(solution)/shard_map/ppermute | solution.py:45
  25.2 3.3 %collective-permute-start.9 = (f32[48,128]{1,0:T(8,128)S(1)}, f32[48,128]{1,0:T(8,128)S(1)}, u32[]{:S(2)}, u32[]{:S(2)}) collective-permute-start(f32[48,128]{1,0:T(8,128)S(1)} %add.20), channel_id=1, source_target_pairs={{0,5},{1,4},{2,7},{3,6},{4,1},{5,0},{6,3},{7,2},{8,13},{9,12},{10,... | collective-permute-start | bytes 73736 | tf_op jit(solution)/shard_map/ppermute | solution.py:45
  25.5 3.3 %collective-permute-start.8 = (f32[48,128]{1,0:T(8,128)S(1)}, f32[48,128]{1,0:T(8,128)S(1)}, u32[]{:S(2)}, u32[]{:S(2)}) collective-permute-start(f32[48,128]{1,0:T(8,128)S(1)} %add.20), channel_id=1, source_target_pairs={{0,17},{1,16},{2,19},{3,18},{4,21},{5,20},{6,23},{7,22},{8,25},{9,... | collective-permute-start | bytes 73736 | tf_op jit(solution)/shard_map/ppermute | solution.py:45

commit v7 on v5

--- a/solution.py
+++ b/solution.py
@@ -39,11 +39,19 @@
     count = int(np.prod([lax.axis_size(a) for a in AXES]))
     if count & (count - 1):
         return lax.psum(value, AXES)
-    steps = [mate] + [
-        1 << k | mate for k in range(count.bit_length() - 1) if 1 << k != mate
-    ]
-    for step in steps:
-        value = value + lax.ppermute(value, AXES, [(i, i ^ step) for i in range(count)])
+
+    def other(step):
+        return lax.ppermute(value, AXES, [(i, i ^ step) for i in range(count)])
+
+    steps = [1 << k for k in range(count.bit_length() - 1) if 1 << k != mate]
+    steps = steps[-1:] + steps[:-1]
+    value = value + other(mate)
+    for k in range(0, len(steps) - 1, 2):
+        near, far = steps[k : k + 2]
+        one, two, both = other(near | mate), other(far | mate), other(near | far | mate)
+        value = (value + one) + (two + both)
+    if len(steps) % 2:
+        value = value + other(steps[-1] | mate)
     return value
 
 

time: 34.3 us -> 32 us (0.933)
  waiting for transfers between devices: 11 us -> 8.44 us
    ppermute x5 -> x7, waiting for transfers between devices: 9.02 us -> 6.46 us  [other(): return lax.ppermute(value, AXES, [(i, i ^ step) for i in range(count)])]
    ppermute x5 -> x7, starting transfers between devices: 7.16 us -> 7.43 us  [other(): return lax.ppermute(value, AXES, [(i, i ^ step) for i in range(count)])]
  transfers between devices with their start and end apart: 10 -> 12, of which waited for: 7 -> 8; matrix products, arithmetic and copies ran while one was open for 0% -> 0% of each run, Pallas kernels for 3% -> 4%
where the time goes in v7:
time: 32 us; the launch traced here: 31.9 us
  starting transfers between devices  13.6 us (42%)
  Pallas kernels  9.08 us (28%)
  waiting for transfers between devices  8.44 us (26%)
  between operations  0.69 us (2%)
    ppermute x7, starting transfers between devices, other(): return lax.ppermute(value, AXES, [(i, i ^ step) for i in range(count)])  7.43 us
    ppermute x7, waiting for transfers between devices, other(): return lax.ppermute(value, AXES, [(i, i ^ step) for i in range(count)])  6.46 us
    ppermute x5, starting transfers between devices, swapped(): return lax.ppermute(value, AXES, out)  6.22 us
    pallas_call x1, Pallas kernels, per_device(): pl.pallas_call(functools.partial(basis_kernel, dims), out_shape=(jax.Shap...  3.81 us
    pallas_call x1, Pallas kernels, per_device(): pl.pallas_call(functools.partial(pack_kernel, dims), out_shape=(jax.Shape...  2.3 us
    ppermute x5, waiting for transfers between devices, swapped(): return lax.ppermute(value, AXES, out)  1.98 us
    pallas_call x1, Pallas kernels, per_device(): pl.pallas_call(functools.partial(panel_kernel, dims, scale, sizes), out_s...  1.78 us
    pallas_call x1, Pallas kernels, per_device(): pl.pallas_call(functools.partial(inner_kernel, dims), out_shape=(jax.Shap...  1.18 us
  transfers between devices with their start and end apart: 12, of which 8 were waited for; matrix products, arithmetic and copies ran while one was open for 0% of the time, Pallas kernels for 4%

profile of v7, /device:TPU:0, one launch (start us, length us, event | category | flops | bytes accessed | tf_op | source)
XLA Modules:
  0.0 31.9 jit_solution(5346711117802463263)
XLA Ops:
  0.6 2.3 %pack.1 = (f32[4,16,96,128]{3,2,1,0:T(8,128)S(1)}, f32[2,1536,128]{2,1,0:T(8,128)S(1)}, bf16[2,4,96,128]{3,2,1,0:T(8,128)(2,1)S(1)}, bf16[2,4,96,128]{3,2,1,0:T(...) custom-call(bf16[1536,128]{1,0:T(8,128)(2,1)} %bitcast.5, ...), custom_call_target="tpu_custom_call" | custom-call | tf_op jit(solution)/shard_map/pack/pallas_call | solution.py:367
  2.9 3.0 %collective-permute-start = (bf16[2,4,96,128]{3,2,1,0:T(8,128)(2,1)S(1)}, bf16[2,4,96,128]{3,2,1,0:T(8,128)(2,1)S(1)}, u32[]{:S(2)}, u32[]{:S(2)}) collective-permute-start(bf16[2,4,96,128]{3,2,1,0:T(8,128)(2,1)S(1)} %get-tuple-element.20), channel_id=1, source_target_pairs={{0,16},{1,17},{2,18},{3,19},{4,20},{5,21},{6,22},{7,23},{8,24},{9,... | collective-permute-start | bytes 589832 | tf_op jit(solution)/shard_map/ppermute | solution.py:35
  6.0 1.6 %collective-permute-start.1 = (bf16[2,4,96,128]{3,2,1,0:T(8,128)(2,1)S(1)}, bf16[2,4,96,128]{3,2,1,0:T(8,128)(2,1)S(1)}, u32[]{:S(2)}, u32[]{:S(2)}) collective-permute-start(bf16[2,4,96,128]{3,2,1,0:T(8,128)(2,1)S(1)} %get-tuple-element.22), channel_id=1, source_target_pairs={{0,4},{1,5},{2,6},{3,7},{4,0},{5,1},{6,2},{7,3},{8,12},{9,13},{10,... | collective-permute-start | bytes 589832 | tf_op jit(solution)/shard_map/ppermute | solution.py:35
  7.6 0.5 %collective-permute-start.3 = (bf16[96,128]{1,0:T(8,128)(2,1)S(1)}, bf16[96,128]{1,0:T(8,128)(2,1)S(1)}, u32[]{:S(2)}, u32[]{:S(2)}) collective-permute-start(bf16[96,128]{1,0:T(8,128)(2,1)S(1)} %get-tuple-element.24), channel_id=1, source_target_pairs={{0,1},{1,0},{2,3},{3,2},{4,5},{5,4},{6,7},{7,6},{8,9},{9,8},{10,11... | collective-permute-start | bytes 73736 | tf_op jit(solution)/shard_map/ppermute | solution.py:35
  8.1 1.1 %collective-permute-start.4 = (bf16[96,128]{1,0:T(8,128)(2,1)S(1)}, bf16[96,128]{1,0:T(8,128)(2,1)S(1)}, u32[]{:S(2)}, u32[]{:S(2)}) collective-permute-start(bf16[96,128]{1,0:T(8,128)(2,1)S(1)} %get-tuple-element.25), channel_id=1, source_target_pairs={{0,3},{1,2},{2,1},{3,0},{4,7},{5,6},{6,5},{7,4},{8,11},{9,10},{10,... | collective-permute-start | bytes 73736 | tf_op jit(solution)/shard_map/ppermute | solution.py:35
  9.2 1.2 %inner.1 = (f32[4,16,96,128]{3,2,1,0:T(8,128)S(1)}, bf16[128,4096]{1,0:T(8,128)(2,1)S(1)}) custom-call(f32[4,16,96,128]{3,2,1,0:T(8,128)S(1)} %get-tuple-element.16.fields, f32[2,1536,128]{2,1,0:T(8,128)S(1)} %get-tuple-element.17.wide), custom_call_target="tpu_custom_call" | custom-call | tf_op jit(solution)/shard_map/inner/pallas_call | solution.py:397
  10.3 0.0 collective-permute-done.3.z0
  10.4 1.0 %collective-permute-done.4.z1 = bf16[96,128]{1,0:T(8,128)(2,1)S(1)} collective-permute-done((bf16[96,128]{1,0:T(8,128)(2,1)S(1)}, bf16[96,128]{1,0:T(8,128)(2,1)S(1)}, u32[]{:S(2)}, u32[]{:S(2)}) %collective-permute-start.4) | collective-permute-done | bytes 24608 | tf_op jit(solution)/shard_map/ppermute | solution.py:35
  11.4 0.9 %collective-permute-done.1.y0 = bf16[2,4,96,128]{3,2,1,0:T(8,128)(2,1)S(1)} collective-permute-done((bf16[2,4,96,128]{3,2,1,0:T(8,128)(2,1)S(1)}, bf16[2,4,96,128]{3,2,1,0:T(8,128)(2,1)S(1)}, u32[]{:S(2)}, u32[]{:S(2)}) %collective-permute-start.1) | collective-permute-done | bytes 196640 | tf_op jit(solution)/shard_map/ppermute | solution.py:35
  12.3 1.8 %panel.1 = (bf16[192,4096]{1,0:T(8,128)(2,1)S(1)}, f32[48,128]{1,0:T(8,128)S(1)}) custom-call(f32[4,16,96,128]{3,2,1,0:T(8,128)S(1)} %get-tuple-element.16.fields, f32[4,16,96,128]{3,2,1,0:T(8,128)S(1)} %get-tuple-element.18.inner, bf16[128,4096]{1,0:T(8,128)(2,1)S(1)} %get-tuple-element.19.select, bf16[2,4,96,128]{3,2,1,0:T(8,128)(2,1)S(1)} %collective-permute-done.x0, ...), custom_call_target="tpu_custom_call" | custom-call | tf_op jit(solution)/shard_map/panel/pallas_call | solution.py:409
  14.1 0.1 collective-permute-start.5
  14.2 1.2 %collective-permute-done.5 = f32[48,128]{1,0:T(8,128)S(1)} collective-permute-done((f32[48,128]{1,0:T(8,128)S(1)}, f32[48,128]{1,0:T(8,128)S(1)}, u32[]{:S(2)}, u32[]{:S(2)}) %collective-permute-start.5) | collective-permute-done | bytes 24608 | tf_op jit(solution)/shard_map/ppermute | solution.py:44
  15.4 1.2 %collective-permute-start.8 = (f32[48,128]{1,0:T(8,128)S(1)}, f32[48,128]{1,0:T(8,128)S(1)}, u32[]{:S(2)}, u32[]{:S(2)}) collective-permute-start(f32[48,128]{1,0:T(8,128)S(1)} %add.21), channel_id=1, source_target_pairs={{0,19},{1,18},{2,17},{3,16},{4,23},{5,22},{6,21},{7,20},{8,27},{9,... | collective-permute-start | bytes 73736 | tf_op jit(solution)/shard_map/ppermute | solution.py:44
  16.6 0.3 %collective-permute-start.7 = (f32[48,128]{1,0:T(8,128)S(1)}, f32[48,128]{1,0:T(8,128)S(1)}, u32[]{:S(2)}, u32[]{:S(2)}) collective-permute-start(f32[48,128]{1,0:T(8,128)S(1)} %add.21), channel_id=1, source_target_pairs={{0,3},{1,2},{2,1},{3,0},{4,7},{5,6},{6,5},{7,4},{8,11},{9,10},{10,... | collective-permute-start | bytes 73736 | tf_op jit(solution)/shard_map/ppermute | solution.py:44
  16.9 1.4 %collective-permute-start.6 = (f32[48,128]{1,0:T(8,128)S(1)}, f32[48,128]{1,0:T(8,128)S(1)}, u32[]{:S(2)}, u32[]{:S(2)}) collective-permute-start(f32[48,128]{1,0:T(8,128)S(1)} %add.21), channel_id=1, source_target_pairs={{0,17},{1,16},{2,19},{3,18},{4,21},{5,20},{6,23},{7,22},{8,25},{9,... | collective-permute-start | bytes 73736 | tf_op jit(solution)/shard_map/ppermute | solution.py:44
  18.4 1.2 %collective-permute-done.8 = f32[48,128]{1,0:T(8,128)S(1)} collective-permute-done((f32[48,128]{1,0:T(8,128)S(1)}, f32[48,128]{1,0:T(8,128)S(1)}, u32[]{:S(2)}, u32[]{:S(2)}) %collective-permute-start.8) | collective-permute-done | bytes 24608 | tf_op jit(solution)/shard_map/ppermute | solution.py:44
  19.5 0.3 collective-permute-done.7
  19.8 0.3 %collective-permute-done.6 = f32[48,128]{1,0:T(8,128)S(1)} collective-permute-done((f32[48,128]{1,0:T(8,128)S(1)}, f32[48,128]{1,0:T(8,128)S(1)}, u32[]{:S(2)}, u32[]{:S(2)}) %collective-permute-start.6) | collective-permute-done | bytes 24608 | tf_op jit(solution)/shard_map/ppermute | solution.py:44
  20.2 3.6 %collective-permute-start.11 = (f32[48,128]{1,0:T(8,128)S(1)}, f32[48,128]{1,0:T(8,128)S(1)}, u32[]{:S(2)}, u32[]{:S(2)}) collective-permute-start(f32[48,128]{1,0:T(8,128)S(1)} %add_add_fusion.1), channel_id=1, source_target_pairs={{0,13},{1,12},{2,15},{3,14},{4,9},{5,8},{6,11},{7,10},{8,5},{9,4},... | collective-permute-start | bytes 73736 | tf_op jit(solution)/shard_map/ppermute | solution.py:44
  23.8 0.5 %collective-permute-start.10 = (f32[48,128]{1,0:T(8,128)S(1)}, f32[48,128]{1,0:T(8,128)S(1)}, u32[]{:S(2)}, u32[]{:S(2)}) collective-permute-start(f32[48,128]{1,0:T(8,128)S(1)} %add_add_fusion.1), channel_id=1, source_target_pairs={{0,9},{1,8},{2,11},{3,10},{4,13},{5,12},{6,15},{7,14},{8,1},{9,0},... | collective-permute-start | bytes 73736 | tf_op jit(solution)/shard_map/ppermute | solution.py:44
  24.3 0.3 collective-permute-start.9
  24.6 0.8 %collective-permute-done.11 = f32[48,128]{1,0:T(8,128)S(1)} collective-permute-done((f32[48,128]{1,0:T(8,128)S(1)}, f32[48,128]{1,0:T(8,128)S(1)}, u32[]{:S(2)}, u32[]{:S(2)}) %collective-permute-start.11) | collective-permute-done | bytes 24608 | tf_op jit(solution)/shard_map/ppermute | solution.py:44
  25.4 2.7 %collective-permute-done.10 = f32[48,128]{1,0:T(8,128)S(1)} collective-permute-done((f32[48,128]{1,0:T(8,128)S(1)}, f32[48,128]{1,0:T(8,128)S(1)}, u32[]{:S(2)}, u32[]{:S(2)}) %collective-permute-start.10) | collective-permute-done | bytes 24608 | tf_op jit(solution)/shard_map/ppermute | solution.py:44
  28.1 3.8 %basis.1 = (f32[3072,128]{1,0:T(8,128)}, f32[96,96]{1,0:T(8,128)}) custom-call(f32[48,128]{1,0:T(8,128)S(1)} %add_add_fusion.moments, bf16[192,4096]{1,0:T(8,128)(2,1)S(1)} %get-tuple-element.27.panel), custom_call_target="tpu_custom_call" | custom-call | tf_op jit(solution)/shard_map/basis/pallas_call | solution.py:421
  (7 shorter events, 0.0 us)
Async XLA Ops:
  2.9 8.5 %collective-permute-start = (bf16[2,4,96,128]{3,2,1,0:T(8,128)(2,1)S(1)}, bf16[2,4,96,128]{3,2,1,0:T(8,128)(2,1)S(1)}, u32[]{:S(2)}, u32[]{:S(2)}) collective-permute-start(bf16[2,4,96,128]{3,2,1,0:T(8,128)(2,1)S(1)} %get-tuple-element.20), channel_id=1, source_target_pairs={{0,16},{1,17},{2,18},{3,19},{4,20},{5,21},{6,22},{7,23},{8,24},{9,... | collective-permute-start | bytes 589832 | tf_op jit(solution)/shard_map/ppermute | solution.py:35
  6.0 6.4 %collective-permute-start.1 = (bf16[2,4,96,128]{3,2,1,0:T(8,128)(2,1)S(1)}, bf16[2,4,96,128]{3,2,1,0:T(8,128)(2,1)S(1)}, u32[]{:S(2)}, u32[]{:S(2)}) collective-permute-start(bf16[2,4,96,128]{3,2,1,0:T(8,128)(2,1)S(1)} %get-tuple-element.22), channel_id=1, source_target_pairs={{0,4},{1,5},{2,6},{3,7},{4,0},{5,1},{6,2},{7,3},{8,12},{9,13},{10,... | collective-permute-start | bytes 589832 | tf_op jit(solution)/shard_map/ppermute | solution.py:35
  7.5 4.8 %collective-permute-start.2 = (bf16[2,4,96,128]{3,2,1,0:T(8,128)(2,1)S(1)}, bf16[2,4,96,128]{3,2,1,0:T(8,128)(2,1)S(1)}, u32[]{:S(2)}, u32[]{:S(2)}) collective-permute-start(bf16[2,4,96,128]{3,2,1,0:T(8,128)(2,1)S(1)} %get-tuple-element.23), channel_id=1, source_target_pairs={{0,1},{1,0},{2,3},{3,2},{4,8},{5,9},{6,10},{7,11},{8,4},{9,5},{10,... | collective-permute-start | bytes 589832 | tf_op jit(solution)/shard_map/ppermute | solution.py:35
  7.6 2.8 %collective-permute-start.3 = (bf16[96,128]{1,0:T(8,128)(2,1)S(1)}, bf16[96,128]{1,0:T(8,128)(2,1)S(1)}, u32[]{:S(2)}, u32[]{:S(2)}) collective-permute-start(bf16[96,128]{1,0:T(8,128)(2,1)S(1)} %get-tuple-element.24), channel_id=1, source_target_pairs={{0,1},{1,0},{2,3},{3,2},{4,5},{5,4},{6,7},{7,6},{8,9},{9,8},{10,11... | collective-permute-start | bytes 73736 | tf_op jit(solution)/shard_map/ppermute | solution.py:35
  8.1 3.3 %collective-permute-start.4 = (bf16[96,128]{1,0:T(8,128)(2,1)S(1)}, bf16[96,128]{1,0:T(8,128)(2,1)S(1)}, u32[]{:S(2)}, u32[]{:S(2)}) collective-permute-start(bf16[96,128]{1,0:T(8,128)(2,1)S(1)} %get-tuple-element.25), channel_id=1, source_target_pairs={{0,3},{1,2},{2,1},{3,0},{4,7},{5,6},{6,5},{7,4},{8,11},{9,10},{10,... | collective-permute-start | bytes 73736 | tf_op jit(solution)/shard_map/ppermute | solution.py:35
  14.1 1.3 %collective-permute-start.5 = (f32[48,128]{1,0:T(8,128)S(1)}, f32[48,128]{1,0:T(8,128)S(1)}, u32[]{:S(2)}, u32[]{:S(2)}) collective-permute-start(f32[48,128]{1,0:T(8,128)S(1)} %get-tuple-element.26), channel_id=1, source_target_pairs={{0,1},{1,0},{2,3},{3,2},{4,5},{5,4},{6,7},{7,6},{8,9},{9,8},{10,11... | collective-permute-start | bytes 73736 | tf_op jit(solution)/shard_map/ppermute | solution.py:44
  15.4 4.2 %collective-permute-start.8 = (f32[48,128]{1,0:T(8,128)S(1)}, f32[48,128]{1,0:T(8,128)S(1)}, u32[]{:S(2)}, u32[]{:S(2)}) collective-permute-start(f32[48,128]{1,0:T(8,128)S(1)} %add.21), channel_id=1, source_target_pairs={{0,19},{1,18},{2,17},{3,16},{4,23},{5,22},{6,21},{7,20},{8,27},{9,... | collective-permute-start | bytes 73736 | tf_op jit(solution)/shard_map/ppermute | solution.py:44
  16.6 3.3 %collective-permute-start.7 = (f32[48,128]{1,0:T(8,128)S(1)}, f32[48,128]{1,0:T(8,128)S(1)}, u32[]{:S(2)}, u32[]{:S(2)}) collective-permute-start(f32[48,128]{1,0:T(8,128)S(1)} %add.21), channel_id=1, source_target_pairs={{0,3},{1,2},{2,1},{3,0},{4,7},{5,6},{6,5},{7,4},{8,11},{9,10},{10,... | collective-permute-start | bytes 73736 | tf_op jit(solution)/shard_map/ppermute | solution.py:44
  16.9 3.3 %collective-permute-start.6 = (f32[48,128]{1,0:T(8,128)S(1)}, f32[48,128]{1,0:T(8,128)S(1)}, u32[]{:S(2)}, u32[]{:S(2)}) collective-permute-start(f32[48,128]{1,0:T(8,128)S(1)} %add.21), channel_id=1, source_target_pairs={{0,17},{1,16},{2,19},{3,18},{4,21},{5,20},{6,23},{7,22},{8,25},{9,... | collective-permute-start | bytes 73736 | tf_op jit(solution)/shard_map/ppermute | solution.py:44
  20.2 5.2 %collective-permute-start.11 = (f32[48,128]{1,0:T(8,128)S(1)}, f32[48,128]{1,0:T(8,128)S(1)}, u32[]{:S(2)}, u32[]{:S(2)}) collective-permute-start(f32[48,128]{1,0:T(8,128)S(1)} %add_add_fusion.1), channel_id=1, source_target_pairs={{0,13},{1,12},{2,15},{3,14},{4,9},{5,8},{6,11},{7,10},{8,5},{9,4},... | collective-permute-start | bytes 73736 | tf_op jit(solution)/shard_map/ppermute | solution.py:44
  23.8 4.3 %collective-permute-start.10 = (f32[48,128]{1,0:T(8,128)S(1)}, f32[48,128]{1,0:T(8,128)S(1)}, u32[]{:S(2)}, u32[]{:S(2)}) collective-permute-start(f32[48,128]{1,0:T(8,128)S(1)} %add_add_fusion.1), channel_id=1, source_target_pairs={{0,9},{1,8},{2,11},{3,10},{4,13},{5,12},{6,15},{7,14},{8,1},{9,0},... | collective-permute-start | bytes 73736 | tf_op jit(solution)/shard_map/ppermute | solution.py:44
  24.3 3.7 %collective-permute-start.9 = (f32[48,128]{1,0:T(8,128)S(1)}, f32[48,128]{1,0:T(8,128)S(1)}, u32[]{:S(2)}, u32[]{:S(2)}) collective-permute-start(f32[48,128]{1,0:T(8,128)S(1)} %add_add_fusion.1), channel_id=1, source_target_pairs={{0,5},{1,4},{2,7},{3,6},{4,1},{5,0},{6,3},{7,2},{8,13},{9,12},{10,... | collective-permute-start | bytes 73736 | tf_op jit(solution)/shard_map/ppermute | solution.py:44

commit v8 on v7

--- a/solution.py
+++ b/solution.py
@@ -92,7 +92,7 @@
 
 
 def pack_kernel(
-    dims, u, v, w, rho, fields, wide, x0, x1, y0, y1, z0, z1, narrow, extra, arrived
+    dims, two_ways, u, v, w, rho, fields, wide, x0, x1, y0, y1, z0, z1, narrow, extra, arrived
 ):
     snaps, nx, ny = dims
     cells = nx * ny
@@ -100,14 +100,15 @@
         pltpu.make_async_copy(ref, narrow.at[f], arrived.at[f])
         for f, ref in enumerate((u, v, w, rho))
     ]
-    for copy in copies:
+    for copy in reversed(copies):
         copy.start()
     x_even = lax.axis_index("gx") % 2 == 0
     y_even = lax.axis_index("gy") % 2 == 0
     z_even = lax.axis_index("gz") % 2 == 0
     lane = lane_index(snaps)
+    pair = lane // 2
     column = jnp.zeros((snaps, LANES), F32)
-    for f in range(4):
+    for f in reversed(range(4)):
         copies[f].wait()
         from_rows = functools.partial(row_of, wide if f < 2 else extra, dims, f % 2)
         if f < 2:
@@ -122,12 +123,13 @@
             if f >= 2:
                 k = (f - 2) * cells + r
                 moved = pltpu.roll(value, 2 * k + 1, 1)
-                column = jnp.where((lane == 2 * k) | (lane == 2 * k + 1), moved, column)
+                column = jnp.where(pair == k, moved, column)
         if f in (0, 3):
             for y in range(ny):
                 first, final = fields[f, y], fields[f, (nx - 1) * ny + y]
                 x0[f // 3, y] = jnp.where(x_even, final, first).astype(BF16)
-                x1[f // 3, y] = jnp.where(x_even, first, final).astype(BF16)
+                if two_ways:
+                    x1[f // 3, y] = jnp.where(x_even, first, final).astype(BF16)
         if f in (1, 3):
             for x in range(nx):
                 first, final = fields[f, x * ny], fields[f, x * ny + ny - 1]
@@ -192,10 +194,10 @@
 
     def add_x(value, f, i, x, y):
         if x == 0:
-            received = jnp.where(x_even, x1[i, y], x0[i, y])
+            received = jnp.where(x_even, x1[i, y], x0[i, y]) if sizes[0] > 2 else x0[i, y]
             value = value - outside(f, x * ny + y, at_x == 0, received)
         if x == nx - 1:
-            received = jnp.where(x_even, x0[i, y], x1[i, y])
+            received = jnp.where(x_even, x0[i, y], x1[i, y]) if sizes[0] > 2 else x0[i, y]
             value = value + outside(f, x * ny + y, at_x == sizes[0] - 1, received)
         return value
 
@@ -208,12 +210,15 @@
             value = value + outside(f, x * ny + y, at_y == sizes[1] - 1, received)
         return value
 
+    near = {}
+
     def add_z(value, i, r):
         k = i * cells + r
-        near = jnp.dot(
-            edges, select[:, k * LANES : (k + 1) * LANES], preferred_element_type=F32
-        )
-        return value + near
+        if k % 2 == 0:
+            near[i] = jnp.dot(
+                edges, select[:, k * LANES : (k + 2) * LANES], preferred_element_type=F32
+            )
+        return value + near[i][:, k % 2 * LANES : (k % 2 + 1) * LANES]
 
     def put(c, value):
         high = value.astype(BF16)
@@ -365,7 +370,7 @@
     y_face = jax.ShapeDtypeStruct((2, nx, snaps, nz), BF16)
     z_face = jax.ShapeDtypeStruct((snaps, nz), BF16)
     fields, wide, x0, x1, y0, y1, z0, z1 = pl.pallas_call(
-        functools.partial(pack_kernel, dims),
+        functools.partial(pack_kernel, dims, sizes[0] > 2),
         out_shape=(
             jax.ShapeDtypeStruct((4, cells, snaps, nz), F32),
             jax.ShapeDtypeStruct((2, snaps * cells, nz), F32),

time: 32 us -> 31.9 us (level)
  no operation moved by 1% of the time
where the time goes in v8:
time: 31.9 us; the launch traced here: 31.7 us
  starting transfers between devices  13.6 us (43%)
  Pallas kernels  8.93 us (28%)
  waiting for transfers between devices  8.44 us (26%)
  between operations  0.69 us (2%)
    ppermute x7, starting transfers between devices, other(): return lax.ppermute(value, AXES, [(i, i ^ step) for i in range(count)])  7.43 us
    ppermute x7, waiting for transfers between devices, other(): return lax.ppermute(value, AXES, [(i, i ^ step) for i in range(count)])  6.46 us
    ppermute x5, starting transfers between devices, swapped(): return lax.ppermute(value, AXES, out)  6.22 us
    pallas_call x1, Pallas kernels, per_device(): pl.pallas_call(functools.partial(basis_kernel, dims), out_shape=(jax.Shap...  3.81 us
    pallas_call x1, Pallas kernels, per_device(): pl.pallas_call(functools.partial(pack_kernel, dims, sizes[0] > 2), out_sh...  2.3 us
    ppermute x5, waiting for transfers between devices, swapped(): return lax.ppermute(value, AXES, out)  1.98 us
    pallas_call x1, Pallas kernels, per_device(): pl.pallas_call(functools.partial(panel_kernel, dims, scale, sizes), out_s...  1.63 us
    pallas_call x1, Pallas kernels, per_device(): pl.pallas_call(functools.partial(inner_kernel, dims), out_shape=(jax.Shap...  1.18 us
  transfers between devices with their start and end apart: 12, of which 8 were waited for; matrix products, arithmetic and copies ran while one was open for 0% of the time, Pallas kernels for 4%

profile of v8, /device:TPU:0, one launch (start us, length us, event | category | flops | bytes accessed | tf_op | source)
XLA Modules:
  0.0 31.7 jit_solution(5600803180671128944)
XLA Ops:
  0.6 2.3 %pack.1 = (f32[4,16,96,128]{3,2,1,0:T(8,128)S(1)}, f32[2,1536,128]{2,1,0:T(8,128)S(1)}, bf16[2,4,96,128]{3,2,1,0:T(8,128)(2,1)S(1)}, bf16[2,4,96,128]{3,2,1,0:T(...) custom-call(bf16[1536,128]{1,0:T(8,128)(2,1)} %bitcast.5, ...), custom_call_target="tpu_custom_call" | custom-call | tf_op jit(solution)/shard_map/pack/pallas_call | solution.py:372
  2.9 3.0 %collective-permute-start = (bf16[2,4,96,128]{3,2,1,0:T(8,128)(2,1)S(1)}, bf16[2,4,96,128]{3,2,1,0:T(8,128)(2,1)S(1)}, u32[]{:S(2)}, u32[]{:S(2)}) collective-permute-start(bf16[2,4,96,128]{3,2,1,0:T(8,128)(2,1)S(1)} %get-tuple-element.20), channel_id=1, source_target_pairs={{0,16},{1,17},{2,18},{3,19},{4,20},{5,21},{6,22},{7,23},{8,24},{9,... | collective-permute-start | bytes 589832 | tf_op jit(solution)/shard_map/ppermute | solution.py:35
  6.0 1.6 %collective-permute-start.1 = (bf16[2,4,96,128]{3,2,1,0:T(8,128)(2,1)S(1)}, bf16[2,4,96,128]{3,2,1,0:T(8,128)(2,1)S(1)}, u32[]{:S(2)}, u32[]{:S(2)}) collective-permute-start(bf16[2,4,96,128]{3,2,1,0:T(8,128)(2,1)S(1)} %get-tuple-element.22), channel_id=1, source_target_pairs={{0,4},{1,5},{2,6},{3,7},{4,0},{5,1},{6,2},{7,3},{8,12},{9,13},{10,... | collective-permute-start | bytes 589832 | tf_op jit(solution)/shard_map/ppermute | solution.py:35
  7.5 0.0 collective-permute-start.2
  7.6 0.5 %collective-permute-start.3 = (bf16[96,128]{1,0:T(8,128)(2,1)S(1)}, bf16[96,128]{1,0:T(8,128)(2,1)S(1)}, u32[]{:S(2)}, u32[]{:S(2)}) collective-permute-start(bf16[96,128]{1,0:T(8,128)(2,1)S(1)} %get-tuple-element.24), channel_id=1, source_target_pairs={{0,1},{1,0},{2,3},{3,2},{4,5},{5,4},{6,7},{7,6},{8,9},{9,8},{10,11... | collective-permute-start | bytes 73736 | tf_op jit(solution)/shard_map/ppermute | solution.py:35
  8.1 1.1 %collective-permute-start.4 = (bf16[96,128]{1,0:T(8,128)(2,1)S(1)}, bf16[96,128]{1,0:T(8,128)(2,1)S(1)}, u32[]{:S(2)}, u32[]{:S(2)}) collective-permute-start(bf16[96,128]{1,0:T(8,128)(2,1)S(1)} %get-tuple-element.25), channel_id=1, source_target_pairs={{0,3},{1,2},{2,1},{3,0},{4,7},{5,6},{6,5},{7,4},{8,11},{9,10},{10,... | collective-permute-start | bytes 73736 | tf_op jit(solution)/shard_map/ppermute | solution.py:35
  9.2 1.2 %inner.1 = (f32[4,16,96,128]{3,2,1,0:T(8,128)S(1)}, bf16[128,4096]{1,0:T(8,128)(2,1)S(1)}) custom-call(f32[4,16,96,128]{3,2,1,0:T(8,128)S(1)} %get-tuple-element.16.fields, f32[2,1536,128]{2,1,0:T(8,128)S(1)} %get-tuple-element.17.wide), custom_call_target="tpu_custom_call" | custom-call | tf_op jit(solution)/shard_map/inner/pallas_call | solution.py:402
  10.4 1.0 %collective-permute-done.4.z1 = bf16[96,128]{1,0:T(8,128)(2,1)S(1)} collective-permute-done((bf16[96,128]{1,0:T(8,128)(2,1)S(1)}, bf16[96,128]{1,0:T(8,128)(2,1)S(1)}, u32[]{:S(2)}, u32[]{:S(2)}) %collective-permute-start.4) | collective-permute-done | bytes 24608 | tf_op jit(solution)/shard_map/ppermute | solution.py:35
  11.4 0.9 %collective-permute-done.1.y0 = bf16[2,4,96,128]{3,2,1,0:T(8,128)(2,1)S(1)} collective-permute-done((bf16[2,4,96,128]{3,2,1,0:T(8,128)(2,1)S(1)}, bf16[2,4,96,128]{3,2,1,0:T(8,128)(2,1)S(1)}, u32[]{:S(2)}, u32[]{:S(2)}) %collective-permute-start.1) | collective-permute-done | bytes 196640 | tf_op jit(solution)/shard_map/ppermute | solution.py:35
  12.3 1.6 %panel.1 = (bf16[192,4096]{1,0:T(8,128)(2,1)S(1)}, f32[48,128]{1,0:T(8,128)S(1)}) custom-call(f32[4,16,96,128]{3,2,1,0:T(8,128)S(1)} %get-tuple-element.16.fields, f32[4,16,96,128]{3,2,1,0:T(8,128)S(1)} %get-tuple-element.18.inner, bf16[128,4096]{1,0:T(8,128)(2,1)S(1)} %get-tuple-element.19.select, bf16[2,4,96,128]{3,2,1,0:T(8,128)(2,1)S(1)} %collective-permute-done.x0, ...), custom_call_target="tpu_custom_call" | custom-call | tf_op jit(solution)/shard_map/panel/pallas_call | solution.py:414
  14.0 0.1 collective-permute-start.5
  14.1 1.2 %collective-permute-done.5 = f32[48,128]{1,0:T(8,128)S(1)} collective-permute-done((f32[48,128]{1,0:T(8,128)S(1)}, f32[48,128]{1,0:T(8,128)S(1)}, u32[]{:S(2)}, u32[]{:S(2)}) %collective-permute-start.5) | collective-permute-done | bytes 24608 | tf_op jit(solution)/shard_map/ppermute | solution.py:44
  15.2 1.2 %collective-permute-start.8 = (f32[48,128]{1,0:T(8,128)S(1)}, f32[48,128]{1,0:T(8,128)S(1)}, u32[]{:S(2)}, u32[]{:S(2)}) collective-permute-start(f32[48,128]{1,0:T(8,128)S(1)} %add.21), channel_id=1, source_target_pairs={{0,19},{1,18},{2,17},{3,16},{4,23},{5,22},{6,21},{7,20},{8,27},{9,... | collective-permute-start | bytes 73736 | tf_op jit(solution)/shard_map/ppermute | solution.py:44
  16.4 0.3 %collective-permute-start.7 = (f32[48,128]{1,0:T(8,128)S(1)}, f32[48,128]{1,0:T(8,128)S(1)}, u32[]{:S(2)}, u32[]{:S(2)}) collective-permute-start(f32[48,128]{1,0:T(8,128)S(1)} %add.21), channel_id=1, source_target_pairs={{0,3},{1,2},{2,1},{3,0},{4,7},{5,6},{6,5},{7,4},{8,11},{9,10},{10,... | collective-permute-start | bytes 73736 | tf_op jit(solution)/shard_map/ppermute | solution.py:44
  16.8 1.4 %collective-permute-start.6 = (f32[48,128]{1,0:T(8,128)S(1)}, f32[48,128]{1,0:T(8,128)S(1)}, u32[]{:S(2)}, u32[]{:S(2)}) collective-permute-start(f32[48,128]{1,0:T(8,128)S(1)} %add.21), channel_id=1, source_target_pairs={{0,17},{1,16},{2,19},{3,18},{4,21},{5,20},{6,23},{7,22},{8,25},{9,... | collective-permute-start | bytes 73736 | tf_op jit(solution)/shard_map/ppermute | solution.py:44
  18.2 1.2 %collective-permute-done.8 = f32[48,128]{1,0:T(8,128)S(1)} collective-permute-done((f32[48,128]{1,0:T(8,128)S(1)}, f32[48,128]{1,0:T(8,128)S(1)}, u32[]{:S(2)}, u32[]{:S(2)}) %collective-permute-start.8) | collective-permute-done | bytes 24608 | tf_op jit(solution)/shard_map/ppermute | solution.py:44
  19.4 0.3 collective-permute-done.7
  19.7 0.3 %collective-permute-done.6 = f32[48,128]{1,0:T(8,128)S(1)} collective-permute-done((f32[48,128]{1,0:T(8,128)S(1)}, f32[48,128]{1,0:T(8,128)S(1)}, u32[]{:S(2)}, u32[]{:S(2)}) %collective-permute-start.6) | collective-permute-done | bytes 24608 | tf_op jit(solution)/shard_map/ppermute | solution.py:44
  20.1 3.6 %collective-permute-start.11 = (f32[48,128]{1,0:T(8,128)S(1)}, f32[48,128]{1,0:T(8,128)S(1)}, u32[]{:S(2)}, u32[]{:S(2)}) collective-permute-start(f32[48,128]{1,0:T(8,128)S(1)} %add_add_fusion.1), channel_id=1, source_target_pairs={{0,13},{1,12},{2,15},{3,14},{4,9},{5,8},{6,11},{7,10},{8,5},{9,4},... | collective-permute-start | bytes 73736 | tf_op jit(solution)/shard_map/ppermute | solution.py:44
  23.6 0.5 %collective-permute-start.10 = (f32[48,128]{1,0:T(8,128)S(1)}, f32[48,128]{1,0:T(8,128)S(1)}, u32[]{:S(2)}, u32[]{:S(2)}) collective-permute-start(f32[48,128]{1,0:T(8,128)S(1)} %add_add_fusion.1), channel_id=1, source_target_pairs={{0,9},{1,8},{2,11},{3,10},{4,13},{5,12},{6,15},{7,14},{8,1},{9,0},... | collective-permute-start | bytes 73736 | tf_op jit(solution)/shard_map/ppermute | solution.py:44
  24.2 0.3 collective-permute-start.9
  24.4 0.8 %collective-permute-done.11 = f32[48,128]{1,0:T(8,128)S(1)} collective-permute-done((f32[48,128]{1,0:T(8,128)S(1)}, f32[48,128]{1,0:T(8,128)S(1)}, u32[]{:S(2)}, u32[]{:S(2)}) %collective-permute-start.11) | collective-permute-done | bytes 24608 | tf_op jit(solution)/shard_map/ppermute | solution.py:44
  25.2 2.7 %collective-permute-done.10 = f32[48,128]{1,0:T(8,128)S(1)} collective-permute-done((f32[48,128]{1,0:T(8,128)S(1)}, f32[48,128]{1,0:T(8,128)S(1)}, u32[]{:S(2)}, u32[]{:S(2)}) %collective-permute-start.10) | collective-permute-done | bytes 24608 | tf_op jit(solution)/shard_map/ppermute | solution.py:44
  27.9 3.8 %basis.1 = (f32[3072,128]{1,0:T(8,128)}, f32[96,96]{1,0:T(8,128)}) custom-call(f32[48,128]{1,0:T(8,128)S(1)} %add_add_fusion.moments, bf16[192,4096]{1,0:T(8,128)(2,1)S(1)} %get-tuple-element.27.panel), custom_call_target="tpu_custom_call" | custom-call | tf_op jit(solution)/shard_map/basis/pallas_call | solution.py:426
  (7 shorter events, 0.0 us)
Async XLA Ops:
  2.9 8.5 %collective-permute-start = (bf16[2,4,96,128]{3,2,1,0:T(8,128)(2,1)S(1)}, bf16[2,4,96,128]{3,2,1,0:T(8,128)(2,1)S(1)}, u32[]{:S(2)}, u32[]{:S(2)}) collective-permute-start(bf16[2,4,96,128]{3,2,1,0:T(8,128)(2,1)S(1)} %get-tuple-element.20), channel_id=1, source_target_pairs={{0,16},{1,17},{2,18},{3,19},{4,20},{5,21},{6,22},{7,23},{8,24},{9,... | collective-permute-start | bytes 589832 | tf_op jit(solution)/shard_map/ppermute | solution.py:35
  6.0 6.4 %collective-permute-start.1 = (bf16[2,4,96,128]{3,2,1,0:T(8,128)(2,1)S(1)}, bf16[2,4,96,128]{3,2,1,0:T(8,128)(2,1)S(1)}, u32[]{:S(2)}, u32[]{:S(2)}) collective-permute-start(bf16[2,4,96,128]{3,2,1,0:T(8,128)(2,1)S(1)} %get-tuple-element.22), channel_id=1, source_target_pairs={{0,4},{1,5},{2,6},{3,7},{4,0},{5,1},{6,2},{7,3},{8,12},{9,13},{10,... | collective-permute-start | bytes 589832 | tf_op jit(solution)/shard_map/ppermute | solution.py:35
  7.5 4.8 %collective-permute-start.2 = (bf16[2,4,96,128]{3,2,1,0:T(8,128)(2,1)S(1)}, bf16[2,4,96,128]{3,2,1,0:T(8,128)(2,1)S(1)}, u32[]{:S(2)}, u32[]{:S(2)}) collective-permute-start(bf16[2,4,96,128]{3,2,1,0:T(8,128)(2,1)S(1)} %get-tuple-element.23), channel_id=1, source_target_pairs={{0,1},{1,0},{2,3},{3,2},{4,8},{5,9},{6,10},{7,11},{8,4},{9,5},{10,... | collective-permute-start | bytes 589832 | tf_op jit(solution)/shard_map/ppermute | solution.py:35
  7.6 2.8 %collective-permute-start.3 = (bf16[96,128]{1,0:T(8,128)(2,1)S(1)}, bf16[96,128]{1,0:T(8,128)(2,1)S(1)}, u32[]{:S(2)}, u32[]{:S(2)}) collective-permute-start(bf16[96,128]{1,0:T(8,128)(2,1)S(1)} %get-tuple-element.24), channel_id=1, source_target_pairs={{0,1},{1,0},{2,3},{3,2},{4,5},{5,4},{6,7},{7,6},{8,9},{9,8},{10,11... | collective-permute-start | bytes 73736 | tf_op jit(solution)/shard_map/ppermute | solution.py:35
  8.1 3.3 %collective-permute-start.4 = (bf16[96,128]{1,0:T(8,128)(2,1)S(1)}, bf16[96,128]{1,0:T(8,128)(2,1)S(1)}, u32[]{:S(2)}, u32[]{:S(2)}) collective-permute-start(bf16[96,128]{1,0:T(8,128)(2,1)S(1)} %get-tuple-element.25), channel_id=1, source_target_pairs={{0,3},{1,2},{2,1},{3,0},{4,7},{5,6},{6,5},{7,4},{8,11},{9,10},{10,... | collective-permute-start | bytes 73736 | tf_op jit(solution)/shard_map/ppermute | solution.py:35
  14.0 1.3 %collective-permute-start.5 = (f32[48,128]{1,0:T(8,128)S(1)}, f32[48,128]{1,0:T(8,128)S(1)}, u32[]{:S(2)}, u32[]{:S(2)}) collective-permute-start(f32[48,128]{1,0:T(8,128)S(1)} %get-tuple-element.26), channel_id=1, source_target_pairs={{0,1},{1,0},{2,3},{3,2},{4,5},{5,4},{6,7},{7,6},{8,9},{9,8},{10,11... | collective-permute-start | bytes 73736 | tf_op jit(solution)/shard_map/ppermute | solution.py:44
  15.2 4.2 %collective-permute-start.8 = (f32[48,128]{1,0:T(8,128)S(1)}, f32[48,128]{1,0:T(8,128)S(1)}, u32[]{:S(2)}, u32[]{:S(2)}) collective-permute-start(f32[48,128]{1,0:T(8,128)S(1)} %add.21), channel_id=1, source_target_pairs={{0,19},{1,18},{2,17},{3,16},{4,23},{5,22},{6,21},{7,20},{8,27},{9,... | collective-permute-start | bytes 73736 | tf_op jit(solution)/shard_map/ppermute | solution.py:44
  16.4 3.3 %collective-permute-start.7 = (f32[48,128]{1,0:T(8,128)S(1)}, f32[48,128]{1,0:T(8,128)S(1)}, u32[]{:S(2)}, u32[]{:S(2)}) collective-permute-start(f32[48,128]{1,0:T(8,128)S(1)} %add.21), channel_id=1, source_target_pairs={{0,3},{1,2},{2,1},{3,0},{4,7},{5,6},{6,5},{7,4},{8,11},{9,10},{10,... | collective-permute-start | bytes 73736 | tf_op jit(solution)/shard_map/ppermute | solution.py:44
  16.8 3.3 %collective-permute-start.6 = (f32[48,128]{1,0:T(8,128)S(1)}, f32[48,128]{1,0:T(8,128)S(1)}, u32[]{:S(2)}, u32[]{:S(2)}) collective-permute-start(f32[48,128]{1,0:T(8,128)S(1)} %add.21), channel_id=1, source_target_pairs={{0,17},{1,16},{2,19},{3,18},{4,21},{5,20},{6,23},{7,22},{8,25},{9,... | collective-permute-start | bytes 73736 | tf_op jit(solution)/shard_map/ppermute | solution.py:44
  20.1 5.2 %collective-permute-start.11 = (f32[48,128]{1,0:T(8,128)S(1)}, f32[48,128]{1,0:T(8,128)S(1)}, u32[]{:S(2)}, u32[]{:S(2)}) collective-permute-start(f32[48,128]{1,0:T(8,128)S(1)} %add_add_fusion.1), channel_id=1, source_target_pairs={{0,13},{1,12},{2,15},{3,14},{4,9},{5,8},{6,11},{7,10},{8,5},{9,4},... | collective-permute-start | bytes 73736 | tf_op jit(solution)/shard_map/ppermute | solution.py:44
  23.6 4.3 %collective-permute-start.10 = (f32[48,128]{1,0:T(8,128)S(1)}, f32[48,128]{1,0:T(8,128)S(1)}, u32[]{:S(2)}, u32[]{:S(2)}) collective-permute-start(f32[48,128]{1,0:T(8,128)S(1)} %add_add_fusion.1), channel_id=1, source_target_pairs={{0,9},{1,8},{2,11},{3,10},{4,13},{5,12},{6,15},{7,14},{8,1},{9,0},... | collective-permute-start | bytes 73736 | tf_op jit(solution)/shard_map/ppermute | solution.py:44
  24.2 3.7 %collective-permute-start.9 = (f32[48,128]{1,0:T(8,128)S(1)}, f32[48,128]{1,0:T(8,128)S(1)}, u32[]{:S(2)}, u32[]{:S(2)}) collective-permute-start(f32[48,128]{1,0:T(8,128)S(1)} %add_add_fusion.1), channel_id=1, source_target_pairs={{0,5},{1,4},{2,7},{3,6},{4,1},{5,0},{6,3},{7,2},{8,13},{9,12},{10,... | collective-permute-start | bytes 73736 | tf_op jit(solution)/shard_map/ppermute | solution.py:44

commit v9 on v8

--- a/solution.py
+++ b/solution.py
@@ -235,7 +235,8 @@
             rx = add_x(inner[1, r], 3, 1, x, y)
             ry = add_y(inner[2, r], 3, 1, x, y)
             rz = add_z(inner[3, r], 1, r)
-            put(cells + r, jnp.sqrt(0.25 * (rx * rx + ry * ry + rz * rz) + 0.25))
+            square = 0.25 * (rx * rx + ry * ry + rz * rz) + 0.25
+            put(cells + r, square * lax.rsqrt(square))
 
     def product(a, b):
         return lax.dot_general(a, b, (((1,), (1,)), ((), ())), preferred_element_type=F32)

time: 31.9 us -> 31.8 us (level)
  no operation moved by 1% of the time
where the time goes in v9:
time: 31.8 us; the launch traced here: 31.6 us
  starting transfers between devices  13.6 us (43%)
  Pallas kernels  8.83 us (28%)
  waiting for transfers between devices  8.43 us (27%)
  between operations  0.69 us (2%)
    ppermute x7, starting transfers between devices, other(): return lax.ppermute(value, AXES, [(i, i ^ step) for i in range(count)])  7.43 us
    ppermute x7, waiting for transfers between devices, other(): return lax.ppermute(value, AXES, [(i, i ^ step) for i in range(count)])  6.45 us
    ppermute x5, starting transfers between devices, swapped(): return lax.ppermute(value, AXES, out)  6.22 us
    pallas_call x1, Pallas kernels, per_device(): pl.pallas_call(functools.partial(basis_kernel, dims), out_shape=(jax.Shap...  3.81 us
    pallas_call x1, Pallas kernels, per_device(): pl.pallas_call(functools.partial(pack_kernel, dims, sizes[0] > 2), out_sh...  2.3 us
    ppermute x5, waiting for transfers between devices, swapped(): return lax.ppermute(value, AXES, out)  1.98 us
    pallas_call x1, Pallas kernels, per_device(): pl.pallas_call(functools.partial(panel_kernel, dims, scale, sizes), out_s...  1.54 us
    pallas_call x1, Pallas kernels, per_device(): pl.pallas_call(functools.partial(inner_kernel, dims), out_shape=(jax.Shap...  1.18 us
  transfers between devices with their start and end apart: 12, of which 8 were waited for; matrix products, arithmetic and copies ran while one was open for 0% of the time, Pallas kernels for 4%

profile of v9, /device:TPU:0, one launch (start us, length us, event | category | flops | bytes accessed | tf_op | source)
XLA Modules:
  0.0 31.6 jit_solution(489442298969220554)
XLA Ops:
  0.6 2.3 %pack.1 = (f32[4,16,96,128]{3,2,1,0:T(8,128)S(1)}, f32[2,1536,128]{2,1,0:T(8,128)S(1)}, bf16[2,4,96,128]{3,2,1,0:T(8,128)(2,1)S(1)}, bf16[2,4,96,128]{3,2,1,0:T(...) custom-call(bf16[1536,128]{1,0:T(8,128)(2,1)} %bitcast.5, ...), custom_call_target="tpu_custom_call" | custom-call | tf_op jit(solution)/shard_map/pack/pallas_call | solution.py:373
  2.9 3.0 %collective-permute-start = (bf16[2,4,96,128]{3,2,1,0:T(8,128)(2,1)S(1)}, bf16[2,4,96,128]{3,2,1,0:T(8,128)(2,1)S(1)}, u32[]{:S(2)}, u32[]{:S(2)}) collective-permute-start(bf16[2,4,96,128]{3,2,1,0:T(8,128)(2,1)S(1)} %get-tuple-element.20), channel_id=1, source_target_pairs={{0,16},{1,17},{2,18},{3,19},{4,20},{5,21},{6,22},{7,23},{8,24},{9,... | collective-permute-start | bytes 589832 | tf_op jit(solution)/shard_map/ppermute | solution.py:35
  6.0 1.6 %collective-permute-start.1 = (bf16[2,4,96,128]{3,2,1,0:T(8,128)(2,1)S(1)}, bf16[2,4,96,128]{3,2,1,0:T(8,128)(2,1)S(1)}, u32[]{:S(2)}, u32[]{:S(2)}) collective-permute-start(bf16[2,4,96,128]{3,2,1,0:T(8,128)(2,1)S(1)} %get-tuple-element.22), channel_id=1, source_target_pairs={{0,4},{1,5},{2,6},{3,7},{4,0},{5,1},{6,2},{7,3},{8,12},{9,13},{10,... | collective-permute-start | bytes 589832 | tf_op jit(solution)/shard_map/ppermute | solution.py:35
  7.5 0.0 collective-permute-start.2
  7.6 0.5 %collective-permute-start.3 = (bf16[96,128]{1,0:T(8,128)(2,1)S(1)}, bf16[96,128]{1,0:T(8,128)(2,1)S(1)}, u32[]{:S(2)}, u32[]{:S(2)}) collective-permute-start(bf16[96,128]{1,0:T(8,128)(2,1)S(1)} %get-tuple-element.24), channel_id=1, source_target_pairs={{0,1},{1,0},{2,3},{3,2},{4,5},{5,4},{6,7},{7,6},{8,9},{9,8},{10,11... | collective-permute-start | bytes 73736 | tf_op jit(solution)/shard_map/ppermute | solution.py:35
  8.1 1.1 %collective-permute-start.4 = (bf16[96,128]{1,0:T(8,128)(2,1)S(1)}, bf16[96,128]{1,0:T(8,128)(2,1)S(1)}, u32[]{:S(2)}, u32[]{:S(2)}) collective-permute-start(bf16[96,128]{1,0:T(8,128)(2,1)S(1)} %get-tuple-element.25), channel_id=1, source_target_pairs={{0,3},{1,2},{2,1},{3,0},{4,7},{5,6},{6,5},{7,4},{8,11},{9,10},{10,... | collective-permute-start | bytes 73736 | tf_op jit(solution)/shard_map/ppermute | solution.py:35
  9.2 1.2 %inner.1 = (f32[4,16,96,128]{3,2,1,0:T(8,128)S(1)}, bf16[128,4096]{1,0:T(8,128)(2,1)S(1)}) custom-call(f32[4,16,96,128]{3,2,1,0:T(8,128)S(1)} %get-tuple-element.16.fields, f32[2,1536,128]{2,1,0:T(8,128)S(1)} %get-tuple-element.17.wide), custom_call_target="tpu_custom_call" | custom-call | tf_op jit(solution)/shard_map/inner/pallas_call | solution.py:403
  10.4 1.0 %collective-permute-done.4.z1 = bf16[96,128]{1,0:T(8,128)(2,1)S(1)} collective-permute-done((bf16[96,128]{1,0:T(8,128)(2,1)S(1)}, bf16[96,128]{1,0:T(8,128)(2,1)S(1)}, u32[]{:S(2)}, u32[]{:S(2)}) %collective-permute-start.4) | collective-permute-done | bytes 24608 | tf_op jit(solution)/shard_map/ppermute | solution.py:35
  11.4 0.9 %collective-permute-done.1.y0 = bf16[2,4,96,128]{3,2,1,0:T(8,128)(2,1)S(1)} collective-permute-done((bf16[2,4,96,128]{3,2,1,0:T(8,128)(2,1)S(1)}, bf16[2,4,96,128]{3,2,1,0:T(8,128)(2,1)S(1)}, u32[]{:S(2)}, u32[]{:S(2)}) %collective-permute-start.1) | collective-permute-done | bytes 196640 | tf_op jit(solution)/shard_map/ppermute | solution.py:35
  12.3 1.5 %panel.1 = (bf16[192,4096]{1,0:T(8,128)(2,1)S(1)}, f32[48,128]{1,0:T(8,128)S(1)}) custom-call(f32[4,16,96,128]{3,2,1,0:T(8,128)S(1)} %get-tuple-element.16.fields, f32[4,16,96,128]{3,2,1,0:T(8,128)S(1)} %get-tuple-element.18.inner, bf16[128,4096]{1,0:T(8,128)(2,1)S(1)} %get-tuple-element.19.select, bf16[2,4,96,128]{3,2,1,0:T(8,128)(2,1)S(1)} %collective-permute-done.x0, ...), custom_call_target="tpu_custom_call" | custom-call | tf_op jit(solution)/shard_map/panel/pallas_call | solution.py:415
  13.9 0.1 collective-permute-start.5
  14.0 1.2 %collective-permute-done.5 = f32[48,128]{1,0:T(8,128)S(1)} collective-permute-done((f32[48,128]{1,0:T(8,128)S(1)}, f32[48,128]{1,0:T(8,128)S(1)}, u32[]{:S(2)}, u32[]{:S(2)}) %collective-permute-start.5) | collective-permute-done | bytes 24608 | tf_op jit(solution)/shard_map/ppermute | solution.py:44
  15.2 1.2 %collective-permute-start.8 = (f32[48,128]{1,0:T(8,128)S(1)}, f32[48,128]{1,0:T(8,128)S(1)}, u32[]{:S(2)}, u32[]{:S(2)}) collective-permute-start(f32[48,128]{1,0:T(8,128)S(1)} %add.21), channel_id=1, source_target_pairs={{0,19},{1,18},{2,17},{3,16},{4,23},{5,22},{6,21},{7,20},{8,27},{9,... | collective-permute-start | bytes 73736 | tf_op jit(solution)/shard_map/ppermute | solution.py:44
  16.4 0.3 %collective-permute-start.7 = (f32[48,128]{1,0:T(8,128)S(1)}, f32[48,128]{1,0:T(8,128)S(1)}, u32[]{:S(2)}, u32[]{:S(2)}) collective-permute-start(f32[48,128]{1,0:T(8,128)S(1)} %add.21), channel_id=1, source_target_pairs={{0,3},{1,2},{2,1},{3,0},{4,7},{5,6},{6,5},{7,4},{8,11},{9,10},{10,... | collective-permute-start | bytes 73736 | tf_op jit(solution)/shard_map/ppermute | solution.py:44
  16.7 1.4 %collective-permute-start.6 = (f32[48,128]{1,0:T(8,128)S(1)}, f32[48,128]{1,0:T(8,128)S(1)}, u32[]{:S(2)}, u32[]{:S(2)}) collective-permute-start(f32[48,128]{1,0:T(8,128)S(1)} %add.21), channel_id=1, source_target_pairs={{0,17},{1,16},{2,19},{3,18},{4,21},{5,20},{6,23},{7,22},{8,25},{9,... | collective-permute-start | bytes 73736 | tf_op jit(solution)/shard_map/ppermute | solution.py:44
  18.1 1.2 %collective-permute-done.8 = f32[48,128]{1,0:T(8,128)S(1)} collective-permute-done((f32[48,128]{1,0:T(8,128)S(1)}, f32[48,128]{1,0:T(8,128)S(1)}, u32[]{:S(2)}, u32[]{:S(2)}) %collective-permute-start.8) | collective-permute-done | bytes 24608 | tf_op jit(solution)/shard_map/ppermute | solution.py:44
  19.3 0.3 collective-permute-done.7
  19.6 0.3 %collective-permute-done.6 = f32[48,128]{1,0:T(8,128)S(1)} collective-permute-done((f32[48,128]{1,0:T(8,128)S(1)}, f32[48,128]{1,0:T(8,128)S(1)}, u32[]{:S(2)}, u32[]{:S(2)}) %collective-permute-start.6) | collective-permute-done | bytes 24608 | tf_op jit(solution)/shard_map/ppermute | solution.py:44
  20.0 3.6 %collective-permute-start.11 = (f32[48,128]{1,0:T(8,128)S(1)}, f32[48,128]{1,0:T(8,128)S(1)}, u32[]{:S(2)}, u32[]{:S(2)}) collective-permute-start(f32[48,128]{1,0:T(8,128)S(1)} %add_add_fusion.1), channel_id=1, source_target_pairs={{0,13},{1,12},{2,15},{3,14},{4,9},{5,8},{6,11},{7,10},{8,5},{9,4},... | collective-permute-start | bytes 73736 | tf_op jit(solution)/shard_map/ppermute | solution.py:44
  23.5 0.5 %collective-permute-start.10 = (f32[48,128]{1,0:T(8,128)S(1)}, f32[48,128]{1,0:T(8,128)S(1)}, u32[]{:S(2)}, u32[]{:S(2)}) collective-permute-start(f32[48,128]{1,0:T(8,128)S(1)} %add_add_fusion.1), channel_id=1, source_target_pairs={{0,9},{1,8},{2,11},{3,10},{4,13},{5,12},{6,15},{7,14},{8,1},{9,0},... | collective-permute-start | bytes 73736 | tf_op jit(solution)/shard_map/ppermute | solution.py:44
  24.1 0.3 collective-permute-start.9
  24.3 0.8 %collective-permute-done.11 = f32[48,128]{1,0:T(8,128)S(1)} collective-permute-done((f32[48,128]{1,0:T(8,128)S(1)}, f32[48,128]{1,0:T(8,128)S(1)}, u32[]{:S(2)}, u32[]{:S(2)}) %collective-permute-start.11) | collective-permute-done | bytes 24608 | tf_op jit(solution)/shard_map/ppermute | solution.py:44
  25.1 2.7 %collective-permute-done.10 = f32[48,128]{1,0:T(8,128)S(1)} collective-permute-done((f32[48,128]{1,0:T(8,128)S(1)}, f32[48,128]{1,0:T(8,128)S(1)}, u32[]{:S(2)}, u32[]{:S(2)}) %collective-permute-start.10) | collective-permute-done | bytes 24608 | tf_op jit(solution)/shard_map/ppermute | solution.py:44
  27.8 3.8 %basis.1 = (f32[3072,128]{1,0:T(8,128)}, f32[96,96]{1,0:T(8,128)}) custom-call(f32[48,128]{1,0:T(8,128)S(1)} %add_add_fusion.moments, bf16[192,4096]{1,0:T(8,128)(2,1)S(1)} %get-tuple-element.27.panel), custom_call_target="tpu_custom_call" | custom-call | tf_op jit(solution)/shard_map/basis/pallas_call | solution.py:427
  (7 shorter events, 0.0 us)
Async XLA Ops:
  2.9 8.5 %collective-permute-start = (bf16[2,4,96,128]{3,2,1,0:T(8,128)(2,1)S(1)}, bf16[2,4,96,128]{3,2,1,0:T(8,128)(2,1)S(1)}, u32[]{:S(2)}, u32[]{:S(2)}) collective-permute-start(bf16[2,4,96,128]{3,2,1,0:T(8,128)(2,1)S(1)} %get-tuple-element.20), channel_id=1, source_target_pairs={{0,16},{1,17},{2,18},{3,19},{4,20},{5,21},{6,22},{7,23},{8,24},{9,... | collective-permute-start | bytes 589832 | tf_op jit(solution)/shard_map/ppermute | solution.py:35
  6.0 6.4 %collective-permute-start.1 = (bf16[2,4,96,128]{3,2,1,0:T(8,128)(2,1)S(1)}, bf16[2,4,96,128]{3,2,1,0:T(8,128)(2,1)S(1)}, u32[]{:S(2)}, u32[]{:S(2)}) collective-permute-start(bf16[2,4,96,128]{3,2,1,0:T(8,128)(2,1)S(1)} %get-tuple-element.22), channel_id=1, source_target_pairs={{0,4},{1,5},{2,6},{3,7},{4,0},{5,1},{6,2},{7,3},{8,12},{9,13},{10,... | collective-permute-start | bytes 589832 | tf_op jit(solution)/shard_map/ppermute | solution.py:35
  7.5 4.8 %collective-permute-start.2 = (bf16[2,4,96,128]{3,2,1,0:T(8,128)(2,1)S(1)}, bf16[2,4,96,128]{3,2,1,0:T(8,128)(2,1)S(1)}, u32[]{:S(2)}, u32[]{:S(2)}) collective-permute-start(bf16[2,4,96,128]{3,2,1,0:T(8,128)(2,1)S(1)} %get-tuple-element.23), channel_id=1, source_target_pairs={{0,1},{1,0},{2,3},{3,2},{4,8},{5,9},{6,10},{7,11},{8,4},{9,5},{10,... | collective-permute-start | bytes 589832 | tf_op jit(solution)/shard_map/ppermute | solution.py:35
  7.6 2.8 %collective-permute-start.3 = (bf16[96,128]{1,0:T(8,128)(2,1)S(1)}, bf16[96,128]{1,0:T(8,128)(2,1)S(1)}, u32[]{:S(2)}, u32[]{:S(2)}) collective-permute-start(bf16[96,128]{1,0:T(8,128)(2,1)S(1)} %get-tuple-element.24), channel_id=1, source_target_pairs={{0,1},{1,0},{2,3},{3,2},{4,5},{5,4},{6,7},{7,6},{8,9},{9,8},{10,11... | collective-permute-start | bytes 73736 | tf_op jit(solution)/shard_map/ppermute | solution.py:35
  8.1 3.3 %collective-permute-start.4 = (bf16[96,128]{1,0:T(8,128)(2,1)S(1)}, bf16[96,128]{1,0:T(8,128)(2,1)S(1)}, u32[]{:S(2)}, u32[]{:S(2)}) collective-permute-start(bf16[96,128]{1,0:T(8,128)(2,1)S(1)} %get-tuple-element.25), channel_id=1, source_target_pairs={{0,3},{1,2},{2,1},{3,0},{4,7},{5,6},{6,5},{7,4},{8,11},{9,10},{10,... | collective-permute-start | bytes 73736 | tf_op jit(solution)/shard_map/ppermute | solution.py:35
  13.9 1.3 %collective-permute-start.5 = (f32[48,128]{1,0:T(8,128)S(1)}, f32[48,128]{1,0:T(8,128)S(1)}, u32[]{:S(2)}, u32[]{:S(2)}) collective-permute-start(f32[48,128]{1,0:T(8,128)S(1)} %get-tuple-element.26), channel_id=1, source_target_pairs={{0,1},{1,0},{2,3},{3,2},{4,5},{5,4},{6,7},{7,6},{8,9},{9,8},{10,11... | collective-permute-start | bytes 73736 | tf_op jit(solution)/shard_map/ppermute | solution.py:44
  15.2 4.2 %collective-permute-start.8 = (f32[48,128]{1,0:T(8,128)S(1)}, f32[48,128]{1,0:T(8,128)S(1)}, u32[]{:S(2)}, u32[]{:S(2)}) collective-permute-start(f32[48,128]{1,0:T(8,128)S(1)} %add.21), channel_id=1, source_target_pairs={{0,19},{1,18},{2,17},{3,16},{4,23},{5,22},{6,21},{7,20},{8,27},{9,... | collective-permute-start | bytes 73736 | tf_op jit(solution)/shard_map/ppermute | solution.py:44
  16.4 3.3 %collective-permute-start.7 = (f32[48,128]{1,0:T(8,128)S(1)}, f32[48,128]{1,0:T(8,128)S(1)}, u32[]{:S(2)}, u32[]{:S(2)}) collective-permute-start(f32[48,128]{1,0:T(8,128)S(1)} %add.21), channel_id=1, source_target_pairs={{0,3},{1,2},{2,1},{3,0},{4,7},{5,6},{6,5},{7,4},{8,11},{9,10},{10,... | collective-permute-start | bytes 73736 | tf_op jit(solution)/shard_map/ppermute | solution.py:44
  16.7 3.3 %collective-permute-start.6 = (f32[48,128]{1,0:T(8,128)S(1)}, f32[48,128]{1,0:T(8,128)S(1)}, u32[]{:S(2)}, u32[]{:S(2)}) collective-permute-start(f32[48,128]{1,0:T(8,128)S(1)} %add.21), channel_id=1, source_target_pairs={{0,17},{1,16},{2,19},{3,18},{4,21},{5,20},{6,23},{7,22},{8,25},{9,... | collective-permute-start | bytes 73736 | tf_op jit(solution)/shard_map/ppermute | solution.py:44
  20.0 5.2 %collective-permute-start.11 = (f32[48,128]{1,0:T(8,128)S(1)}, f32[48,128]{1,0:T(8,128)S(1)}, u32[]{:S(2)}, u32[]{:S(2)}) collective-permute-start(f32[48,128]{1,0:T(8,128)S(1)} %add_add_fusion.1), channel_id=1, source_target_pairs={{0,13},{1,12},{2,15},{3,14},{4,9},{5,8},{6,11},{7,10},{8,5},{9,4},... | collective-permute-start | bytes 73736 | tf_op jit(solution)/shard_map/ppermute | solution.py:44
  23.5 4.3 %collective-permute-start.10 = (f32[48,128]{1,0:T(8,128)S(1)}, f32[48,128]{1,0:T(8,128)S(1)}, u32[]{:S(2)}, u32[]{:S(2)}) collective-permute-start(f32[48,128]{1,0:T(8,128)S(1)} %add_add_fusion.1), channel_id=1, source_target_pairs={{0,9},{1,8},{2,11},{3,10},{4,13},{5,12},{6,15},{7,14},{8,1},{9,0},... | collective-permute-start | bytes 73736 | tf_op jit(solution)/shard_map/ppermute | solution.py:44
  24.1 3.7 %collective-permute-start.9 = (f32[48,128]{1,0:T(8,128)S(1)}, f32[48,128]{1,0:T(8,128)S(1)}, u32[]{:S(2)}, u32[]{:S(2)}) collective-permute-start(f32[48,128]{1,0:T(8,128)S(1)} %add_add_fusion.1), channel_id=1, source_target_pairs={{0,5},{1,4},{2,7},{3,6},{4,1},{5,0},{6,3},{7,2},{8,13},{9,12},{10,... | collective-permute-start | bytes 73736 | tf_op jit(solution)/shard_map/ppermute | solution.py:44

commit v10 on v9

--- a/solution.py
+++ b/solution.py
@@ -214,11 +214,11 @@
 
     def add_z(value, i, r):
         k = i * cells + r
-        if k % 2 == 0:
+        if k % 4 == 0:
             near[i] = jnp.dot(
-                edges, select[:, k * LANES : (k + 2) * LANES], preferred_element_type=F32
+                edges, select[:, k * LANES : (k + 4) * LANES], preferred_element_type=F32
             )
-        return value + near[i][:, k % 2 * LANES : (k % 2 + 1) * LANES]
+        return value + near[i][:, k % 4 * LANES : (k % 4 + 1) * LANES]
 
     def put(c, value):
         high = value.astype(BF16)

time: 31.8 us -> 31.8 us (level)
  no operation moved by 1% of the time
where the time goes in v10:
time: 31.8 us; the launch traced here: 31.6 us
  starting transfers between devices  13.6 us (43%)
  Pallas kernels  8.81 us (28%)
  waiting for transfers between devices  8.44 us (27%)
  between operations  0.69 us (2%)
    ppermute x7, starting transfers between devices, other(): return lax.ppermute(value, AXES, [(i, i ^ step) for i in range(count)])  7.43 us
    ppermute x7, waiting for transfers between devices, other(): return lax.ppermute(value, AXES, [(i, i ^ step) for i in range(count)])  6.46 us
    ppermute x5, starting transfers between devices, swapped(): return lax.ppermute(value, AXES, out)  6.22 us
    pallas_call x1, Pallas kernels, per_device(): pl.pallas_call(functools.partial(basis_kernel, dims), out_shape=(jax.Shap...  3.81 us
    pallas_call x1, Pallas kernels, per_device(): pl.pallas_call(functools.partial(pack_kernel, dims, sizes[0] > 2), out_sh...  2.3 us
    ppermute x5, waiting for transfers between devices, swapped(): return lax.ppermute(value, AXES, out)  1.98 us
    pallas_call x1, Pallas kernels, per_device(): pl.pallas_call(functools.partial(panel_kernel, dims, scale, sizes), out_s...  1.51 us
    pallas_call x1, Pallas kernels, per_device(): pl.pallas_call(functools.partial(inner_kernel, dims), out_shape=(jax.Shap...  1.18 us
  transfers between devices with their start and end apart: 12, of which 8 were waited for; matrix products, arithmetic and copies ran while one was open for 0% of the time, Pallas kernels for 4%

profile of v10, /device:TPU:0, one launch (start us, length us, event | category | flops | bytes accessed | tf_op | source)
XLA Modules:
  0.0 31.6 jit_solution(16407514188699053443)
XLA Ops:
  0.6 2.3 %pack.1 = (f32[4,16,96,128]{3,2,1,0:T(8,128)S(1)}, f32[2,1536,128]{2,1,0:T(8,128)S(1)}, bf16[2,4,96,128]{3,2,1,0:T(8,128)(2,1)S(1)}, bf16[2,4,96,128]{3,2,1,0:T(...) custom-call(bf16[1536,128]{1,0:T(8,128)(2,1)} %bitcast.5, ...), custom_call_target="tpu_custom_call" | custom-call | tf_op jit(solution)/shard_map/pack/pallas_call | solution.py:373
  2.9 3.0 %collective-permute-start = (bf16[2,4,96,128]{3,2,1,0:T(8,128)(2,1)S(1)}, bf16[2,4,96,128]{3,2,1,0:T(8,128)(2,1)S(1)}, u32[]{:S(2)}, u32[]{:S(2)}) collective-permute-start(bf16[2,4,96,128]{3,2,1,0:T(8,128)(2,1)S(1)} %get-tuple-element.20), channel_id=1, source_target_pairs={{0,16},{1,17},{2,18},{3,19},{4,20},{5,21},{6,22},{7,23},{8,24},{9,... | collective-permute-start | bytes 589832 | tf_op jit(solution)/shard_map/ppermute | solution.py:35
  6.0 1.6 %collective-permute-start.1 = (bf16[2,4,96,128]{3,2,1,0:T(8,128)(2,1)S(1)}, bf16[2,4,96,128]{3,2,1,0:T(8,128)(2,1)S(1)}, u32[]{:S(2)}, u32[]{:S(2)}) collective-permute-start(bf16[2,4,96,128]{3,2,1,0:T(8,128)(2,1)S(1)} %get-tuple-element.22), channel_id=1, source_target_pairs={{0,4},{1,5},{2,6},{3,7},{4,0},{5,1},{6,2},{7,3},{8,12},{9,13},{10,... | collective-permute-start | bytes 589832 | tf_op jit(solution)/shard_map/ppermute | solution.py:35
  7.6 0.5 %collective-permute-start.3 = (bf16[96,128]{1,0:T(8,128)(2,1)S(1)}, bf16[96,128]{1,0:T(8,128)(2,1)S(1)}, u32[]{:S(2)}, u32[]{:S(2)}) collective-permute-start(bf16[96,128]{1,0:T(8,128)(2,1)S(1)} %get-tuple-element.24), channel_id=1, source_target_pairs={{0,1},{1,0},{2,3},{3,2},{4,5},{5,4},{6,7},{7,6},{8,9},{9,8},{10,11... | collective-permute-start | bytes 73736 | tf_op jit(solution)/shard_map/ppermute | solution.py:35
  8.1 1.1 %collective-permute-start.4 = (bf16[96,128]{1,0:T(8,128)(2,1)S(1)}, bf16[96,128]{1,0:T(8,128)(2,1)S(1)}, u32[]{:S(2)}, u32[]{:S(2)}) collective-permute-start(bf16[96,128]{1,0:T(8,128)(2,1)S(1)} %get-tuple-element.25), channel_id=1, source_target_pairs={{0,3},{1,2},{2,1},{3,0},{4,7},{5,6},{6,5},{7,4},{8,11},{9,10},{10,... | collective-permute-start | bytes 73736 | tf_op jit(solution)/shard_map/ppermute | solution.py:35
  9.2 1.2 %inner.1 = (f32[4,16,96,128]{3,2,1,0:T(8,128)S(1)}, bf16[128,4096]{1,0:T(8,128)(2,1)S(1)}) custom-call(f32[4,16,96,128]{3,2,1,0:T(8,128)S(1)} %get-tuple-element.16.fields, f32[2,1536,128]{2,1,0:T(8,128)S(1)} %get-tuple-element.17.wide), custom_call_target="tpu_custom_call" | custom-call | tf_op jit(solution)/shard_map/inner/pallas_call | solution.py:403
  10.3 0.0 collective-permute-done.3.z0
  10.4 1.0 %collective-permute-done.4.z1 = bf16[96,128]{1,0:T(8,128)(2,1)S(1)} collective-permute-done((bf16[96,128]{1,0:T(8,128)(2,1)S(1)}, bf16[96,128]{1,0:T(8,128)(2,1)S(1)}, u32[]{:S(2)}, u32[]{:S(2)}) %collective-permute-start.4) | collective-permute-done | bytes 24608 | tf_op jit(solution)/shard_map/ppermute | solution.py:35
  11.4 0.9 %collective-permute-done.1.y0 = bf16[2,4,96,128]{3,2,1,0:T(8,128)(2,1)S(1)} collective-permute-done((bf16[2,4,96,128]{3,2,1,0:T(8,128)(2,1)S(1)}, bf16[2,4,96,128]{3,2,1,0:T(8,128)(2,1)S(1)}, u32[]{:S(2)}, u32[]{:S(2)}) %collective-permute-start.1) | collective-permute-done | bytes 196640 | tf_op jit(solution)/shard_map/ppermute | solution.py:35
  12.3 1.5 %panel.1 = (bf16[192,4096]{1,0:T(8,128)(2,1)S(1)}, f32[48,128]{1,0:T(8,128)S(1)}) custom-call(f32[4,16,96,128]{3,2,1,0:T(8,128)S(1)} %get-tuple-element.16.fields, f32[4,16,96,128]{3,2,1,0:T(8,128)S(1)} %get-tuple-element.18.inner, bf16[128,4096]{1,0:T(8,128)(2,1)S(1)} %get-tuple-element.19.select, bf16[2,4,96,128]{3,2,1,0:T(8,128)(2,1)S(1)} %collective-permute-done.x0, ...), custom_call_target="tpu_custom_call" | custom-call | tf_op jit(solution)/shard_map/panel/pallas_call | solution.py:415
  13.9 0.1 collective-permute-start.5
  13.9 1.2 %collective-permute-done.5 = f32[48,128]{1,0:T(8,128)S(1)} collective-permute-done((f32[48,128]{1,0:T(8,128)S(1)}, f32[48,128]{1,0:T(8,128)S(1)}, u32[]{:S(2)}, u32[]{:S(2)}) %collective-permute-start.5) | collective-permute-done | bytes 24608 | tf_op jit(solution)/shard_map/ppermute | solution.py:44
  15.1 1.2 %collective-permute-start.8 = (f32[48,128]{1,0:T(8,128)S(1)}, f32[48,128]{1,0:T(8,128)S(1)}, u32[]{:S(2)}, u32[]{:S(2)}) collective-permute-start(f32[48,128]{1,0:T(8,128)S(1)} %add.21), channel_id=1, source_target_pairs={{0,19},{1,18},{2,17},{3,16},{4,23},{5,22},{6,21},{7,20},{8,27},{9,... | collective-permute-start | bytes 73736 | tf_op jit(solution)/shard_map/ppermute | solution.py:44
  16.3 0.3 %collective-permute-start.7 = (f32[48,128]{1,0:T(8,128)S(1)}, f32[48,128]{1,0:T(8,128)S(1)}, u32[]{:S(2)}, u32[]{:S(2)}) collective-permute-start(f32[48,128]{1,0:T(8,128)S(1)} %add.21), channel_id=1, source_target_pairs={{0,3},{1,2},{2,1},{3,0},{4,7},{5,6},{6,5},{7,4},{8,11},{9,10},{10,... | collective-permute-start | bytes 73736 | tf_op jit(solution)/shard_map/ppermute | solution.py:44
  16.7 1.4 %collective-permute-start.6 = (f32[48,128]{1,0:T(8,128)S(1)}, f32[48,128]{1,0:T(8,128)S(1)}, u32[]{:S(2)}, u32[]{:S(2)}) collective-permute-start(f32[48,128]{1,0:T(8,128)S(1)} %add.21), channel_id=1, source_target_pairs={{0,17},{1,16},{2,19},{3,18},{4,21},{5,20},{6,23},{7,22},{8,25},{9,... | collective-permute-start | bytes 73736 | tf_op jit(solution)/shard_map/ppermute | solution.py:44
  18.1 1.2 %collective-permute-done.8 = f32[48,128]{1,0:T(8,128)S(1)} collective-permute-done((f32[48,128]{1,0:T(8,128)S(1)}, f32[48,128]{1,0:T(8,128)S(1)}, u32[]{:S(2)}, u32[]{:S(2)}) %collective-permute-start.8) | collective-permute-done | bytes 24608 | tf_op jit(solution)/shard_map/ppermute | solution.py:44
  19.3 0.3 collective-permute-done.7
  19.6 0.3 %collective-permute-done.6 = f32[48,128]{1,0:T(8,128)S(1)} collective-permute-done((f32[48,128]{1,0:T(8,128)S(1)}, f32[48,128]{1,0:T(8,128)S(1)}, u32[]{:S(2)}, u32[]{:S(2)}) %collective-permute-start.6) | collective-permute-done | bytes 24608 | tf_op jit(solution)/shard_map/ppermute | solution.py:44
  19.9 3.6 %collective-permute-start.11 = (f32[48,128]{1,0:T(8,128)S(1)}, f32[48,128]{1,0:T(8,128)S(1)}, u32[]{:S(2)}, u32[]{:S(2)}) collective-permute-start(f32[48,128]{1,0:T(8,128)S(1)} %add_add_fusion.1), channel_id=1, source_target_pairs={{0,13},{1,12},{2,15},{3,14},{4,9},{5,8},{6,11},{7,10},{8,5},{9,4},... | collective-permute-start | bytes 73736 | tf_op jit(solution)/shard_map/ppermute | solution.py:44
  23.5 0.5 %collective-permute-start.10 = (f32[48,128]{1,0:T(8,128)S(1)}, f32[48,128]{1,0:T(8,128)S(1)}, u32[]{:S(2)}, u32[]{:S(2)}) collective-permute-start(f32[48,128]{1,0:T(8,128)S(1)} %add_add_fusion.1), channel_id=1, source_target_pairs={{0,9},{1,8},{2,11},{3,10},{4,13},{5,12},{6,15},{7,14},{8,1},{9,0},... | collective-permute-start | bytes 73736 | tf_op jit(solution)/shard_map/ppermute | solution.py:44
  24.0 0.3 collective-permute-start.9
  24.3 0.8 %collective-permute-done.11 = f32[48,128]{1,0:T(8,128)S(1)} collective-permute-done((f32[48,128]{1,0:T(8,128)S(1)}, f32[48,128]{1,0:T(8,128)S(1)}, u32[]{:S(2)}, u32[]{:S(2)}) %collective-permute-start.11) | collective-permute-done | bytes 24608 | tf_op jit(solution)/shard_map/ppermute | solution.py:44
  25.1 2.7 %collective-permute-done.10 = f32[48,128]{1,0:T(8,128)S(1)} collective-permute-done((f32[48,128]{1,0:T(8,128)S(1)}, f32[48,128]{1,0:T(8,128)S(1)}, u32[]{:S(2)}, u32[]{:S(2)}) %collective-permute-start.10) | collective-permute-done | bytes 24608 | tf_op jit(solution)/shard_map/ppermute | solution.py:44
  27.8 3.8 %basis.1 = (f32[3072,128]{1,0:T(8,128)}, f32[96,96]{1,0:T(8,128)}) custom-call(f32[48,128]{1,0:T(8,128)S(1)} %add_add_fusion.moments, bf16[192,4096]{1,0:T(8,128)(2,1)S(1)} %get-tuple-element.27.panel), custom_call_target="tpu_custom_call" | custom-call | tf_op jit(solution)/shard_map/basis/pallas_call | solution.py:427
  (7 shorter events, 0.0 us)
Async XLA Ops:
  2.9 8.5 %collective-permute-start = (bf16[2,4,96,128]{3,2,1,0:T(8,128)(2,1)S(1)}, bf16[2,4,96,128]{3,2,1,0:T(8,128)(2,1)S(1)}, u32[]{:S(2)}, u32[]{:S(2)}) collective-permute-start(bf16[2,4,96,128]{3,2,1,0:T(8,128)(2,1)S(1)} %get-tuple-element.20), channel_id=1, source_target_pairs={{0,16},{1,17},{2,18},{3,19},{4,20},{5,21},{6,22},{7,23},{8,24},{9,... | collective-permute-start | bytes 589832 | tf_op jit(solution)/shard_map/ppermute | solution.py:35
  6.0 6.4 %collective-permute-start.1 = (bf16[2,4,96,128]{3,2,1,0:T(8,128)(2,1)S(1)}, bf16[2,4,96,128]{3,2,1,0:T(8,128)(2,1)S(1)}, u32[]{:S(2)}, u32[]{:S(2)}) collective-permute-start(bf16[2,4,96,128]{3,2,1,0:T(8,128)(2,1)S(1)} %get-tuple-element.22), channel_id=1, source_target_pairs={{0,4},{1,5},{2,6},{3,7},{4,0},{5,1},{6,2},{7,3},{8,12},{9,13},{10,... | collective-permute-start | bytes 589832 | tf_op jit(solution)/shard_map/ppermute | solution.py:35
  7.5 4.8 %collective-permute-start.2 = (bf16[2,4,96,128]{3,2,1,0:T(8,128)(2,1)S(1)}, bf16[2,4,96,128]{3,2,1,0:T(8,128)(2,1)S(1)}, u32[]{:S(2)}, u32[]{:S(2)}) collective-permute-start(bf16[2,4,96,128]{3,2,1,0:T(8,128)(2,1)S(1)} %get-tuple-element.23), channel_id=1, source_target_pairs={{0,1},{1,0},{2,3},{3,2},{4,8},{5,9},{6,10},{7,11},{8,4},{9,5},{10,... | collective-permute-start | bytes 589832 | tf_op jit(solution)/shard_map/ppermute | solution.py:35
  7.6 2.8 %collective-permute-start.3 = (bf16[96,128]{1,0:T(8,128)(2,1)S(1)}, bf16[96,128]{1,0:T(8,128)(2,1)S(1)}, u32[]{:S(2)}, u32[]{:S(2)}) collective-permute-start(bf16[96,128]{1,0:T(8,128)(2,1)S(1)} %get-tuple-element.24), channel_id=1, source_target_pairs={{0,1},{1,0},{2,3},{3,2},{4,5},{5,4},{6,7},{7,6},{8,9},{9,8},{10,11... | collective-permute-start | bytes 73736 | tf_op jit(solution)/shard_map/ppermute | solution.py:35
  8.1 3.3 %collective-permute-start.4 = (bf16[96,128]{1,0:T(8,128)(2,1)S(1)}, bf16[96,128]{1,0:T(8,128)(2,1)S(1)}, u32[]{:S(2)}, u32[]{:S(2)}) collective-permute-start(bf16[96,128]{1,0:T(8,128)(2,1)S(1)} %get-tuple-element.25), channel_id=1, source_target_pairs={{0,3},{1,2},{2,1},{3,0},{4,7},{5,6},{6,5},{7,4},{8,11},{9,10},{10,... | collective-permute-start | bytes 73736 | tf_op jit(solution)/shard_map/ppermute | solution.py:35
  13.9 1.3 %collective-permute-start.5 = (f32[48,128]{1,0:T(8,128)S(1)}, f32[48,128]{1,0:T(8,128)S(1)}, u32[]{:S(2)}, u32[]{:S(2)}) collective-permute-start(f32[48,128]{1,0:T(8,128)S(1)} %get-tuple-element.26), channel_id=1, source_target_pairs={{0,1},{1,0},{2,3},{3,2},{4,5},{5,4},{6,7},{7,6},{8,9},{9,8},{10,11... | collective-permute-start | bytes 73736 | tf_op jit(solution)/shard_map/ppermute | solution.py:44
  15.1 4.2 %collective-permute-start.8 = (f32[48,128]{1,0:T(8,128)S(1)}, f32[48,128]{1,0:T(8,128)S(1)}, u32[]{:S(2)}, u32[]{:S(2)}) collective-permute-start(f32[48,128]{1,0:T(8,128)S(1)} %add.21), channel_id=1, source_target_pairs={{0,19},{1,18},{2,17},{3,16},{4,23},{5,22},{6,21},{7,20},{8,27},{9,... | collective-permute-start | bytes 73736 | tf_op jit(solution)/shard_map/ppermute | solution.py:44
  16.3 3.3 %collective-permute-start.7 = (f32[48,128]{1,0:T(8,128)S(1)}, f32[48,128]{1,0:T(8,128)S(1)}, u32[]{:S(2)}, u32[]{:S(2)}) collective-permute-start(f32[48,128]{1,0:T(8,128)S(1)} %add.21), channel_id=1, source_target_pairs={{0,3},{1,2},{2,1},{3,0},{4,7},{5,6},{6,5},{7,4},{8,11},{9,10},{10,... | collective-permute-start | bytes 73736 | tf_op jit(solution)/shard_map/ppermute | solution.py:44
  16.7 3.3 %collective-permute-start.6 = (f32[48,128]{1,0:T(8,128)S(1)}, f32[48,128]{1,0:T(8,128)S(1)}, u32[]{:S(2)}, u32[]{:S(2)}) collective-permute-start(f32[48,128]{1,0:T(8,128)S(1)} %add.21), channel_id=1, source_target_pairs={{0,17},{1,16},{2,19},{3,18},{4,21},{5,20},{6,23},{7,22},{8,25},{9,... | collective-permute-start | bytes 73736 | tf_op jit(solution)/shard_map/ppermute | solution.py:44
  19.9 5.2 %collective-permute-start.11 = (f32[48,128]{1,0:T(8,128)S(1)}, f32[48,128]{1,0:T(8,128)S(1)}, u32[]{:S(2)}, u32[]{:S(2)}) collective-permute-start(f32[48,128]{1,0:T(8,128)S(1)} %add_add_fusion.1), channel_id=1, source_target_pairs={{0,13},{1,12},{2,15},{3,14},{4,9},{5,8},{6,11},{7,10},{8,5},{9,4},... | collective-permute-start | bytes 73736 | tf_op jit(solution)/shard_map/ppermute | solution.py:44
  23.5 4.3 %collective-permute-start.10 = (f32[48,128]{1,0:T(8,128)S(1)}, f32[48,128]{1,0:T(8,128)S(1)}, u32[]{:S(2)}, u32[]{:S(2)}) collective-permute-start(f32[48,128]{1,0:T(8,128)S(1)} %add_add_fusion.1), channel_id=1, source_target_pairs={{0,9},{1,8},{2,11},{3,10},{4,13},{5,12},{6,15},{7,14},{8,1},{9,0},... | collective-permute-start | bytes 73736 | tf_op jit(solution)/shard_map/ppermute | solution.py:44
  24.0 3.7 %collective-permute-start.9 = (f32[48,128]{1,0:T(8,128)S(1)}, f32[48,128]{1,0:T(8,128)S(1)}, u32[]{:S(2)}, u32[]{:S(2)}) collective-permute-start(f32[48,128]{1,0:T(8,128)S(1)} %add_add_fusion.1), channel_id=1, source_target_pairs={{0,5},{1,4},{2,7},{3,6},{4,1},{5,0},{6,3},{7,2},{8,13},{9,12},{10,... | collective-permute-start | bytes 73736 | tf_op jit(solution)/shard_map/ppermute | solution.py:44
